TPU v7x, 32 devices: a whole 2x2x4 slice. The times are simulated.
32 devices in a mesh: fsdp: 8 (over z, y), ctx: 2 (over x), tp: 2 (over core).
Axes of the slice: x: 2, y: 2, z: 4, core: 2. Of those that a mesh axis runs over, the one named last changes fastest.
Arguments:
- tokens: bfloat16 [3584, 2304], P(('fsdp', 'ctx')), may hold values from -6 to 6
- cotangent: bfloat16 [3584, 2304], P(('fsdp', 'ctx')), may hold values from -6 to 6
- lengths: int32 [8, 1], P('fsdp'), may hold values from 224 to 448, as said below
- positions: int32 [8, 448], P('fsdp'), may hold values from 0 to 447, each once within a row
- query_weight: bfloat16 [2304, 2048], P('fsdp', 'tp'), may hold values from -0.5 to 0.5
- key_weight: bfloat16 [2304, 1024], P('fsdp', 'tp'), may hold values from -0.5 to 0.5
- value_weight: bfloat16 [2304, 1024], P('fsdp', 'tp'), may hold values from -0.125 to 0.125
- output_weight: bfloat16 [2048, 2304], P('tp', 'fsdp'), may hold values from -0.125 to 0.125
- gate_weight: bfloat16 [2304, 9216], P('fsdp', 'tp'), may hold values from -0.125 to 0.125
- up_weight: bfloat16 [2304, 9216], P('fsdp', 'tp'), may hold values from -0.125 to 0.125
- down_weight: bfloat16 [9216, 2304], P('tp', 'fsdp'), may hold values from -0.0625 to 0.0625
- gain_attn_in: bfloat16 [2304], P('fsdp'), may hold values from -0.5 to 0.5
- gain_attn_out: bfloat16 [2304], P('fsdp'), may hold values from -0.5 to 0.5
- gain_ffn_in: bfloat16 [2304], P('fsdp'), may hold values from -0.5 to 0.5
- gain_ffn_out: bfloat16 [2304], P('fsdp'), may hold values from -0.5 to 0.5
Outputs:
- block_out: bfloat16 [3584, 2304], P(('fsdp', 'ctx'))
- tokens_grad: bfloat16 [3584, 2304], P(('fsdp', 'ctx'))
- query_weight_grad: float32 [2304, 2048], P(('fsdp', 'ctx'), 'tp')
- key_weight_grad: float32 [2304, 1024], P(('fsdp', 'ctx'), 'tp')
- value_weight_grad: float32 [2304, 1024], P(('fsdp', 'ctx'), 'tp')
- output_weight_grad: float32 [2048, 2304], P('tp', ('fsdp', 'ctx'))
- gate_weight_grad: float32 [2304, 9216], P(('fsdp', 'ctx'), 'tp')
- up_weight_grad: float32 [2304, 9216], P(('fsdp', 'ctx'), 'tp')
- down_weight_grad: float32 [9216, 2304], P('tp', ('fsdp', 'ctx'))
- gain_attn_in_grad: float32 [2304], P(('fsdp', 'ctx'))
- gain_attn_out_grad: float32 [2304], P(('fsdp', 'ctx'))
- gain_ffn_in_grad: float32 [2304], P(('fsdp', 'ctx'))
- gain_ffn_out_grad: float32 [2304], P(('fsdp', 'ctx'))
Inputs may be any that keep to these rules, and one draw needn't show every extreme that they name: lengths[g, 0] is the number of live tokens of group g's sequence; in every draw some group has exactly 448 and another exactly 224. Each row of positions is a permutation of 0 to 447.
All inputs are finite; a program needn't handle non-finite values.
Results may differ from a plain program's by a relative error of at most 0.018.
The roundings to bfloat16 on the way count: a program that leaves them out, or rounds other values in their place, can miss the bound.
Values may be sent and summed in bfloat16 or wider, within the bound.
No kernel may reach another device: no remote copies, remote signals or barrier semaphores. Data moves between devices by JAX's collectives and lax.ppermute only.
A program may use at most 640 MiB of HBM per device.

v0:
```python
import jax
import jax.numpy as jnp
from jax import lax
from jax.sharding import PartitionSpec as P

HEAD_DIM = 256


eps_norm = 1e-06
soft_cap = 50.0


def rms_scale(field, gain_vec):
    factor = lax.rsqrt(jnp.mean(field * field, axis=-1, keepdims=True) + eps_norm)
    return field * factor * (1.0 + gain_vec)


def gelu_tanh(value_in):
    return (
        0.5
        * value_in
        * (
            1.0
            + jnp.tanh(0.7978845608028654 * (value_in + 0.044715 * value_in * value_in * value_in))
        )
    )


def glu_apply(gate_act, up_act):
    return gelu_tanh(gate_act) * up_act


def norm_back(field, gain_vec, cot_in):
    pullback = jax.vjp(rms_scale, field, gain_vec)[1]
    return pullback(cot_in)


def placement_of(doc_lengths, packed):
    doc_ends = jnp.cumsum(doc_lengths)
    after_end = packed[:, None] >= doc_ends[None, :]
    segment = jnp.sum(after_end.astype(jnp.int32), axis=1)
    inner = packed - jnp.sum(jnp.where(after_end, doc_lengths[None, :], 0), axis=1)
    return (segment, inner)


def angles_of(inner, head_size):
    half_size = head_size // 2
    freq = jnp.power(10000.0, -jnp.arange(half_size, dtype=jnp.float32) * (2.0 / head_size))
    return inner.astype(jnp.float32)[:, None] * freq[None, :]


def rotate(field, angles):
    half_size = field.shape[-1] // 2
    cosine = jnp.cos(angles)[:, None, :]
    sine = jnp.sin(angles)[:, None, :]
    first_half = field[..., :half_size]
    second_half = field[..., half_size:]
    return jnp.concatenate(
        [first_half * cosine - second_half * sine, second_half * cosine + first_half * sine],
        axis=-1,
    )


def scores_of(query_groups, keys_all, allowed):
    raw_scores = jnp.einsum(
        "qkgd,skd->kgqs", query_groups, keys_all, preferred_element_type=jnp.float32
    )
    tanh_ratio = jnp.tanh(raw_scores / soft_cap)
    masked = jnp.where(allowed[None, None], soft_cap * tanh_ratio, -1e30)
    return (tanh_ratio, masked)


def tp_total(partial_sum):
    return lax.psum(partial_sum, "tp")


def attention_weights(
    query_weight,
    key_weight,
    value_weight,
    output_weight,
    gain_attn_in,
    gain_attn_out,
    gain_ffn_in,
    gain_ffn_out,
):
    return (
        lax.all_gather(query_weight, "fsdp", axis=0, tiled=True),
        lax.all_gather(key_weight, "fsdp", axis=0, tiled=True),
        lax.all_gather(value_weight, "fsdp", axis=0, tiled=True),
        lax.all_gather(output_weight, "fsdp", axis=1, tiled=True),
        lax.all_gather(gain_attn_in, "fsdp", axis=0, tiled=True),
        lax.all_gather(gain_attn_out, "fsdp", axis=0, tiled=True),
        lax.all_gather(gain_ffn_in, "fsdp", axis=0, tiled=True),
        lax.all_gather(gain_ffn_out, "fsdp", axis=0, tiled=True),
    )


def ffn_weights(gate_weight, up_weight, down_weight):
    return (
        lax.all_gather(gate_weight, "fsdp", axis=0, tiled=True),
        lax.all_gather(up_weight, "fsdp", axis=0, tiled=True),
        lax.all_gather(down_weight, "fsdp", axis=1, tiled=True),
    )


def local(
    tokens,
    cotangent,
    lengths,
    positions,
    query_weight,
    key_weight,
    value_weight,
    output_weight,
    gate_weight,
    up_weight,
    down_weight,
    gain_attn_in,
    gain_attn_out,
    gain_ffn_in,
    gain_ffn_out,
):
    tok_rows = tokens.shape[0]
    group_rows = positions.shape[1]
    head_size = HEAD_DIM
    kv_local = key_weight.shape[1] // head_size
    q_local = query_weight.shape[1] // head_size
    group_size = q_local // kv_local
    query_scale = head_size ** (-0.5)
    f32 = jnp.float32
    b16 = jnp.bfloat16
    segment_all, inner_all = placement_of(lengths[0], positions[0])
    first_row = lax.axis_index("ctx") * tok_rows
    slot_rows = lax.dynamic_slice_in_dim(positions[0], first_row, tok_rows)
    seg_rows = lax.dynamic_slice_in_dim(segment_all, first_row, tok_rows)
    inner_rows = lax.dynamic_slice_in_dim(inner_all, first_row, tok_rows)
    angles = angles_of(inner_rows, head_size)
    allowed = (seg_rows[:, None] == segment_all[None, :]) & (
        inner_all[None, :] <= inner_rows[:, None]
    )
    seq_group = lax.all_gather(tokens, "ctx", axis=0, tiled=True)
    resid_in = jnp.take(seq_group, slot_rows, axis=0).astype(f32)
    attn_full = attention_weights(
        query_weight,
        key_weight,
        value_weight,
        output_weight,
        gain_attn_in,
        gain_attn_out,
        gain_ffn_in,
        gain_ffn_out,
    )
    gain_list = [piece.astype(f32) for piece in attn_full[4:]]
    wo_full = attn_full[3]
    normed_attn = rms_scale(resid_in, gain_list[0]).astype(b16)
    query_lin = jnp.dot(normed_attn, attn_full[0], preferred_element_type=f32)
    key_lin = jnp.dot(normed_attn, attn_full[1], preferred_element_type=f32)
    value_own = jnp.dot(normed_attn, attn_full[2], preferred_element_type=f32).astype(b16)
    queries = (
        rotate(query_lin.reshape(tok_rows, q_local, head_size), angles) * query_scale
    ).astype(b16)
    keys_own = rotate(key_lin.reshape(tok_rows, kv_local, head_size), angles).astype(b16)
    keys_all, values_all = (
        lax.all_gather(keys_own.reshape(tok_rows, kv_local * head_size), "ctx", axis=0, tiled=True),
        lax.all_gather(value_own, "ctx", axis=0, tiled=True),
    )
    keys_all = keys_all.reshape(-1, kv_local, head_size)
    values_all = values_all.reshape(-1, kv_local, head_size)
    query_groups = queries.reshape(tok_rows, kv_local, group_size, head_size)
    tanh_ratio, masked = scores_of(query_groups, keys_all, allowed)
    row_peak = jnp.max(masked, axis=-1, keepdims=True)
    exp_terms = jnp.exp(masked - row_peak)
    denom_sum = jnp.sum(exp_terms, axis=-1, keepdims=True)
    log_total = row_peak + jnp.log(denom_sum)
    probs_low = (exp_terms / denom_sum).astype(b16)
    attended = (
        jnp.einsum("kgqs,skd->qkgd", probs_low, values_all, preferred_element_type=f32)
        .reshape(tok_rows, q_local * head_size)
        .astype(b16)
    )
    attn_out = tp_total(jnp.dot(attended, wo_full, preferred_element_type=f32))
    middle = resid_in + rms_scale(attn_out, gain_list[1])
    ffn_full = ffn_weights(gate_weight, up_weight, down_weight)
    wd_full = ffn_full[2]
    normed_ffn = rms_scale(middle, gain_list[2]).astype(b16)
    gate_act = jnp.dot(normed_ffn, ffn_full[0], preferred_element_type=f32)
    up_act = jnp.dot(normed_ffn, ffn_full[1], preferred_element_type=f32)
    hidden = glu_apply(gate_act, up_act).astype(b16)
    ffn_out = tp_total(jnp.dot(hidden, wd_full, preferred_element_type=f32))
    block_out = (middle + rms_scale(ffn_out, gain_list[3])).astype(b16)
    d_out = cotangent.astype(f32)
    ffn_full = ffn_weights(gate_weight, up_weight, down_weight)
    wd_full = ffn_full[2]
    d_ffn_raw, gain_four_term = norm_back(ffn_out, gain_list[3], d_out)
    d_ffn_out = d_ffn_raw.astype(b16)
    d_hidden = jnp.einsum("rd,fd->rf", d_ffn_out, wd_full, preferred_element_type=f32)
    d_gate_raw, d_up_raw = jax.vjp(glu_apply, gate_act, up_act)[1](d_hidden)
    d_gate = d_gate_raw.astype(b16)
    d_up = d_up_raw.astype(b16)
    d_normed_ffn = tp_total(
        jnp.einsum("rf,df->rd", d_gate, ffn_full[0], preferred_element_type=f32)
        + jnp.einsum("rf,df->rd", d_up, ffn_full[1], preferred_element_type=f32)
    )
    d_gate_up = jnp.concatenate([d_gate, d_up], axis=1)
    ffn_rows = lax.psum_scatter(
        jnp.concatenate(
            [
                jnp.einsum("rc,rf->cf", normed_ffn, d_gate_up, preferred_element_type=f32),
                jnp.einsum("rc,rf->cf", d_ffn_out, hidden, preferred_element_type=f32),
            ],
            axis=1,
        ),
        ("fsdp", "ctx"),
        scatter_dimension=0,
        tiled=True,
    )
    d_middle_part, gain_three_term = norm_back(middle, gain_list[2], d_normed_ffn)
    d_middle = d_out + d_middle_part
    d_attn_raw, gain_two_term = norm_back(attn_out, gain_list[1], d_middle)
    d_attn_out = d_attn_raw.astype(b16)
    attn_full = attention_weights(
        query_weight,
        key_weight,
        value_weight,
        output_weight,
        gain_attn_in,
        gain_attn_out,
        gain_ffn_in,
        gain_ffn_out,
    )
    wo_full = attn_full[3]
    d_attended = jnp.einsum("rd,hd->rh", d_attn_out, wo_full, preferred_element_type=f32).astype(
        b16
    )
    out_term = jnp.einsum("rd,rh->dh", d_attn_out, attended, preferred_element_type=f32)
    d_att_groups = d_attended.reshape(tok_rows, kv_local, group_size, head_size)
    tanh_ratio, masked = scores_of(query_groups, keys_all, allowed)
    probs = jnp.exp(masked - log_total)
    probs_low = probs.astype(b16)
    d_probs = jnp.einsum("qkgd,skd->kgqs", d_att_groups, values_all, preferred_element_type=f32)
    d_soft = probs * (d_probs - jnp.sum(probs * d_probs, axis=-1, keepdims=True))
    d_scores = (d_soft * (1.0 - tanh_ratio * tanh_ratio)).astype(b16)
    d_queries = jnp.einsum("kgqs,skd->qkgd", d_scores, keys_all, preferred_element_type=f32)
    d_keys_all = jnp.einsum("kgqs,qkgd->skd", d_scores, query_groups, preferred_element_type=f32)
    d_values_all = jnp.einsum("kgqs,qkgd->skd", probs_low, d_att_groups, preferred_element_type=f32)
    d_keys_own, d_values_own = (
        lax.psum_scatter(
            d_keys_all.reshape(-1, kv_local * head_size).astype(jnp.bfloat16),
            "ctx",
            scatter_dimension=0,
            tiled=True,
        ).astype(jnp.float32),
        lax.psum_scatter(
            d_values_all.reshape(-1, kv_local * head_size).astype(jnp.bfloat16),
            "ctx",
            scatter_dimension=0,
            tiled=True,
        ).astype(jnp.float32),
    )
    d_query_lin = (
        rotate(d_queries.reshape(tok_rows, q_local, head_size) * query_scale, -angles)
        .reshape(tok_rows, q_local * head_size)
        .astype(b16)
    )
    d_key_lin = (
        rotate(d_keys_own.reshape(tok_rows, kv_local, head_size), -angles)
        .reshape(tok_rows, kv_local * head_size)
        .astype(b16)
    )
    d_value = d_values_own.astype(b16)
    d_normed_attn = tp_total(
        jnp.einsum("rh,dh->rd", d_query_lin, attn_full[0], preferred_element_type=f32)
        + jnp.einsum("rh,dh->rd", d_key_lin, attn_full[1], preferred_element_type=f32)
        + jnp.einsum("rh,dh->rd", d_value, attn_full[2], preferred_element_type=f32)
    )
    attn_terms = jnp.concatenate(
        [
            jnp.einsum("rd,rh->dh", normed_attn, d_query_lin, preferred_element_type=f32),
            jnp.einsum("rd,rh->dh", normed_attn, d_key_lin, preferred_element_type=f32),
            jnp.einsum("rd,rh->dh", normed_attn, d_value, preferred_element_type=f32),
            out_term,
        ],
        axis=1,
    )
    resid_part, gain_one_term = norm_back(resid_in, gain_list[0], d_normed_attn)
    slot_grad = (d_middle + resid_part).astype(b16)
    grad_group = lax.all_gather(slot_grad, "ctx", axis=0, tiled=True)
    inverse = (
        jnp.zeros((group_rows,), jnp.int32)
        .at[positions[0]]
        .set(jnp.arange(group_rows, dtype=jnp.int32))
    )
    tokens_grad = jnp.take(
        grad_group, lax.dynamic_slice_in_dim(inverse, first_row, tok_rows), axis=0
    )
    gain_terms = jnp.stack([gain_one_term, gain_two_term, gain_three_term, gain_four_term], axis=1)
    attn_rows, gain_rows = (
        lax.psum_scatter(attn_terms, ("fsdp", "ctx"), scatter_dimension=0, tiled=True),
        lax.psum_scatter(gain_terms, ("fsdp", "ctx"), scatter_dimension=0, tiled=True),
    )
    q_cols = query_weight.shape[1]
    k_cols = key_weight.shape[1]
    v_cols = value_weight.shape[1]
    ff_local = gate_weight.shape[1]
    query_weight_grad = attn_rows[:, :q_cols]
    key_weight_grad = attn_rows[:, q_cols : q_cols + k_cols]
    value_weight_grad = attn_rows[:, q_cols + k_cols : q_cols + k_cols + v_cols]
    output_weight_grad = attn_rows[:, q_cols + k_cols + v_cols :].T
    gate_weight_grad = ffn_rows[:, :ff_local]
    up_weight_grad = ffn_rows[:, ff_local : 2 * ff_local]
    down_weight_grad = ffn_rows[:, 2 * ff_local :].T
    return (
        block_out,
        tokens_grad,
        query_weight_grad,
        key_weight_grad,
        value_weight_grad,
        output_weight_grad,
        gate_weight_grad,
        up_weight_grad,
        down_weight_grad,
        gain_rows[:, 0],
        gain_rows[:, 1],
        gain_rows[:, 2],
        gain_rows[:, 3],
    )


def solution(mesh):
    in_specs = (
        P(("fsdp", "ctx"), None),
        P(("fsdp", "ctx"), None),
        P("fsdp", None),
        P("fsdp", None),
        P("fsdp", "tp"),
        P("fsdp", "tp"),
        P("fsdp", "tp"),
        P("tp", "fsdp"),
        P("fsdp", "tp"),
        P("fsdp", "tp"),
        P("tp", "fsdp"),
        P("fsdp"),
        P("fsdp"),
        P("fsdp"),
        P("fsdp"),
    )
    out_specs = (
        P(("fsdp", "ctx"), None),
        P(("fsdp", "ctx"), None),
        P(("fsdp", "ctx"), "tp"),
        P(("fsdp", "ctx"), "tp"),
        P(("fsdp", "ctx"), "tp"),
        P("tp", ("fsdp", "ctx")),
        P(("fsdp", "ctx"), "tp"),
        P(("fsdp", "ctx"), "tp"),
        P("tp", ("fsdp", "ctx")),
        P(("fsdp", "ctx")),
        P(("fsdp", "ctx")),
        P(("fsdp", "ctx")),
        P(("fsdp", "ctx")),
    )
    return jax.shard_map(local, mesh=mesh, in_specs=in_specs, out_specs=out_specs, check_vma=False)
```

profile of v0, /device:TPU:0, one launch (start us, length us, event | category | flops | bytes accessed | tf_op | source)
XLA Modules:
  0.0 4143.8 jit_solution(3369562125840458318)
XLA Ops:
  13.6 39.5 all-reduce.4
  60.9 38.5 all-gather.12.cloned.1.call-done
  101.8 6.8 all_gather.55
  108.8 43.5 %all-gather.14.cloned.1.call-done = bf16[2304,512]{1,0:T(8,128)(2,1)} async-done(((bf16[288,512]{1,0:T(8,128)(2,1)}), bf16[2304,512]{1,0:T(8,128)(2,1)}) %all-gather.14.cloned.1.call-update) | async-done | bytes 2359312 | tf_op jit(solution)/shard_map/all_gather | solution.py:89
  155.5 7.0 all_gather.57
  163.4 69.3 %all-gather.16.cloned.1.call-done = bf16[2304,1024]{1,0:T(8,128)(2,1)} async-done(((bf16[288,1024]{1,0:T(8,128)(2,1)}), bf16[2304,1024]{1,0:T(8,128)(2,1)}) %all-gather.16.cloned.1.call-update) | async-done | bytes 4718608 | tf_op jit(solution)/shard_map/all_gather | solution.py:88
  240.9 71.9 %all-gather.18.cloned.1.call-done = bf16[1024,2304]{0,1:T(8,128)(2,1)} async-done(((bf16[1024,288]{0,1:T(8,128)(2,1)}), bf16[1024,2304]{0,1:T(8,128)(2,1)}) %all-gather.18.cloned.1.call-update) | async-done | bytes 4718608 | tf_op jit(solution)/shard_map/all_gather | solution.py:91
  312.8 5.2 fusion.131
  321.9 15.7 all-reduce.10.cloned.1.call-done
  343.8 403.2 %all-gather.20.cloned.1.call-done = bf16[2304,4608]{1,0:T(8,128)(2,1)} async-done(((bf16[288,4608]{1,0:T(8,128)(2,1)}), bf16[2304,4608]{1,0:T(8,128)(2,1)}) %all-gather.20.cloned.1.call-update) | async-done | bytes 21233680 | tf_op jit(solution)/shard_map/all_gather | solution.py:101
  747.0 14.3 fusion.132
  761.3 393.9 %all-gather.22.cloned.1.call-done = bf16[2304,4608]{1,0:T(8,128)(2,1)} async-done(((bf16[288,4608]{1,0:T(8,128)(2,1)}), bf16[2304,4608]{1,0:T(8,128)(2,1)}) %all-gather.22.cloned.1.call-update) | async-done | bytes 21233680 | tf_op jit(solution)/shard_map/all_gather | solution.py:102
  1155.2 16.5 multiply_convert_fusion.1
  1171.7 391.8 %all-gather.24.cloned.1.call-done = bf16[4608,2304]{0,1:T(8,128)(2,1)} async-done(((bf16[4608,288]{0,1:T(8,128)(2,1)}), bf16[4608,2304]{0,1:T(8,128)(2,1)}) %all-gather.24.cloned.1.call-update) | async-done | bytes 21233680 | tf_op jit(solution)/shard_map/all_gather | solution.py:103
  1563.5 12.3 fusion.133
  1577.7 19.5 all-reduce.12.cloned.1.call-done
  1604.6 12.0 multiply_convert_fusion
  1616.6 13.3 fusion.134
  1629.9 12.6 convolution_add_fusion.2
  1644.0 21.0 all-reduce.14.cloned.1.call-done
  1696.8 5.2 fusion.135
  1707.7 11.9 reduce-scatter.12.cloned.1.call-done
  1724.9 5.2 fusion.136
  1738.4 6.5 all-reduce.16.cloned.1.call-done
  1753.0 18.1 pad_maximum_fusion.1
  1771.1 27.8 copy.94
  1800.1 18.2 fusion.137
  1818.4 29.6 fusion.7
  1848.0 85.1 %pad_maximum_fusion = f32[2304,13824]{1,0:T(8,128)} fusion(f32[2304,4608]{1,0:T(8,128)} %fusion.137, f32[2304,9216]{1,0:T(8,128)} %fusion.7), kind=kLoop, calls=%fused_computation.4 | loop fusion | flops 31850496 | bytes 254803968 | tf_op jit(solution)/shard_map/concatenate | solution.py:207
  1945.9 367.3 %reduce-scatter.16.cloned.1.call-done = f32[144,3072]{1,0:T(8,128)} async-done(((f32[2304,3072]{1,0:T(8,128)}), f32[144,3072]{1,0:T(8,128)}) %reduce-scatter.16.cloned.1.call-update) | async-done | bytes 1769488
  2317.4 1812.4 %reduce-scatter.14.cloned.1.call-done = f32[144,13824]{1,0:T(8,128)} async-done(((f32[2304,13824]{1,0:T(8,128)}), f32[144,13824]{1,0:T(8,128)}) %reduce-scatter.14.cloned.1.call-update) | async-done | bytes 7962640 | tf_op jit(solution)/shard_map/reduce_scatter | solution.py:206
  4129.8 6.8 slice_bitcast_fusion
  (287 shorter events, 125.0 us)
Async XLA Ops:
  7.2 45.9 %copy-start.39 = (s32[1,448]{1,0:T(1,128)S(1)}, s32[1,448]{1,0:T(1,128)}, u32[]{:S(2)}) copy-start(s32[1,448]{1,0:T(1,128)} %param.20) | copy-start | bytes 5380
  7.2 48.6 %all-gather.10.cloned.1.call-start = ((), (), s32[]{:S(2)}) async-start(), calls=%async_computation.5 | async-start | bytes 3096576 | tf_op jit(solution)/shard_map/all_gather | solution.py:142
  8.0 91.4 %all-gather.12.cloned.1.call-start = ((), (), s32[]{:S(2)}) async-start(), calls=%async_computation.6 | async-start | bytes 2654208 | tf_op jit(solution)/shard_map/all_gather | solution.py:90
  8.7 143.5 %all-gather.14.cloned.1.call-start = ((), (), s32[]{:S(2)}) async-start(), calls=%async_computation.7 | async-start | bytes 2654208 | tf_op jit(solution)/shard_map/all_gather | solution.py:89
  9.5 223.3 %all-gather.16.cloned.1.call-start = ((), (), s32[]{:S(2)}) async-start(), calls=%async_computation.8 | async-start | bytes 5308416 | tf_op jit(solution)/shard_map/all_gather | solution.py:88
  10.0 302.8 %all-gather.18.cloned.1.call-start = ((), (), s32[]{:S(2)}) async-start(), calls=%async_computation.9 | async-start | bytes 5308416 | tf_op jit(solution)/shard_map/all_gather | solution.py:91
  10.6 326.9 %all-reduce.10.cloned.1.call-start = ((), (), s32[]{:S(2)}) async-start(), calls=%async_computation.10 | async-start | bytes 4128768 | tf_op jit(solution)/shard_map/psum | solution.py:74
  53.4 98.9 %copy-start.41 = (pred[224]{0:T(512)(128)(4,1)}, pred[224]{0:T(512)(128)(4,1)S(1)}, u32[]{:S(2)}) copy-start(pred[224]{0:T(512)(128)(4,1)S(1)} %compare_and_fusion.2) | copy-start | bytes 676
  53.4 179.3 %copy-start.25 = (f32[2304]{0:T(1024)}, f32[2304]{0:T(1024)S(1)}, u32[]{:S(2)}) copy-start(f32[2304]{0:T(1024)S(1)} %convert_add_fusion.5) | copy-start | bytes 27652
  60.9 91.3 %copy-start.37 = (f32[224]{0:T(256)}, f32[224]{0:T(256)S(1)}, u32[]{:S(2)}) copy-start(f32[224]{0:T(256)S(1)} %fusion.85) | copy-start | bytes 2692
  240.9 77.2 %copy-start.18 = (bf16[224,1024]{1,0:T(8,128)(2,1)}, bf16[224,1024]{1,0:T(8,128)(2,1)S(1)}, u32[]{:S(2)}) copy-start(bf16[224,1024]{1,0:T(8,128)(2,1)S(1)} %convert_element_type.139) | copy-start | bytes 1376260
  318.1 428.9 %all-gather.20.cloned.1.call-start = ((), (), s32[]{:S(2)}) async-start(), calls=%async_computation.11 | async-start | bytes 23887872 | tf_op jit(solution)/shard_map/all_gather | solution.py:101
  318.9 836.4 %all-gather.22.cloned.1.call-start = ((), (), s32[]{:S(2)}) async-start(), calls=%async_computation.12 | async-start | bytes 23887872 | tf_op jit(solution)/shard_map/all_gather | solution.py:102
  319.6 1243.9 %all-gather.24.cloned.1.call-start = ((), (), s32[]{:S(2)}) async-start(), calls=%async_computation.13 | async-start | bytes 23887872 | tf_op jit(solution)/shard_map/all_gather | solution.py:103
  320.4 1276.8 %all-reduce.12.cloned.1.call-start = ((), (), s32[]{:S(2)}) async-start(), calls=%async_computation.14 | async-start | bytes 4128768 | tf_op jit(solution)/shard_map/psum | solution.py:74
  1575.8 89.2 %all-reduce.14.cloned.1.call-start = ((), (), s32[]{:S(2)}) async-start(), calls=%async_computation.15 | async-start | bytes 4128768 | tf_op jit(solution)/shard_map/psum | solution.py:74
  1603.8 12.7 copy-start.7
  1616.6 13.3 copy-start.14
  1616.6 13.3 copy-start.12
  1642.5 60.2 %reduce-scatter.10.cloned.1.call-start = ((), (), s32[]{:S(2)}) async-start(), calls=%async_computation.16 | async-start | bytes 688128 | tf_op jit(solution)/shard_map/reduce_scatter | solution.py:248
  1665.0 8.7 slice-start
  1687.6 32.0 reduce-scatter.12.cloned.1.call-start
  1696.6 48.3 %all-reduce.16.cloned.1.call-start = ((), (), s32[]{:S(2)}) async-start(), calls=%async_computation.18 | async-start | bytes 4128768 | tf_op jit(solution)/shard_map/psum | solution.py:74
  1723.5 213.3 %reduce-scatter.18.cloned.1.call-start = ((), (), s32[]{:S(2)}) async-start(), calls=%async_computation.22 | async-start | bytes 1253376
  1738.4 8.8 copy-start.55
  1738.4 10.4 copy-start.4
  1748.7 191.9 %all-gather.26.cloned.1.call-start = ((), (), s32[]{:S(2)}) async-start(), calls=%async_computation.19 | async-start | bytes 3096576 | tf_op jit(solution)/shard_map/all_gather | solution.py:288
  1752.0 561.1 %reduce-scatter.16.cloned.1.call-start = ((), (), s32[]{:S(2)}) async-start(), calls=%async_computation.21 | async-start | bytes 30081024
  1798.9 19.4 copy-start.11
  1798.9 2330.8 %reduce-scatter.14.cloned.1.call-start = ((), (), s32[]{:S(2)}) async-start(), calls=%async_computation.20 | async-start | bytes 135364608 | tf_op jit(solution)/shard_map/reduce_scatter | solution.py:206
  1800.1 18.3 copy-start.13
  1800.1 18.3 copy-start.15
  (56 other events, 170.6 us)
Sparse Core Ops, SparseCore 0:
  9.6 35.4 all-gather.9
  47.3 52.0 all-gather.11
  101.6 50.6 all-gather.13
  154.3 78.4 all-gather.15
  234.8 78.0 all-gather.17
  318.2 19.2 all-reduce.9
  339.1 407.8 all-gather.19
  748.5 406.6 all-gather.21
  1156.8 406.6 all-gather.23
  1576.0 21.1 all-reduce.11
  1642.6 22.3 all-reduce.13
  1687.7 14.9 reduce-scatter.9
  1705.7 13.8 reduce-scatter.11
  1723.7 21.1 all-reduce.15
  1750.0 124.7 reduce-scatter.17
  1876.8 31.7 all-gather.25
  1914.2 398.8 reduce-scatter.15
  2319.0 1810.7 reduce-scatter.13
where the time goes:
time: 4150 us; the launch traced here: 4140 us
  waiting for transfers between devices  3670 us (88%)
  matrix products  186 us (4%)
  other arithmetic  137 us (3%)
  local copies, waits for them, and re-layouts  75.6 us (2%)
  blocking collectives  53.3 us (1%)
    reduce_scatter x1, waiting for transfers between devices, local(): lax.psum_scatter(jnp.concatenate([jnp.einsum('rc,rf->cf', normed_ffn, d_g...  1810 us
    all_gather x1, waiting for transfers between devices, ffn_weights(): lax.all_gather(gate_weight, 'fsdp', axis=0, tiled=True)  403 us
    all_gather x1, waiting for transfers between devices, ffn_weights(): lax.all_gather(up_weight, 'fsdp', axis=0, tiled=True)  394 us
    all_gather x1, waiting for transfers between devices, ffn_weights(): lax.all_gather(down_weight, 'fsdp', axis=1, tiled=True)  392 us
    unnamed x20, waiting for transfers between devices  373 us
    concatenate x1, other arithmetic, local(): jnp.concatenate([jnp.einsum('rc,rf->cf', normed_ffn, d_gate_up, preferred...  85.1 us
  transfers between devices with their start and end apart: 18, of which 15 were waited for; matrix products, arithmetic and copies ran while one was open for 7% of the time, Pallas kernels for 0%

commit v1 on v0

v1 whole, which is shorter than its diff:
```python
import functools

import jax
import jax.numpy as jnp
from jax import lax
from jax.sharding import PartitionSpec as P

HEAD_DIM = 256

eps_norm = 1e-06
soft_cap = 50.0
f32 = jnp.float32
b16 = jnp.bfloat16


def rms_scale(field, gain_vec):
    factor = lax.rsqrt(jnp.mean(field * field, axis=-1, keepdims=True) + eps_norm)
    return field * factor * (1.0 + gain_vec)


def gelu_tanh(value_in):
    return (
        0.5
        * value_in
        * (
            1.0
            + jnp.tanh(0.7978845608028654 * (value_in + 0.044715 * value_in * value_in * value_in))
        )
    )


def glu_apply(gate_act, up_act):
    return gelu_tanh(gate_act) * up_act


def norm_back(field, gain_vec, cot_in):
    pullback = jax.vjp(rms_scale, field, gain_vec)[1]
    return pullback(cot_in)


def placement_of(doc_lengths, packed):
    doc_ends = jnp.cumsum(doc_lengths)
    after_end = packed[:, None] >= doc_ends[None, :]
    segment = jnp.sum(after_end.astype(jnp.int32), axis=1)
    inner = packed - jnp.sum(jnp.where(after_end, doc_lengths[None, :], 0), axis=1)
    return (segment, inner)


def angles_of(inner, head_size):
    half_size = head_size // 2
    freq = jnp.power(10000.0, -jnp.arange(half_size, dtype=f32) * (2.0 / head_size))
    return inner.astype(f32)[:, None] * freq[None, :]


def rotate(field, angles):
    half_size = field.shape[-1] // 2
    cosine = jnp.cos(angles)[:, None, :]
    sine = jnp.sin(angles)[:, None, :]
    first_half = field[..., :half_size]
    second_half = field[..., half_size:]
    return jnp.concatenate(
        [first_half * cosine - second_half * sine, second_half * cosine + first_half * sine],
        axis=-1,
    )


def dot(lhs, rhs, dims):
    return lax.dot_general(lhs, rhs, (dims, ((), ())), preferred_element_type=f32)


def swap(piece, axis):
    return lax.ppermute(piece, axis, [(0, 1), (1, 0)])


def hop(piece, step, n):
    return lax.ppermute(piece, "fsdp", [(d, d ^ step) for d in range(n)])


def gather_rows(own, n):
    have = [own]
    bit = n // 2
    while bit:
        have = have + [hop(piece, bit, n) for piece in have]
        bit //= 2
    mine = jnp.concatenate(have)
    return jnp.concatenate([mine, swap(mine, "tp")])


def scatter_rows(part, n):
    rows = part.shape[0] // (2 * n)
    most = n * rows
    both = part[:most] + swap(part[most:].astype(b16), "tp").astype(f32)
    blocks = [both[k * rows : (k + 1) * rows] for k in range(n)]
    bit = 1
    while bit < n:
        keep = len(blocks) // 2
        blocks = [
            blocks[k] + hop(blocks[keep + k].astype(b16), bit, n).astype(f32) for k in range(keep)
        ]
        bit *= 2
    return blocks[0]


def gather_group(own):
    across = swap(own, "ctx")
    beside = swap(jnp.concatenate([own, across]), "tp")
    rows = own.shape[0]
    return jnp.concatenate([own, beside[:rows], across, beside[rows:]])


def scatter_group(part):
    rows = part.shape[0] // 4
    b0, b1, b2, b3 = [part[k * rows : (k + 1) * rows] for k in range(4)]
    got = swap(jnp.concatenate([b1, b3]), "tp")
    return b0 + got[:rows] + swap(b2 + got[rows:], "ctx")


def natural(own, other, index, axis):
    first = jnp.where(index == 0, own, other)
    second = jnp.where(index == 0, other, own)
    return jnp.concatenate([first, second], axis=axis)


def local(
    n,
    tokens,
    cotangent,
    lengths,
    positions,
    query_weight,
    key_weight,
    value_weight,
    output_weight,
    gate_weight,
    up_weight,
    down_weight,
    gain_attn_in,
    gain_attn_out,
    gain_ffn_in,
    gain_ffn_out,
):
    me = lax.axis_index("fsdp")
    ctx = lax.axis_index("ctx")
    tp = lax.axis_index("tp")
    tok_rows, width = tokens.shape
    rows = tok_rows // 2
    head_size = HEAD_DIM
    d_rows = query_weight.shape[0]
    d_half = d_rows // 2
    q_cols = query_weight.shape[1] // 2
    k_cols = key_weight.shape[1] // 2
    q_local = q_cols // head_size
    kv_local = k_cols // head_size
    group_size = q_local // kv_local
    query_scale = head_size ** (-0.5)
    ff_local = gate_weight.shape[1]
    ff_own = ff_local // n

    starts = [
        c * tok_rows + t * rows for c in (ctx, 1 - ctx) for t in (tp, 1 - tp)
    ]
    packed = jnp.concatenate(
        [lax.dynamic_slice_in_dim(positions[0], start, rows) for start in starts]
    )
    segment, inner = placement_of(lengths[0], packed)
    angles = angles_of(inner, head_size)
    allowed = (segment[:, None] == segment[None, :]) & (inner[None, :] <= inner[:, None])

    mine = lax.dynamic_slice_in_dim(tokens, tp * rows, rows)
    across = swap(mine, "ctx")
    beside = swap(across, "tp")
    seq_group = jnp.concatenate([tokens, across, beside])
    row_ids = jnp.arange(rows, dtype=jnp.int32)
    seq_ids = jnp.concatenate(
        [ctx * tok_rows + jnp.arange(tok_rows, dtype=jnp.int32), starts[2] + row_ids, starts[3] + row_ids]
    )
    pick = (packed[:, None] == seq_ids[None, :]).astype(b16)
    slot_in = dot(pick, seq_group, ((1,), (0,)))
    resid_in = slot_in[:rows]

    qkv_own = jnp.concatenate(
        [
            lax.dynamic_slice_in_dim(query_weight, ctx * q_cols, q_cols, 1),
            lax.dynamic_slice_in_dim(key_weight, ctx * k_cols, k_cols, 1),
            lax.dynamic_slice_in_dim(value_weight, ctx * k_cols, k_cols, 1),
        ],
        axis=1,
    )
    qkv_weight = lax.all_gather(qkv_own, "fsdp", axis=0, tiled=True)
    out_own = lax.dynamic_slice_in_dim(output_weight, ctx * q_cols, q_cols, 0).T
    out_weight = lax.all_gather(out_own, "fsdp", axis=0, tiled=True)
    gains = lax.all_gather(
        jnp.concatenate([gain_attn_in, gain_attn_out, gain_ffn_in, gain_ffn_out])
        .astype(f32)
        .reshape(1, 4 * d_rows),
        "fsdp",
        axis=0,
        tiled=True,
    )
    gains = gains.reshape(n, 4, d_rows).transpose(1, 0, 2).reshape(4, width)

    ffn_own = jnp.stack([gate_weight, up_weight, down_weight.T])
    ffn_own = ffn_own.reshape(3, 2, d_half, n, ff_own).transpose(3, 1, 0, 2, 4)
    ffn_own = lax.dynamic_index_in_dim(ffn_own, ctx, 1, keepdims=False)
    ffn_full = [jnp.zeros((n, 2, d_half, ff_own), b16) for _ in range(3)]
    for k in range(n):
        piece = lax.dynamic_index_in_dim(ffn_own, me ^ k, 0, keepdims=False)
        if k:
            piece = hop(piece, k, n)
        second = swap(piece, "ctx")
        for which in range(3):
            for half, side in ((piece, ctx), (second, 1 - ctx)):
                ffn_full[which] = lax.dynamic_update_slice(
                    ffn_full[which], half[which][None, None], (me ^ k, side, 0, 0)
                )
    gate_full, up_full, down_full = [full.reshape(width, ff_own) for full in ffn_full]

    normed_attn = rms_scale(slot_in, gains[0]).astype(b16)
    qkv = dot(normed_attn, qkv_weight, ((1,), (0,)))
    all_rows = 2 * tok_rows
    query_lin = qkv[:, :q_cols].reshape(all_rows, q_local, head_size)
    key_lin = qkv[:, q_cols : q_cols + k_cols].reshape(all_rows, kv_local, head_size)
    values = qkv[:, q_cols + k_cols :].astype(b16).reshape(all_rows, kv_local, head_size)
    queries = (rotate(query_lin, angles) * query_scale).astype(b16)
    queries = queries.reshape(all_rows, kv_local, group_size, head_size)
    keys = rotate(key_lin, angles).astype(b16)
    raw_scores = jnp.einsum("qkgd,skd->kgqs", queries, keys, preferred_element_type=f32)
    tanh_ratio = jnp.tanh(raw_scores / soft_cap)
    masked = jnp.where(allowed[None, None], soft_cap * tanh_ratio, -1e30)
    row_peak = jnp.max(masked, axis=-1, keepdims=True)
    exp_terms = jnp.exp(masked - row_peak)
    probs = exp_terms / jnp.sum(exp_terms, axis=-1, keepdims=True)
    probs_low = probs.astype(b16)
    attended = (
        jnp.einsum("kgqs,skd->qkgd", probs_low, values, preferred_element_type=f32)
        .reshape(all_rows, q_cols)
        .astype(b16)
    )
    attn_out = scatter_group(dot(attended, out_weight, ((1,), (1,))))
    middle = resid_in + rms_scale(attn_out, gains[1])

    normed_ffn = gather_rows(rms_scale(middle, gains[2]).astype(b16), n)
    gate_act = dot(normed_ffn, gate_full, ((1,), (0,)))
    up_act = dot(normed_ffn, up_full, ((1,), (0,)))
    hidden = glu_apply(gate_act, up_act).astype(b16)
    ffn_out = scatter_rows(dot(hidden, down_full, ((1,), (1,))), n)
    block_own = (middle + rms_scale(ffn_out, gains[3])).astype(b16)
    block_out = natural(block_own, swap(block_own, "tp"), tp, 0)

    d_out = lax.dynamic_slice_in_dim(cotangent, tp * rows, rows).astype(f32)
    d_ffn_raw, gain_four_term = norm_back(ffn_out, gains[3], d_out)
    d_ffn_out = gather_rows(d_ffn_raw.astype(b16), n)
    d_hidden = dot(d_ffn_out, down_full, ((1,), (0,)))
    d_gate_raw, d_up_raw = jax.vjp(glu_apply, gate_act, up_act)[1](d_hidden)
    d_gate = d_gate_raw.astype(b16)
    d_up = d_up_raw.astype(b16)
    d_normed_ffn = scatter_rows(
        dot(d_gate, gate_full, ((1,), (1,))) + dot(d_up, up_full, ((1,), (1,))), n
    )
    ffn_terms = [
        dot(normed_ffn, d_gate, ((0,), (0,))),
        dot(normed_ffn, d_up, ((0,), (0,))),
        dot(d_ffn_out, hidden, ((0,), (0,))),
    ]
    ffn_terms = [term.reshape(n, 2, d_half, ff_own) for term in ffn_terms]
    ffn_keep = [lax.dynamic_index_in_dim(term, ctx, 1, keepdims=False) for term in ffn_terms]
    ffn_send = [
        lax.dynamic_index_in_dim(term, 1 - ctx, 1, keepdims=False).astype(b16)
        for term in ffn_terms
    ]
    ffn_sum = [keep + swap(send, "ctx").astype(f32) for keep, send in zip(ffn_keep, ffn_send)]
    ffn_low = jnp.stack([term.astype(b16) for term in ffn_sum], axis=1)
    ffn_grads = ffn_sum
    for k in range(1, n):
        piece = hop(lax.dynamic_index_in_dim(ffn_low, me ^ k, 0, keepdims=False), k, n)
        ffn_grads = [
            lax.dynamic_update_index_in_dim(grad, piece[which].astype(f32), me ^ k, 0)
            for which, grad in enumerate(ffn_grads)
        ]
    gate_weight_grad = ffn_grads[0].transpose(1, 0, 2).reshape(d_half, ff_local)
    up_weight_grad = ffn_grads[1].transpose(1, 0, 2).reshape(d_half, ff_local)
    down_weight_grad = ffn_grads[2].transpose(0, 2, 1).reshape(ff_local, d_half)

    d_middle_part, gain_three_term = norm_back(middle, gains[2], d_normed_ffn)
    d_middle = d_out + d_middle_part
    d_attn_raw, gain_two_term = norm_back(attn_out, gains[1], d_middle)
    d_attn_out = gather_group(d_attn_raw.astype(b16))
    d_attended = dot(d_attn_out, out_weight, ((1,), (0,))).astype(b16)
    d_att = d_attended.reshape(all_rows, kv_local, group_size, head_size)
    d_probs = jnp.einsum("qkgd,skd->kgqs", d_att, values, preferred_element_type=f32)
    d_soft = probs * (d_probs - jnp.sum(probs * d_probs, axis=-1, keepdims=True))
    d_scores = (d_soft * (1.0 - tanh_ratio * tanh_ratio)).astype(b16)
    d_queries = jnp.einsum("kgqs,skd->qkgd", d_scores, keys, preferred_element_type=f32)
    d_keys = jnp.einsum("kgqs,qkgd->skd", d_scores, queries, preferred_element_type=f32)
    d_values = jnp.einsum("kgqs,qkgd->skd", probs_low, d_att, preferred_element_type=f32)
    d_query_lin = (
        rotate(d_queries.reshape(all_rows, q_local, head_size) * query_scale, -angles)
        .reshape(all_rows, q_cols)
        .astype(b16)
    )
    d_key_lin = rotate(d_keys, -angles).reshape(all_rows, k_cols).astype(b16)
    d_value = d_values.reshape(all_rows, k_cols).astype(b16)
    d_qkv = jnp.concatenate([d_query_lin, d_key_lin, d_value], axis=1)
    d_normed_attn = scatter_group(dot(d_qkv, qkv_weight, ((1,), (1,))))
    resid_part, gain_one_term = norm_back(resid_in, gains[0], d_normed_attn)
    slot_grad = gather_group((d_middle + resid_part).astype(b16))
    place = (
        (ctx * tok_rows + jnp.arange(tok_rows, dtype=jnp.int32))[:, None] == packed[None, :]
    ).astype(b16)
    tokens_grad = dot(place, slot_grad, ((1,), (0,))).astype(b16)

    attn_terms = jnp.concatenate(
        [
            dot(normed_attn, d_qkv, ((0,), (0,))),
            dot(d_attn_out, attended, ((0,), (0,))),
        ],
        axis=1,
    ).astype(b16)
    attn_rows = lax.psum_scatter(attn_terms, "fsdp", scatter_dimension=0, tiled=True)
    attn_rows = attn_rows.reshape(2, d_half, -1)
    attn_own = lax.dynamic_index_in_dim(attn_rows, ctx, 0, keepdims=False)
    attn_other = swap(lax.dynamic_index_in_dim(attn_rows, 1 - ctx, 0, keepdims=False), "ctx")
    edges = [0, q_cols, q_cols + k_cols, q_cols + 2 * k_cols, 2 * q_cols + 2 * k_cols]
    attn_grads = [
        natural(attn_own[:, a:b].astype(f32), attn_other[:, a:b].astype(f32), ctx, 1)
        for a, b in zip(edges[:-1], edges[1:])
    ]

    gain_terms = jnp.stack([gain_one_term, gain_two_term, gain_three_term, gain_four_term])
    gain_terms = gain_terms.reshape(4, 2 * n, d_half).transpose(1, 0, 2).reshape(2 * n, 4 * d_half)
    gain_terms = gain_terms + swap(gain_terms, "tp")
    gain_rows = lax.psum_scatter(gain_terms, ("fsdp", "ctx"), scatter_dimension=0, tiled=True)
    gain_rows = gain_rows.reshape(4, d_half)
    return (
        block_out,
        tokens_grad,
        attn_grads[0],
        attn_grads[1],
        attn_grads[2],
        attn_grads[3].T,
        gate_weight_grad,
        up_weight_grad,
        down_weight_grad,
        gain_rows[0],
        gain_rows[1],
        gain_rows[2],
        gain_rows[3],
    )


def solution(mesh):
    in_specs = (
        P(("fsdp", "ctx"), None),
        P(("fsdp", "ctx"), None),
        P("fsdp", None),
        P("fsdp", None),
        P("fsdp", "tp"),
        P("fsdp", "tp"),
        P("fsdp", "tp"),
        P("tp", "fsdp"),
        P("fsdp", "tp"),
        P("fsdp", "tp"),
        P("tp", "fsdp"),
        P("fsdp"),
        P("fsdp"),
        P("fsdp"),
        P("fsdp"),
    )
    out_specs = (
        P(("fsdp", "ctx"), None),
        P(("fsdp", "ctx"), None),
        P(("fsdp", "ctx"), "tp"),
        P(("fsdp", "ctx"), "tp"),
        P(("fsdp", "ctx"), "tp"),
        P("tp", ("fsdp", "ctx")),
        P(("fsdp", "ctx"), "tp"),
        P(("fsdp", "ctx"), "tp"),
        P("tp", ("fsdp", "ctx")),
        P(("fsdp", "ctx")),
        P(("fsdp", "ctx")),
        P(("fsdp", "ctx")),
        P(("fsdp", "ctx")),
    )
    step = functools.partial(local, mesh.shape["fsdp"])
    return jax.shard_map(step, mesh=mesh, in_specs=in_specs, out_specs=out_specs, check_vma=False)
```

time: 4150 us -> 1160 us (0.28)
  waiting for transfers between devices: 3670 us -> 571 us
  local copies, waits for them, and re-layouts: 75.6 us -> 158 us
  starting transfers between devices: 2.07 us -> 71.3 us
  blocking collectives: 53.3 us -> 122 us
  other arithmetic: 137 us -> 80.2 us
  matrix products: 186 us -> 132 us
    reduce_scatter x3 -> x1, waiting for transfers between devices: 1820 us -> 0.01 us  [local(): lax.psum_scatter(attn_terms, 'fsdp', scatter_dimension=0, tiled=True)]
    all_gather x9 -> x2, waiting for transfers between devices: 1410 us -> 77.8 us  [the longest x1 40 us: local(): qkv_weight = lax.all_gather(qkv_own, 'fsdp', axis=0, tiled=True)]
    ppermute x0 -> x70, waiting for transfers between devices: none -> 493 us  [the longest x42 338 us: hop(): return lax.ppermute(piece, 'fsdp', [(d, d ^ step) for d in range(n)])]
    unnamed x20 -> x3, waiting for transfers between devices: 373 us -> 0.05 us
    concatenate x2 -> x11, other arithmetic: 103 us -> 13 us  [the longest x1 5.62 us: local(): jnp.concatenate([dot(normed_attn, d_qkv, ((0,), (0,))), dot(d_attn_out, a...]
    ppermute x0 -> x70, starting transfers between devices: none -> 71.2 us  [the longest x42 51.9 us: hop(): return lax.ppermute(piece, 'fsdp', [(d, d ^ step) for d in range(n)])]
    psum x4 -> x0, waiting for transfers between devices: 62.6 us -> none  [tp_total(): return lax.psum(partial_sum, 'tp')]
    dot_general x26 -> x23, matrix products: 186 us -> 132 us  [the longest x17 125 us: dot(): lax.dot_general(lhs, rhs, (dims, ((), ())), preferred_element_type=f32)]
  transfers between devices with their start and end apart: 18 -> 73, of which waited for: 15 -> 48; matrix products, arithmetic and copies ran while one was open for 7% -> 16% of each run, Pallas kernels for 0% -> 0%
where the time goes in v1:
time: 1160 us; the launch traced here: 1150 us
  waiting for transfers between devices  571 us (49%)
  local copies, waits for them, and re-layouts  158 us (14%)
  matrix products  132 us (11%)
  blocking collectives  122 us (11%)
  other arithmetic  80.2 us (7%)
  starting transfers between devices  71.3 us (6%)
  between operations  16.4 us (1%)
    ppermute x42, waiting for transfers between devices, hop(): return lax.ppermute(piece, 'fsdp', [(d, d ^ step) for d in range(n)])  338 us
    ppermute x28, waiting for transfers between devices, swap(): return lax.ppermute(piece, axis, [(0, 1), (1, 0)])  155 us
    dot_general x17, matrix products, dot(): lax.dot_general(lhs, rhs, (dims, ((), ())), preferred_element_type=f32)  125 us
    unnamed x1, blocking collectives  90.6 us
    unnamed x207, local copies, waits for them, and re-layouts  58.9 us
    ppermute x42, starting transfers between devices, hop(): return lax.ppermute(piece, 'fsdp', [(d, d ^ step) for d in range(n)])  51.9 us
    all_gather x1, waiting for transfers between devices, local(): qkv_weight = lax.all_gather(qkv_own, 'fsdp', axis=0, tiled=True)  40 us
    all_gather x1, waiting for transfers between devices, local(): out_weight = lax.all_gather(out_own, 'fsdp', axis=0, tiled=True)  37.8 us
  transfers between devices with their start and end apart: 73, of which 48 were waited for; matrix products, arithmetic and copies ran while one was open for 16% of the time, Pallas kernels for 0%

profile of v1, /device:TPU:0, one launch (start us, length us, event | category | flops | bytes accessed | tf_op | source)
XLA Modules:
  0.0 1150.1 jit_solution(1037541501683271396)
XLA Ops:
  15.2 31.4 %all-gather = f32[8,1,1152]{2,1,0:T(1,128)S(1)} all-gather(f32[1,1,1152]{2,1,0:T(1,128)S(1)} %bitcast_convert_fusion.2), channel_id=1, replica_groups=mesh['fsdp'=8,'ctx'=2,'tp'=2] {'fsdp'}, dimensions={0}, use_global_device_ids=true | all-gather | bytes 41472 | tf_op jit(solution)/shard_map/all_gather | solution.py:192
  53.8 40.0 %all-gather.4.cloned.1.call-done = bf16[2304,1024]{1,0:T(8,128)(2,1)} async-done(((bf16[288,1024]{1,0:T(8,128)(2,1)}), bf16[2304,1024]{1,0:T(8,128)(2,1)}) %all-gather.4.cloned.1.call-update) | async-done | bytes 4718608 | tf_op jit(solution)/shard_map/all_gather | solution.py:189
  108.9 37.8 %all-gather.6.cloned.1.call-done = bf16[2304,512]{1,0:T(8,128)(2,1)} async-done(((bf16[288,512]{1,0:T(8,128)(2,1)}), bf16[2304,512]{1,0:T(8,128)(2,1)}) %all-gather.6.cloned.1.call-update) | async-done | bytes 2359312 | tf_op jit(solution)/shard_map/all_gather | solution.py:191
  211.9 22.0 %collective-permute-done.5 = bf16[112,2304]{1,0:T(8,128)(2,1)S(1)} collective-permute-done((bf16[112,2304]{1,0:T(8,128)(2,1)S(1)}, bf16[112,2304]{1,0:T(8,128)(2,1)S(1)}, u32[]{:S(2)}, u32[]{:S(2)}) %collective-permute-start.5) | collective-permute-done | bytes 516128 | tf_op jit(solution)/shard_map/ppermute | solution.py:76
  248.9 10.6 collective-permute-done.8
  271.4 21.1 %collective-permute-done.10 = bf16[112,2304]{1,0:T(8,128)(2,1)S(1)} collective-permute-done((bf16[112,2304]{1,0:T(8,128)(2,1)S(1)}, bf16[112,2304]{1,0:T(8,128)(2,1)S(1)}, u32[]{:S(2)}, u32[]{:S(2)}) %collective-permute-start.10) | collective-permute-done | bytes 516128 | tf_op jit(solution)/shard_map/ppermute | solution.py:76
  323.5 38.0 %collective-permute-done.19 = bf16[3,144,576]{2,1,0:T(8,128)(2,1)S(1)} collective-permute-done((bf16[3,144,576]{2,1,0:T(8,128)(2,1)}, bf16[3,144,576]{2,1,0:T(8,128)(2,1)S(1)}, u32[]{:S(2)}, u32[]{:S(2)}) %collective-permute-start.19) | collective-permute-done | bytes 497696 | tf_op jit(solution)/shard_map/ppermute | solution.py:76
  366.8 18.4 %collective-permute-done.21 = bf16[3,144,576]{2,1,0:T(8,128)(2,1)S(1)} collective-permute-done((bf16[3,144,576]{2,1,0:T(8,128)(2,1)}, bf16[3,144,576]{2,1,0:T(8,128)(2,1)S(1)}, u32[]{:S(2)}, u32[]{:S(2)}) %collective-permute-start.21) | collective-permute-done | bytes 497696 | tf_op jit(solution)/shard_map/ppermute | solution.py:76
  402.2 10.2 collective-permute-done.22
  438.4 11.5 %fusion.192 = f32[1792,576]{0,1:T(8,128)} fusion(bf16[1792,2304]{1,0:T(8,128)(2,1)S(1)} %constant_dynamic-update-slice_fusion.8, bf16[2304,576]{1,0:T(8,128)(2,1)} %bitcast.35), kind=kOutput, calls=%fused_computation.456 | convolution fusion | flops 4756340736 | bytes 15040512 | tf_op jit(solution)/shard_map/dot_general | solution.py:68
  449.9 14.4 %multiply_convert_fusion.1 = (bf16[1792,576]{0,1:T(8,128)(2,1)}, f32[1792,576]{0,1:T(8,128)}) fusion(f32[1792,576]{0,1:T(8,128)} %fusion.192, bf16[1792,2304]{1,0:T(8,128)(2,1)} %copy-done.57, bf16[2304,576]{1,0:T(8,128)(2,1)} %bitcast.52), kind=kOutput, calls=%fused_computation.20 | convolution fusion | flops 4766662656 | bytes 21233664 | tf_op jit(solution)/shard_map/dot_general | solution.py:68
  488.3 10.3 fusion.180
  504.5 11.1 collective-permute-done.32
  526.7 11.1 collective-permute-done.31
  548.1 15.2 %collective-permute-done.30 = bf16[112,2304]{1,0:T(8,128)(2,1)S(1)} collective-permute-done((bf16[112,2304]{1,0:T(8,128)(2,1)}, bf16[112,2304]{1,0:T(8,128)(2,1)S(1)}, u32[]{:S(2)}, u32[]{:S(2)}) %collective-permute-start.30) | collective-permute-done | bytes 516128 | tf_op jit(solution)/shard_map/ppermute | solution.py:76
  573.5 18.7 %collective-permute-done.36 = bf16[112,2304]{1,0:T(8,128)(2,1)S(1)} collective-permute-done((bf16[112,2304]{1,0:T(8,128)(2,1)S(1)}, bf16[112,2304]{1,0:T(8,128)(2,1)S(1)}, u32[]{:S(2)}, u32[]{:S(2)}) %collective-permute-start.36) | collective-permute-done | bytes 516128 | tf_op jit(solution)/shard_map/ppermute | solution.py:76
  594.4 11.5 collective-permute-done.38
  607.6 10.3 collective-permute-done.41
  641.3 12.4 %fusion.3 = (bf16[1792,576]{0,1:T(8,128)(2,1)S(1)}, bf16[1792,576]{0,1:T(8,128)(2,1)S(1)}) fusion(f32[1792,576]{0,1:T(8,128)S(1)} %copy-done.81, f32[1792,576]{0,1:T(8,128)} %get-tuple-element.226, bf16[1792,2304]{1,0:T(8,128)(2,1)} %copy-done.55, bf16[2304,576]{1,0:T(8,128)(2,1)S(1)} %bitcast.455), kind=kOutput, calls=%fused_computation.16 | convolution fusion | flops 4785242112 | bytes 23298048 | tf_op jit(solution)/shard_map/dot_general | solution.py:68
  653.7 13.6 %fusion.194 = f32[1792,2304]{1,0:T(8,128)} fusion(bf16[1792,576]{0,1:T(8,128)(2,1)S(1)} %get-tuple-element.63, bf16[2304,576]{1,0:T(8,128)(2,1)} %bitcast.52), kind=kOutput, calls=%fused_computation.458 | convolution fusion | flops 4756340736 | bytes 21233664 | tf_op jit(solution)/shard_map/dot_general | solution.py:68
  667.3 15.2 %convolution_add_fusion = f32[1792,2304]{1,0:T(8,128)} fusion(f32[1792,2304]{1,0:T(8,128)} %fusion.194, bf16[1792,576]{0,1:T(8,128)(2,1)S(1)} %get-tuple-element.62, bf16[2304,576]{1,0:T(8,128)(2,1)} %bitcast.35), kind=kOutput, calls=%fused_computation | convolution fusion | flops 4760469504 | bytes 37748736 | tf_op jit(solution)/shard_map/dot_general | solution.py:68
  693.5 10.3 fusion.177
  709.0 11.1 collective-permute-done.49
  731.2 11.1 collective-permute-done.48
  752.5 14.1 %collective-permute-done.47 = bf16[112,2304]{1,0:T(8,128)(2,1)S(1)} collective-permute-done((bf16[112,2304]{1,0:T(8,128)(2,1)S(1)}, bf16[112,2304]{1,0:T(8,128)(2,1)S(1)}, u32[]{:S(2)}, u32[]{:S(2)}) %collective-permute-start.47) | collective-permute-done | bytes 516128 | tf_op jit(solution)/shard_map/ppermute | solution.py:76
  804.8 10.3 copy.101
  865.8 28.8 %collective-permute-done.60 = bf16[8,144,576]{2,1,0:T(8,128)(2,1)} collective-permute-done((bf16[8,144,576]{2,1,0:T(8,128)(2,1)}, bf16[8,144,576]{2,1,0:T(8,128)(2,1)}, u32[]{:S(2)}, u32[]{:S(2)}) %collective-permute-start.60) | collective-permute-done | bytes 1327136 | tf_op jit(solution)/shard_map/ppermute | solution.py:72
  897.2 28.2 %collective-permute-done.61 = bf16[8,144,576]{2,1,0:T(8,128)(2,1)} collective-permute-done((bf16[8,144,576]{2,1,0:T(8,128)(2,1)}, bf16[8,144,576]{2,1,0:T(8,128)(2,1)}, u32[]{:S(2)}, u32[]{:S(2)}) %collective-permute-start.61) | collective-permute-done | bytes 1327136 | tf_op jit(solution)/shard_map/ppermute | solution.py:72
  959.9 16.9 %collective-permute-done.63 = bf16[3,144,576]{2,1,0:T(8,128)(2,1)S(1)} collective-permute-done((bf16[3,144,576]{2,1,0:T(8,128)(2,1)S(1)}, bf16[3,144,576]{2,1,0:T(8,128)(2,1)S(1)}, u32[]{:S(2)}, u32[]{:S(2)}) %collective-permute-start.63) | collective-permute-done | bytes 497696 | tf_op jit(solution)/shard_map/ppermute | solution.py:76
  978.4 11.1 collective-permute-done.64
  992.9 10.2 collective-permute-done.67
  1038.3 90.6 %all-reduce = f32[16,576]{1,0:T(8,128)S(1)} all-reduce(f32[16,576]{1,0:T(8,128)S(1)} %add.561), channel_id=3, replica_groups=mesh['fsdp'=8,'ctx'=2,'tp'=2] {'fsdp','ctx'}, use_global_device_ids=true, to_apply=%region_17.18.clone | all-reduce | flops 9216 | bytes 73728
  (503 shorter events, 506.4 us)
Async XLA Ops:
  7.3 86.5 %all-gather.4.cloned.1.call-start = ((), (), s32[]{:S(2)}) async-start(), calls=%async_computation.1 | async-start | bytes 5308416 | tf_op jit(solution)/shard_map/all_gather | solution.py:189
  10.2 136.4 %all-gather.6.cloned.1.call-start = ((), (), s32[]{:S(2)}) async-start(), calls=%async_computation.2 | async-start | bytes 2654208 | tf_op jit(solution)/shard_map/all_gather | solution.py:191
  10.3 37.3 %collective-permute-start = (bf16[112,2304]{1,0:T(8,128)(2,1)S(1)}, bf16[112,2304]{1,0:T(8,128)(2,1)S(1)}, u32[]{:S(2)}, u32[]{:S(2)}) collective-permute-start(bf16[112,2304]{1,0:T(8,128)(2,1)S(1)} %constant_dynamic-slice_fusion.11), channel_id=1, source_target_pairs={{0,2},{2,0},{1,3},{3,1},{4,6},{6,4},{5,7},{7,5},{8,10},{10,8},{9,1... | collective-permute-start | bytes 1548296 | tf_op jit(solution)/shard_map/ppermute | solution.py:72
  14.1 1116.0 %reduce-scatter.4.cloned.1.call-start = ((), (), s32[]{:S(2)}) async-start(), calls=%async_computation.3 | async-start | bytes 7962624 | tf_op jit(solution)/shard_map/reduce_scatter | solution.py:319
  198.0 114.1 %collective-permute-start.12 = (bf16[3,144,576]{2,1,0:T(8,128)(2,1)S(1)}, bf16[3,144,576]{2,1,0:T(8,128)(2,1)}, u32[]{:S(2)}, u32[]{:S(2)}) collective-permute-start(bf16[3,144,576]{2,1,0:T(8,128)(2,1)S(1)} %bitcast.457), channel_id=1, source_target_pairs={{0,2},{2,0},{1,3},{3,1},{4,6},{6,4},{5,7},{7,5},{8,10},{10,8},{9,1... | collective-permute-start | bytes 1493000 | tf_op jit(solution)/shard_map/ppermute | solution.py:72
  199.6 100.0 %collective-permute-start.13 = (bf16[3,144,576]{2,1,0:T(8,128)(2,1)S(1)}, bf16[3,144,576]{2,1,0:T(8,128)(2,1)}, u32[]{:S(2)}, u32[]{:S(2)}) collective-permute-start(bf16[3,144,576]{2,1,0:T(8,128)(2,1)S(1)} %bitcast.466), channel_id=1, source_target_pairs={{0,4},{4,0},{8,12},{12,8},{16,20},{20,16},{24,28},{28,24},{1,5},{5... | collective-permute-start | bytes 1493000 | tf_op jit(solution)/shard_map/ppermute | solution.py:76
  201.1 111.1 %collective-permute-start.15 = (bf16[3,144,576]{2,1,0:T(8,128)(2,1)}, bf16[3,144,576]{2,1,0:T(8,128)(2,1)}, u32[]{:S(2)}, u32[]{:S(2)}) collective-permute-start(bf16[3,144,576]{2,1,0:T(8,128)(2,1)} %bitcast.438), channel_id=1, source_target_pairs={{0,8},{4,12},{8,0},{12,4},{16,24},{20,28},{24,16},{28,20},{1,9},{5... | collective-permute-start | bytes 1493000 | tf_op jit(solution)/shard_map/ppermute | solution.py:76
  201.7 32.1 %collective-permute-start.5 = (bf16[112,2304]{1,0:T(8,128)(2,1)S(1)}, bf16[112,2304]{1,0:T(8,128)(2,1)S(1)}, u32[]{:S(2)}, u32[]{:S(2)}) collective-permute-start(bf16[112,2304]{1,0:T(8,128)(2,1)S(1)} %get-tuple-element.43), channel_id=1, source_target_pairs={{0,8},{4,12},{8,0},{12,4},{16,24},{20,28},{24,16},{28,20},{1,9},{5... | collective-permute-start | bytes 1548296 | tf_op jit(solution)/shard_map/ppermute | solution.py:76
  211.0 33.9 %collective-permute-start.6 = (bf16[112,2304]{1,0:T(8,128)(2,1)S(1)}, bf16[112,2304]{1,0:T(8,128)(2,1)S(1)}, u32[]{:S(2)}, u32[]{:S(2)}) collective-permute-start(bf16[112,2304]{1,0:T(8,128)(2,1)S(1)} %collective-permute-done.4), channel_id=1, source_target_pairs={{0,8},{4,12},{8,0},{12,4},{16,24},{20,28},{24,16},{28,20},{1,9},{5... | collective-permute-start | bytes 1548296 | tf_op jit(solution)/shard_map/ppermute | solution.py:76
  259.4 33.0 %collective-permute-start.10 = (bf16[112,2304]{1,0:T(8,128)(2,1)S(1)}, bf16[112,2304]{1,0:T(8,128)(2,1)S(1)}, u32[]{:S(2)}, u32[]{:S(2)}) collective-permute-start(bf16[112,2304]{1,0:T(8,128)(2,1)S(1)} %collective-permute-done.6), channel_id=1, source_target_pairs={{0,4},{4,0},{8,12},{12,8},{16,20},{20,16},{24,28},{28,24},{1,5},{5... | collective-permute-start | bytes 1548296 | tf_op jit(solution)/shard_map/ppermute | solution.py:76
  270.5 51.1 %collective-permute-start.17 = (bf16[3,144,576]{2,1,0:T(8,128)(2,1)S(1)}, bf16[3,144,576]{2,1,0:T(8,128)(2,1)}, u32[]{:S(2)}, u32[]{:S(2)}) collective-permute-start(bf16[3,144,576]{2,1,0:T(8,128)(2,1)S(1)} %bitcast.465), channel_id=1, source_target_pairs={{0,12},{4,8},{8,4},{12,0},{16,28},{20,24},{24,20},{28,16},{1,13},{... | collective-permute-start | bytes 1493000 | tf_op jit(solution)/shard_map/ppermute | solution.py:76
  293.3 142.6 %collective-permute-start.11 = (bf16[896,2304]{1,0:T(8,128)(2,1)}, bf16[896,2304]{1,0:T(8,128)(2,1)}, u32[]{:S(2)}, u32[]{:S(2)}) collective-permute-start(bf16[896,2304]{1,0:T(8,128)(2,1)} %get-tuple-element.191), channel_id=1, source_target_pairs={{0,1},{1,0},{2,3},{3,2},{4,5},{5,4},{6,7},{7,6},{8,9},{9,8},{10,11... | collective-permute-start | bytes 12386312 | tf_op jit(solution)/shard_map/ppermute | solution.py:72
  312.1 49.4 %collective-permute-start.19 = (bf16[3,144,576]{2,1,0:T(8,128)(2,1)}, bf16[3,144,576]{2,1,0:T(8,128)(2,1)S(1)}, u32[]{:S(2)}, u32[]{:S(2)}) collective-permute-start(bf16[3,144,576]{2,1,0:T(8,128)(2,1)} %bitcast.470), channel_id=1, source_target_pairs={{0,16},{4,20},{8,24},{12,28},{16,0},{20,4},{24,8},{28,12},{1,17},{... | collective-permute-start | bytes 1493000 | tf_op jit(solution)/shard_map/ppermute | solution.py:76
  312.2 51.3 %collective-permute-start.16 = (bf16[3,144,576]{2,1,0:T(8,128)(2,1)}, bf16[3,144,576]{2,1,0:T(8,128)(2,1)S(1)}, u32[]{:S(2)}, u32[]{:S(2)}) collective-permute-start(bf16[3,144,576]{2,1,0:T(8,128)(2,1)} %collective-permute-done.15), channel_id=1, source_target_pairs={{0,2},{2,0},{1,3},{3,1},{4,6},{6,4},{5,7},{7,5},{8,10},{10,8},{9,1... | collective-permute-start | bytes 1493000 | tf_op jit(solution)/shard_map/ppermute | solution.py:72
  316.9 68.3 %collective-permute-start.21 = (bf16[3,144,576]{2,1,0:T(8,128)(2,1)}, bf16[3,144,576]{2,1,0:T(8,128)(2,1)S(1)}, u32[]{:S(2)}, u32[]{:S(2)}) collective-permute-start(bf16[3,144,576]{2,1,0:T(8,128)(2,1)} %bitcast.469), channel_id=1, source_target_pairs={{0,20},{4,16},{8,28},{12,24},{16,4},{20,0},{24,12},{28,8},{1,21},{... | collective-permute-start | bytes 1493000 | tf_op jit(solution)/shard_map/ppermute | solution.py:76
  321.6 66.0 %collective-permute-start.23 = (bf16[3,144,576]{2,1,0:T(8,128)(2,1)S(1)}, bf16[3,144,576]{2,1,0:T(8,128)(2,1)S(1)}, u32[]{:S(2)}, u32[]{:S(2)}) collective-permute-start(bf16[3,144,576]{2,1,0:T(8,128)(2,1)S(1)} %bitcast.468), channel_id=1, source_target_pairs={{0,24},{4,28},{8,16},{12,20},{16,8},{20,12},{24,0},{28,4},{1,25},{... | collective-permute-start | bytes 1493000 | tf_op jit(solution)/shard_map/ppermute | solution.py:76
  389.1 35.2 %collective-permute-start.24 = (bf16[3,144,576]{2,1,0:T(8,128)(2,1)S(1)}, bf16[3,144,576]{2,1,0:T(8,128)(2,1)S(1)}, u32[]{:S(2)}, u32[]{:S(2)}) collective-permute-start(bf16[3,144,576]{2,1,0:T(8,128)(2,1)S(1)} %collective-permute-done.23), channel_id=1, source_target_pairs={{0,2},{2,0},{1,3},{3,1},{4,6},{6,4},{5,7},{7,5},{8,10},{10,8},{9,1... | collective-permute-start | bytes 1493000 | tf_op jit(solution)/shard_map/ppermute | solution.py:72
  389.7 45.4 %collective-permute-start.26 = (bf16[3,144,576]{2,1,0:T(8,128)(2,1)S(1)}, bf16[3,144,576]{2,1,0:T(8,128)(2,1)S(1)}, u32[]{:S(2)}, u32[]{:S(2)}) collective-permute-start(bf16[3,144,576]{2,1,0:T(8,128)(2,1)S(1)} %collective-permute-done.25), channel_id=1, source_target_pairs={{0,2},{2,0},{1,3},{3,1},{4,6},{6,4},{5,7},{7,5},{8,10},{10,8},{9,1... | collective-permute-start | bytes 1493000 | tf_op jit(solution)/shard_map/ppermute | solution.py:72
  503.1 34.7 %collective-permute-start.31 = (bf16[112,2304]{1,0:T(8,128)(2,1)S(1)}, bf16[112,2304]{1,0:T(8,128)(2,1)S(1)}, u32[]{:S(2)}, u32[]{:S(2)}) collective-permute-start(bf16[112,2304]{1,0:T(8,128)(2,1)S(1)} %get-tuple-element.82), channel_id=1, source_target_pairs={{0,4},{4,0},{8,12},{12,8},{16,20},{20,16},{24,28},{28,24},{1,5},{5... | collective-permute-start | bytes 1548296 | tf_op jit(solution)/shard_map/ppermute | solution.py:76
  572.0 35.4 %collective-permute-start.39 = (bf16[112,2304]{1,0:T(8,128)(2,1)S(1)}, bf16[112,2304]{1,0:T(8,128)(2,1)S(1)}, u32[]{:S(2)}, u32[]{:S(2)}) collective-permute-start(bf16[112,2304]{1,0:T(8,128)(2,1)S(1)} %get-tuple-element.37), channel_id=1, source_target_pairs={{0,4},{4,0},{8,12},{12,8},{16,20},{20,16},{24,28},{28,24},{1,5},{5... | collective-permute-start | bytes 1548296 | tf_op jit(solution)/shard_map/ppermute | solution.py:76
  707.5 34.7 %collective-permute-start.48 = (bf16[112,2304]{1,0:T(8,128)(2,1)S(1)}, bf16[112,2304]{1,0:T(8,128)(2,1)S(1)}, u32[]{:S(2)}, u32[]{:S(2)}) collective-permute-start(bf16[112,2304]{1,0:T(8,128)(2,1)S(1)} %get-tuple-element.78), channel_id=1, source_target_pairs={{0,4},{4,0},{8,12},{12,8},{16,20},{20,16},{24,28},{28,24},{1,5},{5... | collective-permute-start | bytes 1548296 | tf_op jit(solution)/shard_map/ppermute | solution.py:76
  827.7 35.2 %collective-permute-start.59 = (bf16[8,144,576]{2,1,0:T(8,128)(2,1)S(1)}, bf16[8,144,576]{2,1,0:T(8,128)(2,1)}, u32[]{:S(2)}, u32[]{:S(2)}) collective-permute-start(bf16[8,144,576]{2,1,0:T(8,128)(2,1)S(1)} %fusion.24), channel_id=1, source_target_pairs={{0,2},{2,0},{1,3},{3,1},{4,6},{6,4},{5,7},{7,5},{8,10},{10,8},{9,1... | collective-permute-start | bytes 3981320 | tf_op jit(solution)/shard_map/ppermute | solution.py:72
  841.1 53.4 %collective-permute-start.60 = (bf16[8,144,576]{2,1,0:T(8,128)(2,1)}, bf16[8,144,576]{2,1,0:T(8,128)(2,1)}, u32[]{:S(2)}, u32[]{:S(2)}) collective-permute-start(bf16[8,144,576]{2,1,0:T(8,128)(2,1)} %fusion.25), channel_id=1, source_target_pairs={{0,2},{2,0},{1,3},{3,1},{4,6},{6,4},{5,7},{7,5},{8,10},{10,8},{9,1... | collective-permute-start | bytes 3981320 | tf_op jit(solution)/shard_map/ppermute | solution.py:72
  852.2 73.1 %collective-permute-start.61 = (bf16[8,144,576]{2,1,0:T(8,128)(2,1)}, bf16[8,144,576]{2,1,0:T(8,128)(2,1)}, u32[]{:S(2)}, u32[]{:S(2)}) collective-permute-start(bf16[8,144,576]{2,1,0:T(8,128)(2,1)} %fusion.26), channel_id=1, source_target_pairs={{0,2},{2,0},{1,3},{3,1},{4,6},{6,4},{5,7},{7,5},{8,10},{10,8},{9,1... | collective-permute-start | bytes 3981320 | tf_op jit(solution)/shard_map/ppermute | solution.py:72
  858.0 72.8 %collective-permute-start.54 = (f32[224,2304]{1,0:T(8,128)}, f32[224,2304]{1,0:T(8,128)}, u32[]{:S(2)}, u32[]{:S(2)}) collective-permute-start(f32[224,2304]{1,0:T(8,128)} %pad_maximum_fusion.4), channel_id=1, source_target_pairs={{0,1},{1,0},{2,3},{3,2},{4,5},{5,4},{6,7},{7,6},{8,9},{9,8},{10,11... | collective-permute-start | bytes 6193160 | tf_op jit(solution)/shard_map/ppermute | solution.py:72
  858.7 74.2 %collective-permute-start.35 = (bf16[112,2304]{1,0:T(8,128)(2,1)}, bf16[112,2304]{1,0:T(8,128)(2,1)S(1)}, u32[]{:S(2)}, u32[]{:S(2)}) collective-permute-start(bf16[112,2304]{1,0:T(8,128)(2,1)} %get-tuple-element.92), channel_id=1, source_target_pairs={{0,1},{1,0},{2,3},{3,2},{4,5},{5,4},{6,7},{7,6},{8,9},{9,8},{10,11... | collective-permute-start | bytes 1548296 | tf_op jit(solution)/shard_map/ppermute | solution.py:72
  935.5 41.3 %collective-permute-start.63 = (bf16[3,144,576]{2,1,0:T(8,128)(2,1)S(1)}, bf16[3,144,576]{2,1,0:T(8,128)(2,1)S(1)}, u32[]{:S(2)}, u32[]{:S(2)}) collective-permute-start(bf16[3,144,576]{2,1,0:T(8,128)(2,1)S(1)} %get-tuple-element.71), channel_id=1, source_target_pairs={{0,8},{4,12},{8,0},{12,4},{16,24},{20,28},{24,16},{28,20},{1,9},{5... | collective-permute-start | bytes 1493000 | tf_op jit(solution)/shard_map/ppermute | solution.py:76
  937.4 52.0 %collective-permute-start.64 = (bf16[3,144,576]{2,1,0:T(8,128)(2,1)S(1)}, bf16[3,144,576]{2,1,0:T(8,128)(2,1)S(1)}, u32[]{:S(2)}, u32[]{:S(2)}) collective-permute-start(bf16[3,144,576]{2,1,0:T(8,128)(2,1)S(1)} %get-tuple-element.70), channel_id=1, source_target_pairs={{0,12},{4,8},{8,4},{12,0},{16,28},{20,24},{24,20},{28,16},{1,13},{... | collective-permute-start | bytes 1493000 | tf_op jit(solution)/shard_map/ppermute | solution.py:76
  938.1 53.5 %collective-permute-start.65 = (bf16[3,144,576]{2,1,0:T(8,128)(2,1)S(1)}, bf16[3,144,576]{2,1,0:T(8,128)(2,1)S(1)}, u32[]{:S(2)}, u32[]{:S(2)}) collective-permute-start(bf16[3,144,576]{2,1,0:T(8,128)(2,1)S(1)} %get-tuple-element.69), channel_id=1, source_target_pairs={{0,16},{4,20},{8,24},{12,28},{16,0},{20,4},{24,8},{28,12},{1,17},{... | collective-permute-start | bytes 1493000 | tf_op jit(solution)/shard_map/ppermute | solution.py:76
  943.3 49.5 %collective-permute-start.66 = (bf16[3,144,576]{2,1,0:T(8,128)(2,1)S(1)}, bf16[3,144,576]{2,1,0:T(8,128)(2,1)S(1)}, u32[]{:S(2)}, u32[]{:S(2)}) collective-permute-start(bf16[3,144,576]{2,1,0:T(8,128)(2,1)S(1)} %get-tuple-element.68), channel_id=1, source_target_pairs={{0,20},{4,16},{8,28},{12,24},{16,4},{20,0},{24,12},{28,8},{1,21},{... | collective-permute-start | bytes 1493000 | tf_op jit(solution)/shard_map/ppermute | solution.py:76
  956.1 47.1 %collective-permute-start.67 = (bf16[3,144,576]{2,1,0:T(8,128)(2,1)S(1)}, bf16[3,144,576]{2,1,0:T(8,128)(2,1)S(1)}, u32[]{:S(2)}, u32[]{:S(2)}) collective-permute-start(bf16[3,144,576]{2,1,0:T(8,128)(2,1)S(1)} %get-tuple-element.67), channel_id=1, source_target_pairs={{0,24},{4,28},{8,16},{12,20},{16,8},{20,12},{24,0},{28,4},{1,25},{... | collective-permute-start | bytes 1493000 | tf_op jit(solution)/shard_map/ppermute | solution.py:76
  992.8 138.5 %collective-permute-start.57 = (bf16[224,2304]{1,0:T(8,128)(2,1)}, bf16[224,2304]{1,0:T(8,128)(2,1)}, u32[]{:S(2)}, u32[]{:S(2)}) collective-permute-start(bf16[224,2304]{1,0:T(8,128)(2,1)} %pad_maximum_fusion.7), channel_id=1, source_target_pairs={{0,1},{1,0},{2,3},{3,2},{4,5},{5,4},{6,7},{7,6},{8,9},{9,8},{10,11... | collective-permute-start | bytes 3096584 | tf_op jit(solution)/shard_map/ppermute | solution.py:72
  (131 other events, 2197.7 us)
Sparse Core Ops, SparseCore 0:
  10.9 82.8 all-gather.3
  96.5 50.0 all-gather.5
  815.2 151.4 reduce-scatter.3

commit v2 on v1

--- a/solution.py
+++ b/solution.py
@@ -1,4 +1,5 @@
 import functools
+import math
 
 import jax
 import jax.numpy as jnp
@@ -76,29 +77,49 @@
     return lax.ppermute(piece, "fsdp", [(d, d ^ step) for d in range(n)])
 
 
-def gather_rows(own, n):
+def gather_rows(own, n, checks=()):
     have = [own]
     bit = n // 2
-    while bit:
-        have = have + [hop(piece, bit, n) for piece in have]
+    while bit > 1:
+        new = [hop(piece, bit, n) for piece in have]
+        if bit == n // 2 and checks:
+            new = [after(piece, *checks) for piece in new]
+        have = have + new
         bit //= 2
-    mine = jnp.concatenate(have)
-    return jnp.concatenate([mine, swap(mine, "tp")])
-
-
-def scatter_rows(part, n):
-    rows = part.shape[0] // (2 * n)
-    most = n * rows
-    both = part[:most] + swap(part[most:].astype(b16), "tp").astype(f32)
-    blocks = [both[k * rows : (k + 1) * rows] for k in range(n)]
-    bit = 1
+    even = jnp.concatenate(have)
+    odd = jnp.concatenate([hop(piece, 1, n) for piece in have])
+    rows = jnp.concatenate([even, odd, swap(even, "tp"), swap(odd, "tp")])
+    return rows, have[-1]
+
+
+def after(value, *others):
+    return lax.optimization_barrier((value, *others))[0]
+
+
+def scatter_blocks(blocks, bit, n):
+    marks = []
     while bit < n:
         keep = len(blocks) // 2
+        marks.append(blocks[-1])
         blocks = [
             blocks[k] + hop(blocks[keep + k].astype(b16), bit, n).astype(f32) for k in range(keep)
         ]
         bit *= 2
-    return blocks[0]
+    return blocks[0], marks
+
+
+def scatter_rows(product, sources, n):
+    most = sources[0].shape[0] // 2
+    half = most // 2
+    rows = most // n
+    ends = [(0, half), (half, most), (most, most + half), (most + half, 2 * most)]
+    take = lambda k: product(*[source[ends[k][0] : ends[k][1]] for source in sources])
+    far = [swap(take(k).astype(b16), "tp") for k in (3, 2)]
+    odd = take(1) + far[0].astype(f32)
+    even = take(0) + far[1].astype(f32)
+    blocks = [part[k * rows : (k + 1) * rows] for part in (even, odd) for k in range(n // 2)]
+    own, marks = scatter_blocks(blocks, 1, n)
+    return own, [odd] + marks[1:]
 
 
 def gather_group(own):
@@ -112,7 +133,20 @@
     rows = part.shape[0] // 4
     b0, b1, b2, b3 = [part[k * rows : (k + 1) * rows] for k in range(4)]
     got = swap(jnp.concatenate([b1, b3]), "tp")
-    return b0 + got[:rows] + swap(b2 + got[rows:], "ctx")
+    return b0 + got[:rows] + swap((b2 + got[rows:]).astype(b16), "ctx").astype(f32)
+
+
+def range_order(n):
+    order, bit = [0], n // 2
+    while bit:
+        order = order + [k ^ bit for k in order]
+        bit //= 2
+    return order
+
+
+def tile_window(units, n):
+    spans = [-(-(d + 1) * units // 128) - d * units // 128 for d in range(n)]
+    return 128 * max(spans)
 
 
 def natural(own, other, index, axis):
@@ -178,7 +212,10 @@
     slot_in = dot(pick, seq_group, ((1,), (0,)))
     resid_in = slot_in[:rows]
 
-    qkv_own = jnp.concatenate(
+    gain_row = jnp.concatenate([gain_attn_in, gain_attn_out, gain_ffn_in, gain_ffn_out])
+    heads_cols = q_cols + 2 * k_cols
+    gain_rows = -(-4 * d_rows // heads_cols)
+    heads_own = jnp.concatenate(
         [
             lax.dynamic_slice_in_dim(query_weight, ctx * q_cols, q_cols, 1),
             lax.dynamic_slice_in_dim(key_weight, ctx * k_cols, k_cols, 1),
@@ -186,34 +223,49 @@
         ],
         axis=1,
     )
-    qkv_weight = lax.all_gather(qkv_own, "fsdp", axis=0, tiled=True)
+    heads_own = jnp.concatenate(
+        [heads_own, jnp.pad(gain_row, (0, 16 * heads_cols - 4 * d_rows)).reshape(16, heads_cols)]
+    )
+    have = [(0, heads_own)]
+    bit = n // 2
+    while bit:
+        have = have + [(k ^ bit, hop(piece, bit, n)) for k, piece in have]
+        bit //= 2
     out_own = lax.dynamic_slice_in_dim(output_weight, ctx * q_cols, q_cols, 0).T
     out_weight = lax.all_gather(out_own, "fsdp", axis=0, tiled=True)
-    gains = lax.all_gather(
-        jnp.concatenate([gain_attn_in, gain_attn_out, gain_ffn_in, gain_ffn_out])
-        .astype(f32)
-        .reshape(1, 4 * d_rows),
-        "fsdp",
-        axis=0,
-        tiled=True,
-    )
-    gains = gains.reshape(n, 4, d_rows).transpose(1, 0, 2).reshape(4, width)
-
-    ffn_own = jnp.stack([gate_weight, up_weight, down_weight.T])
-    ffn_own = ffn_own.reshape(3, 2, d_half, n, ff_own).transpose(3, 1, 0, 2, 4)
-    ffn_own = lax.dynamic_index_in_dim(ffn_own, ctx, 1, keepdims=False)
-    ffn_full = [jnp.zeros((n, 2, d_half, ff_own), b16) for _ in range(3)]
-    for k in range(n):
-        piece = lax.dynamic_index_in_dim(ffn_own, me ^ k, 0, keepdims=False)
-        if k:
-            piece = hop(piece, k, n)
-        second = swap(piece, "ctx")
-        for which in range(3):
-            for half, side in ((piece, ctx), (second, 1 - ctx)):
-                ffn_full[which] = lax.dynamic_update_slice(
-                    ffn_full[which], half[which][None, None], (me ^ k, side, 0, 0)
-                )
-    gate_full, up_full, down_full = [full.reshape(width, ff_own) for full in ffn_full]
+    qkv_weight = jnp.zeros((n, d_rows, heads_cols), b16)
+    gains = jnp.zeros((n, gain_rows, heads_cols), b16)
+    for k, piece in have:
+        put = lambda whole, part: lax.dynamic_update_slice_in_dim(whole, part[None], me ^ k, 0)
+        qkv_weight = put(qkv_weight, piece[:d_rows])
+        gains = put(gains, piece[d_rows : d_rows + gain_rows])
+    qkv_weight = qkv_weight.reshape(width, heads_cols)
+    gains = gains.reshape(n, gain_rows * heads_cols)[:, : 4 * d_rows]
+    gains = gains.reshape(n, 4, d_rows).transpose(1, 0, 2).reshape(4, width).astype(f32)
+
+    window = tile_window(ff_own, n)
+    first = lambda device: (device * ff_own) & -128
+    unit = first(me) + jnp.arange(window, dtype=jnp.int32)
+    valid = ((unit >= me * ff_own) & (unit < (me + 1) * ff_own))[None]
+
+    def to_units(weights):
+        halves = [lax.dynamic_slice_in_dim(weight, ctx * d_half, d_half) for weight in weights]
+        own = jnp.stack(
+            [
+                jnp.concatenate([half[:, first(d) : first(d) + window] for half in halves], axis=1)
+                for d in range(n)
+            ]
+        )
+        return lax.all_to_all(own, "fsdp", 0, 0, tiled=True)
+
+    def both_halves(half, other):
+        whole = jnp.zeros((n, 2, *half.shape[1:]), b16)
+        whole = lax.dynamic_update_slice_in_dim(whole, half[:, None], ctx, 1)
+        whole = lax.dynamic_update_slice_in_dim(whole, other[:, None], 1 - ctx, 1)
+        return whole.reshape(width, half.shape[2])
+
+    far_piece = have[n // 2 - 1][1]
+    gu_half = to_units([after(weight, far_piece) for weight in (gate_weight, up_weight)])
 
     normed_attn = rms_scale(slot_in, gains[0]).astype(b16)
     qkv = dot(normed_attn, qkv_weight, ((1,), (0,)))
@@ -239,53 +291,78 @@
     attn_out = scatter_group(dot(attended, out_weight, ((1,), (1,))))
     middle = resid_in + rms_scale(attn_out, gains[1])
 
-    normed_ffn = gather_rows(rms_scale(middle, gains[2]).astype(b16), n)
-    gate_act = dot(normed_ffn, gate_full, ((1,), (0,)))
-    up_act = dot(normed_ffn, up_full, ((1,), (0,)))
-    hidden = glu_apply(gate_act, up_act).astype(b16)
-    ffn_out = scatter_rows(dot(hidden, down_full, ((1,), (1,))), n)
+    normed_own = rms_scale(middle, gains[2]).astype(b16)
+    gu_other = swap(after(gu_half, attn_out), "ctx")
+    normed_ffn, mark = gather_rows(normed_own, n)
+    down_half = to_units([after(down_weight.T, mark)])
+    down_other = swap(after(down_half, gu_other), "ctx")
+    gu_full = both_halves(gu_half, gu_other)
+    down_full = both_halves(down_half, down_other)
+    gate_and_up = dot(normed_ffn, gu_full, ((1,), (0,)))
+    gate_act, up_act = gate_and_up[:, :window], gate_and_up[:, window:]
+    hidden = jnp.where(valid, glu_apply(gate_act, up_act), 0.0).astype(b16)
+    ffn_out, _ = scatter_rows(lambda part: dot(part, down_full, ((1,), (1,))), [hidden], n)
     block_own = (middle + rms_scale(ffn_out, gains[3])).astype(b16)
     block_out = natural(block_own, swap(block_own, "tp"), tp, 0)
 
     d_out = lax.dynamic_slice_in_dim(cotangent, tp * rows, rows).astype(f32)
     d_ffn_raw, gain_four_term = norm_back(ffn_out, gains[3], d_out)
-    d_ffn_out = gather_rows(d_ffn_raw.astype(b16), n)
+    d_ffn_out, _ = gather_rows(d_ffn_raw.astype(b16), n)
     d_hidden = dot(d_ffn_out, down_full, ((1,), (0,)))
-    d_gate_raw, d_up_raw = jax.vjp(glu_apply, gate_act, up_act)[1](d_hidden)
-    d_gate = d_gate_raw.astype(b16)
-    d_up = d_up_raw.astype(b16)
-    d_normed_ffn = scatter_rows(
-        dot(d_gate, gate_full, ((1,), (1,))) + dot(d_up, up_full, ((1,), (1,))), n
-    )
-    ffn_terms = [
-        dot(normed_ffn, d_gate, ((0,), (0,))),
-        dot(normed_ffn, d_up, ((0,), (0,))),
-        dot(d_ffn_out, hidden, ((0,), (0,))),
-    ]
-    ffn_terms = [term.reshape(n, 2, d_half, ff_own) for term in ffn_terms]
-    ffn_keep = [lax.dynamic_index_in_dim(term, ctx, 1, keepdims=False) for term in ffn_terms]
-    ffn_send = [
-        lax.dynamic_index_in_dim(term, 1 - ctx, 1, keepdims=False).astype(b16)
-        for term in ffn_terms
-    ]
-    ffn_sum = [keep + swap(send, "ctx").astype(f32) for keep, send in zip(ffn_keep, ffn_send)]
-    ffn_low = jnp.stack([term.astype(b16) for term in ffn_sum], axis=1)
-    ffn_grads = ffn_sum
-    for k in range(1, n):
-        piece = hop(lax.dynamic_index_in_dim(ffn_low, me ^ k, 0, keepdims=False), k, n)
-        ffn_grads = [
-            lax.dynamic_update_index_in_dim(grad, piece[which].astype(f32), me ^ k, 0)
-            for which, grad in enumerate(ffn_grads)
+    d_pair = jax.vjp(glu_apply, gate_act, up_act)[1](d_hidden)
+    d_gate, d_up = [jnp.where(valid, part, 0.0).astype(b16) for part in d_pair]
+    d_normed_ffn, marks = scatter_rows(
+        lambda part: dot(part, gu_full, ((1,), (1,))),
+        [jnp.concatenate([d_gate, d_up], axis=1)],
+        n,
+    )
+
+    def halves(terms):
+        terms = terms.reshape(n, 2, d_half, window)
+        send = lax.dynamic_index_in_dim(terms, 1 - ctx, 1, keepdims=False).astype(b16)
+        return send, lax.dynamic_index_in_dim(terms, ctx, 1, keepdims=False)
+
+    down_send, down_keep = halves(dot(after(d_ffn_out, marks[0]), hidden, ((0,), (0,))))
+    late_normed = after(normed_ffn, marks[-1], down_send)
+    gate_send, gate_keep = halves(dot(late_normed, d_gate, ((0,), (0,))))
+    up_send, up_keep = halves(dot(after(late_normed, gate_send), d_up, ((0,), (0,))))
+    down_got, gate_got = swap(down_send, "ctx"), swap(gate_send, "ctx")
+
+    def to_owners(keeps, gots, gate):
+        gots = [after(got, gate) for got in gots]
+        low = [(keep + got.astype(f32)).astype(b16) for keep, got in zip(keeps, gots)]
+        return lax.all_to_all(jnp.concatenate(low, axis=2), "fsdp", 0, 0, tiled=True)
+
+    def columns_joined(whole):
+        period = 128 // math.gcd(ff_own, 128)
+        tiles = period * ff_own // 128
+        parts = whole.reshape(n // period, period, *whole.shape[1:]).astype(f32)
+        runs = []
+        for tile in range(tiles):
+            holds = [
+                d
+                for d in range(period)
+                if d * ff_own < (tile + 1) * 128 and (d + 1) * ff_own > tile * 128
+            ]
+            if runs and runs[-1][0] == holds and len(holds) == 1:
+                runs[-1][2] = tile + 1
+            else:
+                runs.append([holds, tile, tile + 1])
+        pieces = [
+            sum(parts[:, d, ..., a * 128 - first(d) : b * 128 - first(d)] for d in holds)
+            for holds, a, b in runs
         ]
-    gate_weight_grad = ffn_grads[0].transpose(1, 0, 2).reshape(d_half, ff_local)
-    up_weight_grad = ffn_grads[1].transpose(1, 0, 2).reshape(d_half, ff_local)
-    down_weight_grad = ffn_grads[2].transpose(0, 2, 1).reshape(ff_local, d_half)
-
+        joined = jnp.concatenate(pieces, axis=-1)
+        return joined.transpose(1, 0, 2).reshape(whole.shape[1], ff_local)
+
+    d_normed_ffn = after(d_normed_ffn, down_got, gate_send, up_send)
     d_middle_part, gain_three_term = norm_back(middle, gains[2], d_normed_ffn)
     d_middle = d_out + d_middle_part
     d_attn_raw, gain_two_term = norm_back(attn_out, gains[1], d_middle)
     d_attn_out = gather_group(d_attn_raw.astype(b16))
+    up_got = swap(after(up_send, d_attn_out), "ctx")
     d_attended = dot(d_attn_out, out_weight, ((1,), (0,))).astype(b16)
+    dg_rows = to_owners([down_keep, gate_keep], [down_got, gate_got], d_attended)
     d_att = d_attended.reshape(all_rows, kv_local, group_size, head_size)
     d_probs = jnp.einsum("qkgd,skd->kgqs", d_att, values, preferred_element_type=f32)
     d_soft = probs * (d_probs - jnp.sum(probs * d_probs, axis=-1, keepdims=True))
@@ -301,25 +378,41 @@
     d_key_lin = rotate(d_keys, -angles).reshape(all_rows, k_cols).astype(b16)
     d_value = d_values.reshape(all_rows, k_cols).astype(b16)
     d_qkv = jnp.concatenate([d_query_lin, d_key_lin, d_value], axis=1)
-    d_normed_attn = scatter_group(dot(d_qkv, qkv_weight, ((1,), (1,))))
+    d_normed_part = dot(d_qkv, qkv_weight, ((1,), (1,)))
+    d_normed_attn = scatter_group(d_normed_part)
     resid_part, gain_one_term = norm_back(resid_in, gains[0], d_normed_attn)
     slot_grad = gather_group((d_middle + resid_part).astype(b16))
-    place = (
+    unpick = (
         (ctx * tok_rows + jnp.arange(tok_rows, dtype=jnp.int32))[:, None] == packed[None, :]
     ).astype(b16)
-    tokens_grad = dot(place, slot_grad, ((1,), (0,))).astype(b16)
-
-    attn_terms = jnp.concatenate(
+    tokens_grad = dot(unpick, slot_grad, ((1,), (0,))).astype(b16)
+
+    attn_terms = [
+        dot(normed_attn, d_qkv, ((0,), (0,))).reshape(n, d_rows, -1),
+        dot(d_attn_out, attended, ((0,), (0,))).reshape(n, d_rows, -1),
+    ]
+    attn_rows, marks = scatter_blocks(
         [
-            dot(normed_attn, d_qkv, ((0,), (0,))),
-            dot(d_attn_out, attended, ((0,), (0,))),
+            jnp.concatenate(
+                [lax.dynamic_index_in_dim(terms, me ^ k, 0, keepdims=False) for terms in attn_terms],
+                axis=1,
+            )
+            for k in range_order(n)
         ],
-        axis=1,
-    ).astype(b16)
-    attn_rows = lax.psum_scatter(attn_terms, "fsdp", scatter_dimension=0, tiled=True)
+        1,
+        n,
+    )
+    dg_rows = after(dg_rows, marks[1])
+    down_rows, gate_rows = dg_rows[..., :window], dg_rows[..., window:]
+    up_rows = to_owners([up_keep], [up_got], dg_rows)
+    gate_weight_grad = columns_joined(gate_rows)
+    up_weight_grad = columns_joined(up_rows)
+    down_weight_grad = columns_joined(down_rows).T
     attn_rows = attn_rows.reshape(2, d_half, -1)
     attn_own = lax.dynamic_index_in_dim(attn_rows, ctx, 0, keepdims=False)
-    attn_other = swap(lax.dynamic_index_in_dim(attn_rows, 1 - ctx, 0, keepdims=False), "ctx")
+    attn_other = swap(
+        lax.dynamic_index_in_dim(attn_rows, 1 - ctx, 0, keepdims=False).astype(b16), "ctx"
+    )
     edges = [0, q_cols, q_cols + k_cols, q_cols + 2 * k_cols, 2 * q_cols + 2 * k_cols]
     attn_grads = [
         natural(attn_own[:, a:b].astype(f32), attn_other[:, a:b].astype(f32), ctx, 1)
@@ -327,10 +420,21 @@
     ]
 
     gain_terms = jnp.stack([gain_one_term, gain_two_term, gain_three_term, gain_four_term])
-    gain_terms = gain_terms.reshape(4, 2 * n, d_half).transpose(1, 0, 2).reshape(2 * n, 4 * d_half)
     gain_terms = gain_terms + swap(gain_terms, "tp")
-    gain_rows = lax.psum_scatter(gain_terms, ("fsdp", "ctx"), scatter_dimension=0, tiled=True)
-    gain_rows = gain_rows.reshape(4, d_half)
+    gain_terms = gain_terms.reshape(4, n, 2, d_half).transpose(1, 2, 0, 3)
+    gain_terms = lax.dynamic_index_in_dim(gain_terms, ctx, 1, keepdims=False) + swap(
+        lax.dynamic_index_in_dim(gain_terms, 1 - ctx, 1, keepdims=False), "ctx"
+    )
+    gain_rows = jnp.stack(
+        [lax.dynamic_index_in_dim(gain_terms, me ^ k, 0, keepdims=False) for k in range_order(n)]
+    )
+    gain_rows = after(gain_rows, up_rows)
+    bit = 1
+    while bit < n:
+        keep = gain_rows.shape[0] // 2
+        gain_rows = gain_rows[:keep] + hop(gain_rows[keep:], bit, n)
+        bit *= 2
+    gain_rows = gain_rows[0]
     return (
         block_out,
         tokens_grad,

time: 1160 us -> 860 us (0.74)
  waiting for transfers between devices: 571 us -> 424 us
  blocking collectives: 122 us -> 0 us
  local copies, waits for them, and re-layouts: 158 us -> 111 us
  starting transfers between devices: 71.3 us -> 113 us
  other arithmetic: 80.2 us -> 64.4 us
    ppermute x28 -> x27, waiting for transfers between devices: 155 us -> 59.4 us  [swap(): return lax.ppermute(piece, axis, [(0, 1), (1, 0)])]
    unnamed x1 -> x0, blocking collectives: 90.6 us -> none
    all_gather x1 -> x0, waiting for transfers between devices: 40 us -> none  [local(): qkv_weight = lax.all_gather(qkv_own, 'fsdp', axis=0, tiled=True)]
    all_gather x1, waiting for transfers between devices: 37.8 us -> 0.02 us  [local(): out_weight = lax.all_gather(out_own, 'fsdp', axis=0, tiled=True)]
    all_gather x1 -> x0, blocking collectives: 31.4 us -> none  [local(): lax.all_gather(jnp.concatenate([gain_attn_in, gain_attn_out, gain_ffn_in,...]
    all_to_all x0 -> x4, starting transfers between devices: none -> 30.8 us  [the longest x2 20.8 us: to_units(): return lax.all_to_all(own, 'fsdp', 0, 0, tiled=True)]
    another operation x12 -> x3, local copies, waits for them, and re-layouts: 31.5 us -> 3.06 us  [the longest x1 1.39 us: local(): jnp.stack([lax.dynamic_index_in_dim(gain_terms, me ^ k, 0, keepdims=False...]
    another operation x9 -> x5, other arithmetic: 31.2 us -> 2.91 us
  transfers between devices with their start and end apart: 73 -> 77, of which waited for: 48 -> 40; matrix products, arithmetic and copies ran while one was open for 16% -> 30% of each run, Pallas kernels for 0% -> 0%
where the time goes in v2:
time: 860 us; the launch traced here: 859 us
  waiting for transfers between devices  424 us (49%)
  matrix products  129 us (15%)
  starting transfers between devices  113 us (13%)
  local copies, waits for them, and re-layouts  111 us (13%)
  other arithmetic  64.4 us (7%)
  between operations  16.7 us (2%)
    ppermute x45, waiting for transfers between devices, hop(): return lax.ppermute(piece, 'fsdp', [(d, d ^ step) for d in range(n)])  344 us
    dot_general x21, matrix products, dot(): lax.dot_general(lhs, rhs, (dims, ((), ())), preferred_element_type=f32)  123 us
    ppermute x27, waiting for transfers between devices, swap(): return lax.ppermute(piece, axis, [(0, 1), (1, 0)])  59.4 us
    ppermute x45, starting transfers between devices, hop(): return lax.ppermute(piece, 'fsdp', [(d, d ^ step) for d in range(n)])  54.5 us
    unnamed x203, local copies, waits for them, and re-layouts  45.5 us
    ppermute x27, starting transfers between devices, swap(): return lax.ppermute(piece, axis, [(0, 1), (1, 0)])  28 us
    all_to_all x2, starting transfers between devices, to_units(): return lax.all_to_all(own, 'fsdp', 0, 0, tiled=True)  20.8 us
    all_to_all x2, waiting for transfers between devices, to_owners(): lax.all_to_all(jnp.concatenate(low, axis=2), 'fsdp', 0, 0, tiled=True)  20.6 us
  transfers between devices with their start and end apart: 77, of which 40 were waited for; matrix products, arithmetic and copies ran while one was open for 30% of the time, Pallas kernels for 0%

profile of v2, /device:TPU:0, one launch (start us, length us, event | category | flops | bytes accessed | tf_op | source)
XLA Modules:
  0.0 859.3 jit_solution(17739152647933604349)
XLA Ops:
  34.2 20.9 %collective-permute-done.2 = bf16[304,1024]{1,0:T(8,128)(2,1)} collective-permute-done((bf16[304,1024]{1,0:T(8,128)(2,1)S(1)}, bf16[304,1024]{1,0:T(8,128)(2,1)}, u32[]{:S(2)}, u32[]{:S(2)}) %collective-permute-start.2) | collective-permute-done | bytes 622624 | tf_op jit(solution)/shard_map/ppermute | solution.py:77
  65.8 14.0 %collective-permute-done.4 = bf16[304,1024]{1,0:T(8,128)(2,1)S(1)} collective-permute-done((bf16[304,1024]{1,0:T(8,128)(2,1)}, bf16[304,1024]{1,0:T(8,128)(2,1)S(1)}, u32[]{:S(2)}, u32[]{:S(2)}) %collective-permute-start.4) | collective-permute-done | bytes 622624 | tf_op jit(solution)/shard_map/ppermute | solution.py:77
  106.8 28.8 %collective-permute-done.8 = bf16[304,1024]{1,0:T(8,128)(2,1)S(1)} collective-permute-done((bf16[304,1024]{1,0:T(8,128)(2,1)}, bf16[304,1024]{1,0:T(8,128)(2,1)S(1)}, u32[]{:S(2)}, u32[]{:S(2)}) %collective-permute-start.8) | collective-permute-done | bytes 622624 | tf_op jit(solution)/shard_map/ppermute | solution.py:77
  164.2 12.2 %collective-permute-done.10 = bf16[112,2304]{1,0:T(8,128)(2,1)S(1)} collective-permute-done((bf16[112,2304]{1,0:T(8,128)(2,1)S(1)}, bf16[112,2304]{1,0:T(8,128)(2,1)S(1)}, u32[]{:S(2)}, u32[]{:S(2)}) %collective-permute-start.10) | collective-permute-done | bytes 516128 | tf_op jit(solution)/shard_map/ppermute | solution.py:73
  195.6 14.2 %collective-permute-done.11 = bf16[112,2304]{1,0:T(8,128)(2,1)} collective-permute-done((bf16[112,2304]{1,0:T(8,128)(2,1)S(1)}, bf16[112,2304]{1,0:T(8,128)(2,1)}, u32[]{:S(2)}, u32[]{:S(2)}) %collective-permute-start.11) | collective-permute-done | bytes 516128 | tf_op jit(solution)/shard_map/ppermute | solution.py:77
  227.3 16.0 %all-to-all-start.1 = ((bf16[8,144,640]{2,1,0:T(8,128)(2,1)}), bf16[8,144,640]{2,1,0:T(8,128)(2,1)}, u32[]{:S(2)}, u32[]{:S(2)}) async-start(bf16[8,144,640]{2,1,0:T(8,128)(2,1)} %fusion.143), calls=%async_computation.1 | async-start | bytes 2949120 | tf_op jit(solution)/shard_map/all_to_all | solution.py:259
  250.2 19.0 %collective-permute-done.17 = bf16[112,2304]{1,0:T(8,128)(2,1)S(1)} collective-permute-done((bf16[112,2304]{1,0:T(8,128)(2,1)}, bf16[112,2304]{1,0:T(8,128)(2,1)S(1)}, u32[]{:S(2)}, u32[]{:S(2)}) %collective-permute-start.17) | collective-permute-done | bytes 516128 | tf_op jit(solution)/shard_map/ppermute | solution.py:77
  283.4 15.0 %fusion.217 = f32[1792,1280]{1,0:T(8,128)S(1)} fusion(bf16[1792,2304]{1,0:T(8,128)(2,1)} %constant_dynamic-update-slice_fusion, bf16[2304,1280]{1,0:T(8,128)(2,1)} %bitcast.44), kind=kOutput, calls=%fused_computation.474 | convolution fusion | flops 10569646080 | bytes 23330816 | tf_op jit(solution)/shard_map/dot_general | solution.py:69
  304.5 12.3 %collective-permute-done.21 = bf16[8,144,640]{2,1,0:T(8,128)(2,1)S(1)} collective-permute-done((bf16[8,144,640]{2,1,0:T(8,128)(2,1)}, bf16[8,144,640]{2,1,0:T(8,128)(2,1)S(1)}, u32[]{:S(2)}, u32[]{:S(2)}) %collective-permute-start.21) | collective-permute-done | bytes 1474592 | tf_op jit(solution)/shard_map/ppermute | solution.py:73
  329.8 10.6 %collective-permute-done.28 = bf16[112,2304]{1,0:T(8,128)(2,1)S(1)} collective-permute-done((bf16[112,2304]{1,0:T(8,128)(2,1)S(1)}, bf16[112,2304]{1,0:T(8,128)(2,1)S(1)}, u32[]{:S(2)}, u32[]{:S(2)}) %collective-permute-start.28) | collective-permute-done | bytes 516128 | tf_op jit(solution)/shard_map/ppermute | solution.py:77
  340.5 11.1 %collective-permute-done.25 = bf16[112,2304]{1,0:T(8,128)(2,1)S(1)} collective-permute-done((bf16[112,2304]{1,0:T(8,128)(2,1)S(1)}, bf16[112,2304]{1,0:T(8,128)(2,1)S(1)}, u32[]{:S(2)}, u32[]{:S(2)}) %collective-permute-start.25) | collective-permute-done | bytes 516128 | tf_op jit(solution)/shard_map/ppermute | solution.py:77
  354.6 8.0 collective-permute-done.27
  362.6 10.1 %collective-permute-done.29 = bf16[112,2304]{1,0:T(8,128)(2,1)S(1)} collective-permute-done((bf16[112,2304]{1,0:T(8,128)(2,1)S(1)}, bf16[112,2304]{1,0:T(8,128)(2,1)S(1)}, u32[]{:S(2)}, u32[]{:S(2)}) %collective-permute-start.29) | collective-permute-done | bytes 516128 | tf_op jit(solution)/shard_map/ppermute | solution.py:77
  374.4 8.1 collective-permute-done.26
  382.5 11.3 %collective-permute-done.30 = bf16[112,2304]{1,0:T(8,128)(2,1)S(1)} collective-permute-done((bf16[112,2304]{1,0:T(8,128)(2,1)S(1)}, bf16[112,2304]{1,0:T(8,128)(2,1)S(1)}, u32[]{:S(2)}, u32[]{:S(2)}) %collective-permute-start.30) | collective-permute-done | bytes 516128 | tf_op jit(solution)/shard_map/ppermute | solution.py:77
  400.0 15.2 %collective-permute-done.32 = bf16[112,2304]{1,0:T(8,128)(2,1)S(1)} collective-permute-done((bf16[112,2304]{1,0:T(8,128)(2,1)S(1)}, bf16[112,2304]{1,0:T(8,128)(2,1)S(1)}, u32[]{:S(2)}, u32[]{:S(2)}) %collective-permute-start.32) | collective-permute-done | bytes 516128 | tf_op jit(solution)/shard_map/ppermute | solution.py:77
  418.8 7.9 collective-permute-done.34
  429.9 22.1 %collective-permute-done.37 = bf16[112,2304]{1,0:T(8,128)(2,1)S(1)} collective-permute-done((bf16[112,2304]{1,0:T(8,128)(2,1)S(1)}, bf16[112,2304]{1,0:T(8,128)(2,1)S(1)}, u32[]{:S(2)}, u32[]{:S(2)}) %collective-permute-start.37) | collective-permute-done | bytes 516128 | tf_op jit(solution)/shard_map/ppermute | solution.py:77
  452.0 7.6 collective-permute-done.38
  468.1 12.9 %select_convert_fusion = (bf16[1792,640]{1,0:T(8,128)(2,1)S(1)}, bf16[1792,640]{1,0:T(8,128)(2,1)S(1)}) fusion(pred[640]{0:T(1024)(128)(4,1)S(1)} %fusion.165, f32[1792,1280]{1,0:T(8,128)S(1)} %bitcast.436, bf16[1792,2304]{1,0:T(8,128)(2,1)} %constant_dynamic-update-slice_fusion.10, bf16[2304,640]{1,0:T(8,128)(2,1)S(1)} %bitcast.458), kind=kOutput, calls=%fused_computation.21 | convolution fusion | flops 5319229440 | bytes 24969856 | tf_op jit(solution)/shard_map/dot_general | solution.py:69
  481.0 8.2 convolution_convert_fusion
  511.2 16.2 %collective-permute-done.44 = bf16[112,2304]{1,0:T(8,128)(2,1)S(1)} collective-permute-done((bf16[112,2304]{1,0:T(8,128)(2,1)S(1)}, bf16[112,2304]{1,0:T(8,128)(2,1)S(1)}, u32[]{:S(2)}, u32[]{:S(2)}) %collective-permute-start.44) | collective-permute-done | bytes 516128 | tf_op jit(solution)/shard_map/ppermute | solution.py:77
  527.4 10.7 %collective-permute-done.47 = bf16[112,2304]{1,0:T(8,128)(2,1)S(1)} collective-permute-done((bf16[112,2304]{1,0:T(8,128)(2,1)S(1)}, bf16[112,2304]{1,0:T(8,128)(2,1)S(1)}, u32[]{:S(2)}, u32[]{:S(2)}) %collective-permute-start.47) | collective-permute-done | bytes 516128 | tf_op jit(solution)/shard_map/ppermute | solution.py:77
  539.5 9.3 %fusion.218 = f32[2304,640]{1,0:T(8,128)S(1)} fusion(bf16[1792,2304]{1,0:T(8,128)(2,1)} %constant_dynamic-update-slice_fusion.10, bf16[1792,640]{1,0:T(8,128)(2,1)S(1)} %copy-done.21), kind=kOutput, calls=%fused_computation.475 | convolution fusion | flops 5284823040 | bytes 16449536 | tf_op jit(solution)/shard_map/dot_general | solution.py:69
  556.7 9.3 %fusion.219 = f32[2304,640]{1,0:T(8,128)S(1)} fusion(bf16[1792,2304]{1,0:T(8,128)(2,1)} %constant_dynamic-update-slice_fusion, bf16[1792,640]{1,0:T(8,128)(2,1)S(1)} %copy-done.75), kind=kOutput, calls=%fused_computation.476 | convolution fusion | flops 5284823040 | bytes 16449536 | tf_op jit(solution)/shard_map/dot_general | solution.py:69
  567.3 10.5 %fusion.220 = f32[2304,640]{1,0:T(8,128)S(1)} fusion(bf16[1792,2304]{1,0:T(8,128)(2,1)} %constant_dynamic-update-slice_fusion, bf16[1792,640]{1,0:T(8,128)(2,1)S(1)} %copy-done.72), kind=kOutput, calls=%fused_computation.477 | convolution fusion | flops 5284823040 | bytes 16449536 | tf_op jit(solution)/shard_map/dot_general | solution.py:69
  587.9 9.0 %collective-permute-done.51 = bf16[112,2304]{1,0:T(8,128)(2,1)S(1)} collective-permute-done((bf16[112,2304]{1,0:T(8,128)(2,1)S(1)}, bf16[112,2304]{1,0:T(8,128)(2,1)S(1)}, u32[]{:S(2)}, u32[]{:S(2)}) %collective-permute-start.51) | collective-permute-done | bytes 516128 | tf_op jit(solution)/shard_map/ppermute | solution.py:73
  656.4 59.6 %collective-permute-done.61 = bf16[288,1536]{1,0:T(8,128)(2,1)S(1)} collective-permute-done((bf16[288,1536]{1,0:T(8,128)(2,1)S(1)}, bf16[288,1536]{1,0:T(8,128)(2,1)S(1)}, u32[]{:S(2)}, u32[]{:S(2)}) %collective-permute-start.61) | collective-permute-done | bytes 884768 | tf_op jit(solution)/shard_map/ppermute | solution.py:77
  719.8 15.1 %collective-permute-done.60 = bf16[288,1536]{1,0:T(8,128)(2,1)S(1)} collective-permute-done((bf16[288,1536]{1,0:T(8,128)(2,1)S(1)}, bf16[288,1536]{1,0:T(8,128)(2,1)S(1)}, u32[]{:S(2)}, u32[]{:S(2)}) %collective-permute-start.60) | collective-permute-done | bytes 884768 | tf_op jit(solution)/shard_map/ppermute | solution.py:77
  764.7 7.7 collective-permute-done.59
  780.1 7.1 collective-permute-start.64
  819.0 20.5 %all-to-all-done.3 = bf16[8,144,640]{2,1,0:T(8,128)(2,1)S(1)} async-done(((bf16[8,144,640]{2,1,0:T(8,128)(2,1)}), bf16[8,144,640]{2,1,0:T(8,128)(2,1)S(1)}, u32[]{:S(2)}, u32[]{:S(2)}) %all-to-all-start.3) | async-done | bytes 1474592 | tf_op jit(solution)/shard_map/all_to_all | solution.py:334
  (539 shorter events, 382.1 us)
Async XLA Ops:
  7.2 146.6 %all-gather.2.cloned.1.call-start = ((), (), s32[]{:S(2)}) async-start(), calls=%async_computation.4 | async-start | bytes 2654208 | tf_op jit(solution)/shard_map/all_gather | solution.py:235
  11.4 85.0 %collective-permute-start.5 = (bf16[304,1024]{1,0:T(8,128)(2,1)S(1)}, bf16[304,1024]{1,0:T(8,128)(2,1)S(1)}, u32[]{:S(2)}, u32[]{:S(2)}) collective-permute-start(bf16[304,1024]{1,0:T(8,128)(2,1)S(1)} %pad_maximum_fusion.21), channel_id=1, source_target_pairs={{0,4},{4,0},{8,12},{12,8},{16,20},{20,16},{24,28},{28,24},{1,5},{5... | collective-permute-start | bytes 1867784 | tf_op jit(solution)/shard_map/ppermute | solution.py:77
  14.4 41.5 %collective-permute-start.3 = (bf16[304,1024]{1,0:T(8,128)(2,1)S(1)}, bf16[304,1024]{1,0:T(8,128)(2,1)S(1)}, u32[]{:S(2)}, u32[]{:S(2)}) collective-permute-start(bf16[304,1024]{1,0:T(8,128)(2,1)S(1)} %pad_maximum_fusion.21), channel_id=1, source_target_pairs={{0,8},{4,12},{8,0},{12,4},{16,24},{20,28},{24,16},{28,20},{1,9},{5... | collective-permute-start | bytes 1867784 | tf_op jit(solution)/shard_map/ppermute | solution.py:77
  16.0 39.1 %collective-permute-start.2 = (bf16[304,1024]{1,0:T(8,128)(2,1)S(1)}, bf16[304,1024]{1,0:T(8,128)(2,1)}, u32[]{:S(2)}, u32[]{:S(2)}) collective-permute-start(bf16[304,1024]{1,0:T(8,128)(2,1)S(1)} %pad_maximum_fusion.21), channel_id=1, source_target_pairs={{0,16},{4,20},{8,24},{12,28},{16,0},{20,4},{24,8},{28,12},{1,17},{... | collective-permute-start | bytes 1867784 | tf_op jit(solution)/shard_map/ppermute | solution.py:77
  55.1 42.1 %collective-permute-start.6 = (bf16[304,1024]{1,0:T(8,128)(2,1)}, bf16[304,1024]{1,0:T(8,128)(2,1)}, u32[]{:S(2)}, u32[]{:S(2)}) collective-permute-start(bf16[304,1024]{1,0:T(8,128)(2,1)} %collective-permute-done.2), channel_id=1, source_target_pairs={{0,4},{4,0},{8,12},{12,8},{16,20},{20,16},{24,28},{28,24},{1,5},{5... | collective-permute-start | bytes 1867784 | tf_op jit(solution)/shard_map/ppermute | solution.py:77
  56.0 48.2 %collective-permute-start.7 = (bf16[304,1024]{1,0:T(8,128)(2,1)S(1)}, bf16[304,1024]{1,0:T(8,128)(2,1)}, u32[]{:S(2)}, u32[]{:S(2)}) collective-permute-start(bf16[304,1024]{1,0:T(8,128)(2,1)S(1)} %collective-permute-done.3), channel_id=1, source_target_pairs={{0,4},{4,0},{8,12},{12,8},{16,20},{20,16},{24,28},{28,24},{1,5},{5... | collective-permute-start | bytes 1867784 | tf_op jit(solution)/shard_map/ppermute | solution.py:77
  86.8 99.5 %all-to-all-start = ((bf16[8,144,1280]{2,1,0:T(8,128)(2,1)}), bf16[8,144,1280]{2,1,0:T(8,128)(2,1)}, u32[]{:S(2)}, u32[]{:S(2)}) async-start(bf16[8,144,1280]{2,1,0:T(8,128)(2,1)} %fusion.112), calls=%async_computation | async-start | bytes 5898240 | tf_op jit(solution)/shard_map/all_to_all | solution.py:259
  91.6 43.9 %collective-permute-start.8 = (bf16[304,1024]{1,0:T(8,128)(2,1)}, bf16[304,1024]{1,0:T(8,128)(2,1)S(1)}, u32[]{:S(2)}, u32[]{:S(2)}) collective-permute-start(bf16[304,1024]{1,0:T(8,128)(2,1)} %copy-done.39), channel_id=1, source_target_pairs={{0,4},{4,0},{8,12},{12,8},{16,20},{20,16},{24,28},{28,24},{1,5},{5... | collective-permute-start | bytes 1867784 | tf_op jit(solution)/shard_map/ppermute | solution.py:77
  193.0 55.3 %collective-permute-start.14 = (bf16[112,2304]{1,0:T(8,128)(2,1)S(1)}, bf16[112,2304]{1,0:T(8,128)(2,1)}, u32[]{:S(2)}, u32[]{:S(2)}) collective-permute-start(bf16[112,2304]{1,0:T(8,128)(2,1)S(1)} %get-tuple-element.62), channel_id=1, source_target_pairs={{0,4},{4,0},{8,12},{12,8},{16,20},{20,16},{24,28},{28,24},{1,5},{5... | collective-permute-start | bytes 1548296 | tf_op jit(solution)/shard_map/ppermute | solution.py:77
  194.1 81.3 %collective-permute-start.20 = (bf16[8,144,1280]{2,1,0:T(8,128)(2,1)}, bf16[8,144,1280]{2,1,0:T(8,128)(2,1)}, u32[]{:S(2)}, u32[]{:S(2)}) collective-permute-start(bf16[8,144,1280]{2,1,0:T(8,128)(2,1)} %all-to-all-done), channel_id=1, source_target_pairs={{0,2},{2,0},{1,3},{3,1},{4,6},{6,4},{5,7},{7,5},{8,10},{10,8},{9,1... | collective-permute-start | bytes 8847368 | tf_op jit(solution)/shard_map/ppermute | solution.py:73
  209.8 40.3 %collective-permute-start.15 = (bf16[112,2304]{1,0:T(8,128)(2,1)}, bf16[112,2304]{1,0:T(8,128)(2,1)}, u32[]{:S(2)}, u32[]{:S(2)}) collective-permute-start(bf16[112,2304]{1,0:T(8,128)(2,1)} %collective-permute-done.11), channel_id=1, source_target_pairs={{0,4},{4,0},{8,12},{12,8},{16,20},{20,16},{24,28},{28,24},{1,5},{5... | collective-permute-start | bytes 1548296 | tf_op jit(solution)/shard_map/ppermute | solution.py:77
  212.3 37.9 %collective-permute-start.16 = (bf16[112,2304]{1,0:T(8,128)(2,1)S(1)}, bf16[112,2304]{1,0:T(8,128)(2,1)}, u32[]{:S(2)}, u32[]{:S(2)}) collective-permute-start(bf16[112,2304]{1,0:T(8,128)(2,1)S(1)} %collective-permute-done.12), channel_id=1, source_target_pairs={{0,4},{4,0},{8,12},{12,8},{16,20},{20,16},{24,28},{28,24},{1,5},{5... | collective-permute-start | bytes 1548296 | tf_op jit(solution)/shard_map/ppermute | solution.py:77
  227.3 54.6 %all-to-all-start.1 = ((bf16[8,144,640]{2,1,0:T(8,128)(2,1)}), bf16[8,144,640]{2,1,0:T(8,128)(2,1)}, u32[]{:S(2)}, u32[]{:S(2)}) async-start(bf16[8,144,640]{2,1,0:T(8,128)(2,1)} %fusion.143), calls=%async_computation.1 | async-start | bytes 2949120 | tf_op jit(solution)/shard_map/all_to_all | solution.py:259
  281.9 34.9 %collective-permute-start.21 = (bf16[8,144,640]{2,1,0:T(8,128)(2,1)}, bf16[8,144,640]{2,1,0:T(8,128)(2,1)S(1)}, u32[]{:S(2)}, u32[]{:S(2)}) collective-permute-start(bf16[8,144,640]{2,1,0:T(8,128)(2,1)} %all-to-all-done.1), channel_id=1, source_target_pairs={{0,2},{2,0},{1,3},{3,1},{4,6},{6,4},{5,7},{7,5},{8,10},{10,8},{9,1... | collective-permute-start | bytes 4423688 | tf_op jit(solution)/shard_map/ppermute | solution.py:73
  327.9 34.7 %collective-permute-start.27 = (bf16[112,2304]{1,0:T(8,128)(2,1)S(1)}, bf16[112,2304]{1,0:T(8,128)(2,1)S(1)}, u32[]{:S(2)}, u32[]{:S(2)}) collective-permute-start(bf16[112,2304]{1,0:T(8,128)(2,1)S(1)} %get-tuple-element.122), channel_id=1, source_target_pairs={{0,4},{4,0},{8,12},{12,8},{16,20},{20,16},{24,28},{28,24},{1,5},{5... | collective-permute-start | bytes 1548296 | tf_op jit(solution)/shard_map/ppermute | solution.py:77
  415.9 36.1 %collective-permute-start.36 = (bf16[112,2304]{1,0:T(8,128)(2,1)S(1)}, bf16[112,2304]{1,0:T(8,128)(2,1)S(1)}, u32[]{:S(2)}, u32[]{:S(2)}) collective-permute-start(bf16[112,2304]{1,0:T(8,128)(2,1)S(1)} %collective-permute-done.32), channel_id=1, source_target_pairs={{0,4},{4,0},{8,12},{12,8},{16,20},{20,16},{24,28},{28,24},{1,5},{5... | collective-permute-start | bytes 1548296 | tf_op jit(solution)/shard_map/ppermute | solution.py:77
  417.3 34.8 %collective-permute-start.37 = (bf16[112,2304]{1,0:T(8,128)(2,1)S(1)}, bf16[112,2304]{1,0:T(8,128)(2,1)S(1)}, u32[]{:S(2)}, u32[]{:S(2)}) collective-permute-start(bf16[112,2304]{1,0:T(8,128)(2,1)S(1)} %collective-permute-done.33), channel_id=1, source_target_pairs={{0,4},{4,0},{8,12},{12,8},{16,20},{20,16},{24,28},{28,24},{1,5},{5... | collective-permute-start | bytes 1548296 | tf_op jit(solution)/shard_map/ppermute | solution.py:77
  428.6 35.4 %collective-permute-start.39 = (bf16[448,2304]{1,0:T(8,128)(2,1)S(1)}, bf16[448,2304]{1,0:T(8,128)(2,1)S(1)}, u32[]{:S(2)}, u32[]{:S(2)}) collective-permute-start(bf16[448,2304]{1,0:T(8,128)(2,1)S(1)} %pad_maximum_fusion.7), channel_id=1, source_target_pairs={{0,1},{1,0},{2,3},{3,2},{4,5},{5,4},{6,7},{7,6},{8,9},{9,8},{10,11... | collective-permute-start | bytes 6193160 | tf_op jit(solution)/shard_map/ppermute | solution.py:73
  501.7 51.3 %collective-permute-start.46 = (bf16[112,2304]{1,0:T(8,128)(2,1)S(1)}, bf16[112,2304]{1,0:T(8,128)(2,1)S(1)}, u32[]{:S(2)}, u32[]{:S(2)}) collective-permute-start(bf16[112,2304]{1,0:T(8,128)(2,1)S(1)} %get-tuple-element.117), channel_id=1, source_target_pairs={{0,4},{4,0},{8,12},{12,8},{16,20},{20,16},{24,28},{28,24},{1,5},{5... | collective-permute-start | bytes 1548296 | tf_op jit(solution)/shard_map/ppermute | solution.py:77
  503.8 34.2 %collective-permute-start.47 = (bf16[112,2304]{1,0:T(8,128)(2,1)S(1)}, bf16[112,2304]{1,0:T(8,128)(2,1)S(1)}, u32[]{:S(2)}, u32[]{:S(2)}) collective-permute-start(bf16[112,2304]{1,0:T(8,128)(2,1)S(1)} %get-tuple-element.119), channel_id=1, source_target_pairs={{0,4},{4,0},{8,12},{12,8},{16,20},{20,16},{24,28},{28,24},{1,5},{5... | collective-permute-start | bytes 1548296 | tf_op jit(solution)/shard_map/ppermute | solution.py:77
  548.9 33.7 %collective-permute-start.50 = (bf16[8,144,640]{2,1,0:T(8,128)(2,1)S(1)}, bf16[8,144,640]{2,1,0:T(8,128)(2,1)S(1)}, u32[]{:S(2)}, u32[]{:S(2)}) collective-permute-start(bf16[8,144,640]{2,1,0:T(8,128)(2,1)S(1)} %fusion.34), channel_id=1, source_target_pairs={{0,2},{2,0},{1,3},{3,1},{4,6},{6,4},{5,7},{7,5},{8,10},{10,8},{9,1... | collective-permute-start | bytes 4423688 | tf_op jit(solution)/shard_map/ppermute | solution.py:73
  598.1 35.4 %collective-permute-start.65 = (bf16[8,144,640]{2,1,0:T(8,128)(2,1)}, bf16[8,144,640]{2,1,0:T(8,128)(2,1)}, u32[]{:S(2)}, u32[]{:S(2)}) collective-permute-start(bf16[8,144,640]{2,1,0:T(8,128)(2,1)} %fusion.36), channel_id=1, source_target_pairs={{0,2},{2,0},{1,3},{3,1},{4,6},{6,4},{5,7},{7,5},{8,10},{10,8},{9,1... | collective-permute-start | bytes 4423688 | tf_op jit(solution)/shard_map/ppermute | solution.py:73
  599.6 200.3 %collective-permute-start.66 = (bf16[8,144,640]{2,1,0:T(8,128)(2,1)}, bf16[8,144,640]{2,1,0:T(8,128)(2,1)}, u32[]{:S(2)}, u32[]{:S(2)}) collective-permute-start(bf16[8,144,640]{2,1,0:T(8,128)(2,1)} %fusion.35), channel_id=1, source_target_pairs={{0,2},{2,0},{1,3},{3,1},{4,6},{6,4},{5,7},{7,5},{8,10},{10,8},{9,1... | collective-permute-start | bytes 4423688 | tf_op jit(solution)/shard_map/ppermute | solution.py:73
  637.0 162.9 %all-to-all-start.2 = ((bf16[8,144,1280]{2,1,0:T(8,128)(2,1)}), bf16[8,144,1280]{2,1,0:T(8,128)(2,1)S(1)}, u32[]{:S(2)}, u32[]{:S(2)}) async-start(bf16[8,144,1280]{2,1,0:T(8,128)(2,1)} %pad_maximum_fusion), calls=%async_computation.2 | async-start | bytes 5898240 | tf_op jit(solution)/shard_map/all_to_all | solution.py:334
  648.6 70.9 %collective-permute-start.53 = (f32[224,2304]{1,0:T(8,128)S(1)}, f32[224,2304]{1,0:T(8,128)S(1)}, u32[]{:S(2)}, u32[]{:S(2)}) collective-permute-start(f32[224,2304]{1,0:T(8,128)S(1)} %pad_maximum_fusion.10), channel_id=1, source_target_pairs={{0,1},{1,0},{2,3},{3,2},{4,5},{5,4},{6,7},{7,6},{8,9},{9,8},{10,11... | collective-permute-start | bytes 6193160 | tf_op jit(solution)/shard_map/ppermute | solution.py:73
  649.1 67.3 %collective-permute-start.58 = (bf16[288,1536]{1,0:T(8,128)(2,1)S(1)}, bf16[288,1536]{1,0:T(8,128)(2,1)S(1)}, u32[]{:S(2)}, u32[]{:S(2)}) collective-permute-start(bf16[288,1536]{1,0:T(8,128)(2,1)S(1)} %pad_maximum_fusion.18), channel_id=1, source_target_pairs={{0,4},{4,0},{8,12},{12,8},{16,20},{20,16},{24,28},{28,24},{1,5},{5... | collective-permute-start | bytes 2654216 | tf_op jit(solution)/shard_map/ppermute | solution.py:77
  651.3 64.8 %collective-permute-start.61 = (bf16[288,1536]{1,0:T(8,128)(2,1)S(1)}, bf16[288,1536]{1,0:T(8,128)(2,1)S(1)}, u32[]{:S(2)}, u32[]{:S(2)}) collective-permute-start(bf16[288,1536]{1,0:T(8,128)(2,1)S(1)} %pad_maximum_fusion.20), channel_id=1, source_target_pairs={{0,4},{4,0},{8,12},{12,8},{16,20},{20,16},{24,28},{28,24},{1,5},{5... | collective-permute-start | bytes 2654216 | tf_op jit(solution)/shard_map/ppermute | solution.py:77
  651.4 83.6 %collective-permute-start.60 = (bf16[288,1536]{1,0:T(8,128)(2,1)S(1)}, bf16[288,1536]{1,0:T(8,128)(2,1)S(1)}, u32[]{:S(2)}, u32[]{:S(2)}) collective-permute-start(bf16[288,1536]{1,0:T(8,128)(2,1)S(1)} %pad_maximum_fusion.19), channel_id=1, source_target_pairs={{0,4},{4,0},{8,12},{12,8},{16,20},{20,16},{24,28},{28,24},{1,5},{5... | collective-permute-start | bytes 2654216 | tf_op jit(solution)/shard_map/ppermute | solution.py:77
  716.0 48.6 %collective-permute-start.57 = (bf16[288,1536]{1,0:T(8,128)(2,1)}, bf16[288,1536]{1,0:T(8,128)(2,1)}, u32[]{:S(2)}, u32[]{:S(2)}) collective-permute-start(bf16[288,1536]{1,0:T(8,128)(2,1)} %pad_maximum_fusion.17), channel_id=1, source_target_pairs={{0,4},{4,0},{8,12},{12,8},{16,20},{20,16},{24,28},{28,24},{1,5},{5... | collective-permute-start | bytes 2654216 | tf_op jit(solution)/shard_map/ppermute | solution.py:77
  719.5 52.8 %collective-permute-start.59 = (bf16[288,1536]{1,0:T(8,128)(2,1)}, bf16[288,1536]{1,0:T(8,128)(2,1)}, u32[]{:S(2)}, u32[]{:S(2)}) collective-permute-start(bf16[288,1536]{1,0:T(8,128)(2,1)} %fusion.29), channel_id=1, source_target_pairs={{0,8},{4,12},{8,0},{12,4},{16,24},{20,28},{24,16},{28,20},{1,9},{5... | collective-permute-start | bytes 2654216 | tf_op jit(solution)/shard_map/ppermute | solution.py:77
  740.4 37.2 %collective-permute-start.63 = (bf16[288,1536]{1,0:T(8,128)(2,1)}, bf16[288,1536]{1,0:T(8,128)(2,1)}, u32[]{:S(2)}, u32[]{:S(2)}) collective-permute-start(bf16[288,1536]{1,0:T(8,128)(2,1)} %fusion.31), channel_id=1, source_target_pairs={{0,16},{4,20},{8,24},{12,28},{16,0},{20,4},{24,8},{28,12},{1,17},{... | collective-permute-start | bytes 2654216 | tf_op jit(solution)/shard_map/ppermute | solution.py:77
  804.7 34.8 %all-to-all-start.3 = ((bf16[8,144,640]{2,1,0:T(8,128)(2,1)}), bf16[8,144,640]{2,1,0:T(8,128)(2,1)S(1)}, u32[]{:S(2)}, u32[]{:S(2)}) async-start(bf16[8,144,640]{2,1,0:T(8,128)(2,1)} %fusion.8), calls=%async_computation.3 | async-start | bytes 2949120 | tf_op jit(solution)/shard_map/all_to_all | solution.py:334
  (129 other events, 1762.0 us)
Sparse Core Ops, SparseCore 0:
  19.5 79.7 all-gather.1

commit v3 on v2

--- a/solution.py
+++ b/solution.py
@@ -4,6 +4,8 @@
 import jax
 import jax.numpy as jnp
 from jax import lax
+from jax.experimental import pallas as pl
+from jax.experimental.pallas import tpu as pltpu
 from jax.sharding import PartitionSpec as P
 
 HEAD_DIM = 256
@@ -53,16 +55,81 @@
     return inner.astype(f32)[:, None] * freq[None, :]
 
 
-def rotate(field, angles):
-    half_size = field.shape[-1] // 2
-    cosine = jnp.cos(angles)[:, None, :]
-    sine = jnp.sin(angles)[:, None, :]
-    first_half = field[..., :half_size]
-    second_half = field[..., half_size:]
+def turn(field, cosine, sine):
+    half = field.shape[1] // 2
+    first, second = field[:, :half], field[:, half:]
     return jnp.concatenate(
-        [first_half * cosine - second_half * sine, second_half * cosine + first_half * sine],
-        axis=-1,
-    )
+        [first * cosine - second * sine, second * cosine + first * sine], axis=1
+    )
+
+
+def softmax_of(query, key, allowed):
+    ratio = jnp.tanh(dot(query, key, ((1,), (1,))) / soft_cap)
+    masked = jnp.where(allowed, soft_cap * ratio, -1e30)
+    terms = jnp.exp(masked - jnp.max(masked, axis=1, keepdims=True))
+    return ratio, terms / jnp.sum(terms, axis=1, keepdims=True)
+
+
+def allowed_of(row_ref, col_ref):
+    segment, inner = row_ref[:, 0:1], row_ref[:, 1:2]
+    return (segment == col_ref[0:1, :]) & (col_ref[1:2, :] <= inner)
+
+
+def attend_body(heads, kv_heads, qkv_ref, cos_ref, sin_ref, row_ref, col_ref, *out_refs):
+    attended_ref, query_ref, key_ref, value_ref = out_refs
+    size = HEAD_DIM
+    allowed = allowed_of(row_ref, col_ref)
+    cosine, sine = cos_ref[...], sin_ref[...]
+    for kv in range(kv_heads):
+        own = slice(kv * size, (kv + 1) * size)
+        at = heads * size + kv * size
+        key = turn(qkv_ref[:, at : at + size], cosine, sine).astype(b16)
+        at += kv_heads * size
+        value = qkv_ref[:, at : at + size].astype(b16)
+        key_ref[:, own] = key
+        value_ref[:, own] = value
+        for head in range(kv * heads // kv_heads, (kv + 1) * heads // kv_heads):
+            own = slice(head * size, (head + 1) * size)
+            query = (turn(qkv_ref[:, own], cosine, sine) * size**-0.5).astype(b16)
+            query_ref[:, own] = query
+            _, probs = softmax_of(query, key, allowed)
+            attended_ref[:, own] = dot(probs.astype(b16), value, ((1,), (0,))).astype(b16)
+
+
+def attend_back_body(heads, kv_heads, d_att_ref, query_ref, key_ref, value_ref, cos_ref, sin_ref, row_ref, col_ref, out_ref):
+    size = HEAD_DIM
+    allowed = allowed_of(row_ref, col_ref)
+    cosine, sine = cos_ref[...], sin_ref[...]
+    for kv in range(kv_heads):
+        own = slice(kv * size, (kv + 1) * size)
+        key, value = key_ref[:, own], value_ref[:, own]
+        d_key = d_value = 0.0
+        for head in range(kv * heads // kv_heads, (kv + 1) * heads // kv_heads):
+            own = slice(head * size, (head + 1) * size)
+            query, d_att = query_ref[:, own], d_att_ref[:, own]
+            ratio, probs = softmax_of(query, key, allowed)
+            d_probs = dot(d_att, value, ((1,), (1,)))
+            d_soft = probs * (d_probs - jnp.sum(probs * d_probs, axis=1, keepdims=True))
+            d_scores = (d_soft * (1.0 - ratio * ratio)).astype(b16)
+            d_query = dot(d_scores, key, ((1,), (0,))) * size**-0.5
+            out_ref[:, own] = turn(d_query, cosine, -sine).astype(b16)
+            d_key += dot(d_scores, query, ((0,), (0,)))
+            d_value += dot(probs.astype(b16), d_att, ((0,), (0,)))
+        at = heads * size + kv * size
+        out_ref[:, at : at + size] = turn(d_key, cosine, -sine).astype(b16)
+        at += kv_heads * size
+        out_ref[:, at : at + size] = d_value.astype(b16)
+
+
+def one_block(body, outs, *args):
+    return pl.pallas_call(
+        body,
+        out_shape=outs,
+        in_specs=[pl.BlockSpec(memory_space=pltpu.VMEM)] * len(args),
+        out_specs=jax.tree.map(lambda _: pl.BlockSpec(memory_space=pltpu.VMEM), outs),
+        compiler_params=pltpu.CompilerParams(vmem_limit_bytes=40 << 20),
+        cost_estimate=pl.CostEstimate(flops=1000, bytes_accessed=1000, transcendentals=0),
+    )(*args)
 
 
 def dot(lhs, rhs, dims):
@@ -78,16 +145,16 @@
 
 
 def gather_rows(own, n, checks=()):
-    have = [own]
+    have, near = [own], hop(own, 1, n)
     bit = n // 2
     while bit > 1:
         new = [hop(piece, bit, n) for piece in have]
-        if bit == n // 2 and checks:
-            new = [after(piece, *checks) for piece in new]
+        if len(have) == 1:
+            new = [after(new[0], near)]
         have = have + new
         bit //= 2
     even = jnp.concatenate(have)
-    odd = jnp.concatenate([hop(piece, 1, n) for piece in have])
+    odd = jnp.concatenate([near] + [hop(piece, 1, n) for piece in have[1:]])
     rows = jnp.concatenate([even, odd, swap(even, "tp"), swap(odd, "tp")])
     return rows, have[-1]
 
@@ -96,14 +163,21 @@
     return lax.optimization_barrier((value, *others))[0]
 
 
-def scatter_blocks(blocks, bit, n):
+def scatter_blocks(blocks, bit, n, serial=False, gates=()):
     marks = []
     while bit < n:
         keep = len(blocks) // 2
         marks.append(blocks[-1])
-        blocks = [
-            blocks[k] + hop(blocks[keep + k].astype(b16), bit, n).astype(f32) for k in range(keep)
-        ]
+        came = [None] * keep
+        order = sorted(range(keep), key=lambda k: keys_of(n)[k], reverse=True)
+        for at, k in enumerate(order):
+            piece = blocks[keep + k].astype(b16)
+            if serial and bit == 1 and at:
+                piece = after(piece, came[order[at - 1]], *(gates if at == 1 else ()))
+            came[k] = hop(piece, bit, n)
+            if serial and bit == 1 and at == 1:
+                marks[0] = came[k]
+        blocks = [block + piece.astype(f32) for block, piece in zip(blocks, came)]
         bit *= 2
     return blocks[0], marks
 
@@ -136,7 +210,7 @@
     return b0 + got[:rows] + swap((b2 + got[rows:]).astype(b16), "ctx").astype(f32)
 
 
-def range_order(n):
+def keys_of(n):
     order, bit = [0], n // 2
     while bit:
         order = order + [k ^ bit for k in order]
@@ -185,8 +259,6 @@
     k_cols = key_weight.shape[1] // 2
     q_local = q_cols // head_size
     kv_local = k_cols // head_size
-    group_size = q_local // kv_local
-    query_scale = head_size ** (-0.5)
     ff_local = gate_weight.shape[1]
     ff_own = ff_local // n
 
@@ -198,7 +270,6 @@
     )
     segment, inner = placement_of(lengths[0], packed)
     angles = angles_of(inner, head_size)
-    allowed = (segment[:, None] == segment[None, :]) & (inner[None, :] <= inner[:, None])
 
     mine = lax.dynamic_slice_in_dim(tokens, tp * rows, rows)
     across = swap(mine, "ctx")
@@ -270,23 +341,17 @@
     normed_attn = rms_scale(slot_in, gains[0]).astype(b16)
     qkv = dot(normed_attn, qkv_weight, ((1,), (0,)))
     all_rows = 2 * tok_rows
-    query_lin = qkv[:, :q_cols].reshape(all_rows, q_local, head_size)
-    key_lin = qkv[:, q_cols : q_cols + k_cols].reshape(all_rows, kv_local, head_size)
-    values = qkv[:, q_cols + k_cols :].astype(b16).reshape(all_rows, kv_local, head_size)
-    queries = (rotate(query_lin, angles) * query_scale).astype(b16)
-    queries = queries.reshape(all_rows, kv_local, group_size, head_size)
-    keys = rotate(key_lin, angles).astype(b16)
-    raw_scores = jnp.einsum("qkgd,skd->kgqs", queries, keys, preferred_element_type=f32)
-    tanh_ratio = jnp.tanh(raw_scores / soft_cap)
-    masked = jnp.where(allowed[None, None], soft_cap * tanh_ratio, -1e30)
-    row_peak = jnp.max(masked, axis=-1, keepdims=True)
-    exp_terms = jnp.exp(masked - row_peak)
-    probs = exp_terms / jnp.sum(exp_terms, axis=-1, keepdims=True)
-    probs_low = probs.astype(b16)
-    attended = (
-        jnp.einsum("kgqs,skd->qkgd", probs_low, values, preferred_element_type=f32)
-        .reshape(all_rows, q_cols)
-        .astype(b16)
+    cosine, sine = jnp.cos(angles), jnp.sin(angles)
+    places = jnp.stack([segment, inner])
+    held = lambda cols: jax.ShapeDtypeStruct((all_rows, cols), b16)
+    attended, queries, keys, values = one_block(
+        functools.partial(attend_body, q_local, kv_local),
+        [held(q_cols), held(q_cols), held(k_cols), held(k_cols)],
+        qkv,
+        cosine,
+        sine,
+        places.T,
+        places,
     )
     attn_out = scatter_group(dot(attended, out_weight, ((1,), (1,))))
     middle = resid_in + rms_scale(attn_out, gains[1])
@@ -361,23 +426,20 @@
     d_attn_raw, gain_two_term = norm_back(attn_out, gains[1], d_middle)
     d_attn_out = gather_group(d_attn_raw.astype(b16))
     up_got = swap(after(up_send, d_attn_out), "ctx")
+    down_rows = to_owners([down_keep], [down_got], d_normed_ffn)
     d_attended = dot(d_attn_out, out_weight, ((1,), (0,))).astype(b16)
-    dg_rows = to_owners([down_keep, gate_keep], [down_got, gate_got], d_attended)
-    d_att = d_attended.reshape(all_rows, kv_local, group_size, head_size)
-    d_probs = jnp.einsum("qkgd,skd->kgqs", d_att, values, preferred_element_type=f32)
-    d_soft = probs * (d_probs - jnp.sum(probs * d_probs, axis=-1, keepdims=True))
-    d_scores = (d_soft * (1.0 - tanh_ratio * tanh_ratio)).astype(b16)
-    d_queries = jnp.einsum("kgqs,skd->qkgd", d_scores, keys, preferred_element_type=f32)
-    d_keys = jnp.einsum("kgqs,qkgd->skd", d_scores, queries, preferred_element_type=f32)
-    d_values = jnp.einsum("kgqs,qkgd->skd", probs_low, d_att, preferred_element_type=f32)
-    d_query_lin = (
-        rotate(d_queries.reshape(all_rows, q_local, head_size) * query_scale, -angles)
-        .reshape(all_rows, q_cols)
-        .astype(b16)
-    )
-    d_key_lin = rotate(d_keys, -angles).reshape(all_rows, k_cols).astype(b16)
-    d_value = d_values.reshape(all_rows, k_cols).astype(b16)
-    d_qkv = jnp.concatenate([d_query_lin, d_key_lin, d_value], axis=1)
+    d_qkv = one_block(
+        functools.partial(attend_back_body, q_local, kv_local),
+        held(q_cols + 2 * k_cols),
+        d_attended,
+        queries,
+        keys,
+        values,
+        cosine,
+        sine,
+        places.T,
+        places,
+    )
     d_normed_part = dot(d_qkv, qkv_weight, ((1,), (1,)))
     d_normed_attn = scatter_group(d_normed_part)
     resid_part, gain_one_term = norm_back(resid_in, gains[0], d_normed_attn)
@@ -397,14 +459,15 @@
                 [lax.dynamic_index_in_dim(terms, me ^ k, 0, keepdims=False) for terms in attn_terms],
                 axis=1,
             )
-            for k in range_order(n)
+            for k in keys_of(n)
         ],
         1,
         n,
-    )
-    dg_rows = after(dg_rows, marks[1])
-    down_rows, gate_rows = dg_rows[..., :window], dg_rows[..., window:]
-    up_rows = to_owners([up_keep], [up_got], dg_rows)
+        serial=True,
+        gates=[down_rows],
+    )
+    gu_rows = after(to_owners([gate_keep, up_keep], [gate_got, up_got], marks[0]), attn_rows)
+    gate_rows, up_rows = gu_rows[..., :window], gu_rows[..., window:]
     gate_weight_grad = columns_joined(gate_rows)
     up_weight_grad = columns_joined(up_rows)
     down_weight_grad = columns_joined(down_rows).T
@@ -426,9 +489,9 @@
         lax.dynamic_index_in_dim(gain_terms, 1 - ctx, 1, keepdims=False), "ctx"
     )
     gain_rows = jnp.stack(
-        [lax.dynamic_index_in_dim(gain_terms, me ^ k, 0, keepdims=False) for k in range_order(n)]
-    )
-    gain_rows = after(gain_rows, up_rows)
+        [lax.dynamic_index_in_dim(gain_terms, me ^ k, 0, keepdims=False) for k in keys_of(n)]
+    )
+    gain_rows = after(gain_rows, attn_rows)
     bit = 1
     while bit < n:
         keep = gain_rows.shape[0] // 2

time: 860 us -> 823 us (0.957)
  starting transfers between devices: 113 us -> 97.1 us
  matrix products: 129 us -> 116 us
  local copies, waits for them, and re-layouts: 111 us -> 98 us
    all_to_all x2, waiting for transfers between devices: 20.6 us -> 0.01 us  [to_owners(): lax.all_to_all(jnp.concatenate(low, axis=2), 'fsdp', 0, 0, tiled=True)]
    ppermute x27, waiting for transfers between devices: 59.4 us -> 70.7 us  [swap(): return lax.ppermute(piece, axis, [(0, 1), (1, 0)])]
    all_to_all x2, starting transfers between devices: 20.8 us -> 9.68 us  [to_units(): return lax.all_to_all(own, 'fsdp', 0, 0, tiled=True)]
    unnamed x203 -> x160, local copies, waits for them, and re-layouts: 45.5 us -> 44.7 us
  transfers between devices with their start and end apart: 77 -> 77, of which waited for: 40 -> 41; matrix products, arithmetic and copies ran while one was open for 30% -> 27% of each run, Pallas kernels for 0% -> 1%
where the time goes in v3:
time: 823 us; the launch traced here: 817 us
  waiting for transfers between devices  423 us (51%)
  matrix products  116 us (14%)
  local copies, waits for them, and re-layouts  98 us (12%)
  starting transfers between devices  97.1 us (12%)
  other arithmetic  62.1 us (8%)
  between operations  16.5 us (2%)
    ppermute x45, waiting for transfers between devices, hop(): return lax.ppermute(piece, 'fsdp', [(d, d ^ step) for d in range(n)])  352 us
    dot_general x21, matrix products, dot(): lax.dot_general(lhs, rhs, (dims, ((), ())), preferred_element_type=f32)  116 us
    ppermute x27, waiting for transfers between devices, swap(): return lax.ppermute(piece, axis, [(0, 1), (1, 0)])  70.7 us
    ppermute x45, starting transfers between devices, hop(): return lax.ppermute(piece, 'fsdp', [(d, d ^ step) for d in range(n)])  58.4 us
    unnamed x160, local copies, waits for them, and re-layouts  44.7 us
    ppermute x27, starting transfers between devices, swap(): return lax.ppermute(piece, axis, [(0, 1), (1, 0)])  19.9 us
  transfers between devices with their start and end apart: 77, of which 41 were waited for; matrix products, arithmetic and copies ran while one was open for 27% of the time, Pallas kernels for 1%

profile of v3, /device:TPU:0, one launch (start us, length us, event | category | flops | bytes accessed | tf_op | source)
XLA Modules:
  0.0 817.1 jit_solution(18416085700106715819)
XLA Ops:
  24.8 8.4 %collective-permute-done = bf16[112,2304]{1,0:T(8,128)(2,1)} collective-permute-done((bf16[112,2304]{1,0:T(8,128)(2,1)S(1)}, bf16[112,2304]{1,0:T(8,128)(2,1)}, u32[]{:S(2)}, u32[]{:S(2)}) %collective-permute-start) | collective-permute-done | bytes 516128 | tf_op jit(solution)/shard_map/ppermute | solution.py:140
  33.2 18.6 %collective-permute-done.2 = bf16[304,1024]{1,0:T(8,128)(2,1)} collective-permute-done((bf16[304,1024]{1,0:T(8,128)(2,1)S(1)}, bf16[304,1024]{1,0:T(8,128)(2,1)}, u32[]{:S(2)}, u32[]{:S(2)}) %collective-permute-start.2) | collective-permute-done | bytes 622624 | tf_op jit(solution)/shard_map/ppermute | solution.py:144
  66.2 13.6 %collective-permute-done.4 = bf16[304,1024]{1,0:T(8,128)(2,1)S(1)} collective-permute-done((bf16[304,1024]{1,0:T(8,128)(2,1)}, bf16[304,1024]{1,0:T(8,128)(2,1)S(1)}, u32[]{:S(2)}, u32[]{:S(2)}) %collective-permute-start.4) | collective-permute-done | bytes 622624 | tf_op jit(solution)/shard_map/ppermute | solution.py:144
  102.6 28.8 %collective-permute-done.8 = bf16[304,1024]{1,0:T(8,128)(2,1)S(1)} collective-permute-done((bf16[304,1024]{1,0:T(8,128)(2,1)S(1)}, bf16[304,1024]{1,0:T(8,128)(2,1)S(1)}, u32[]{:S(2)}, u32[]{:S(2)}) %collective-permute-start.8) | collective-permute-done | bytes 622624 | tf_op jit(solution)/shard_map/ppermute | solution.py:144
  150.6 12.2 %collective-permute-done.10 = bf16[112,2304]{1,0:T(8,128)(2,1)S(1)} collective-permute-done((bf16[112,2304]{1,0:T(8,128)(2,1)S(1)}, bf16[112,2304]{1,0:T(8,128)(2,1)S(1)}, u32[]{:S(2)}, u32[]{:S(2)}) %collective-permute-start.10) | collective-permute-done | bytes 516128 | tf_op jit(solution)/shard_map/ppermute | solution.py:140
  168.7 7.8 collective-permute-start.13
  189.9 13.5 %collective-permute-done.11 = bf16[112,2304]{1,0:T(8,128)(2,1)} collective-permute-done((bf16[112,2304]{1,0:T(8,128)(2,1)S(1)}, bf16[112,2304]{1,0:T(8,128)(2,1)}, u32[]{:S(2)}, u32[]{:S(2)}) %collective-permute-start.11) | collective-permute-done | bytes 516128 | tf_op jit(solution)/shard_map/ppermute | solution.py:144
  232.9 20.1 %collective-permute-done.17 = bf16[112,2304]{1,0:T(8,128)(2,1)S(1)} collective-permute-done((bf16[112,2304]{1,0:T(8,128)(2,1)}, bf16[112,2304]{1,0:T(8,128)(2,1)S(1)}, u32[]{:S(2)}, u32[]{:S(2)}) %collective-permute-start.17) | collective-permute-done | bytes 516128 | tf_op jit(solution)/shard_map/ppermute | solution.py:144
  267.2 15.0 %fusion.154 = f32[1792,1280]{1,0:T(8,128)S(1)} fusion(bf16[1792,2304]{1,0:T(8,128)(2,1)} %constant_dynamic-update-slice_fusion, bf16[2304,1280]{1,0:T(8,128)(2,1)} %bitcast.35), kind=kOutput, calls=%fused_computation.394 | convolution fusion | flops 10569646080 | bytes 23330816 | tf_op jit(solution)/shard_map/dot_general | solution.py:136
  288.3 12.3 %collective-permute-done.21 = bf16[8,144,640]{2,1,0:T(8,128)(2,1)S(1)} collective-permute-done((bf16[8,144,640]{2,1,0:T(8,128)(2,1)}, bf16[8,144,640]{2,1,0:T(8,128)(2,1)S(1)}, u32[]{:S(2)}, u32[]{:S(2)}) %collective-permute-start.21) | collective-permute-done | bytes 1474592 | tf_op jit(solution)/shard_map/ppermute | solution.py:140
  313.6 10.7 %collective-permute-done.28 = bf16[112,2304]{1,0:T(8,128)(2,1)S(1)} collective-permute-done((bf16[112,2304]{1,0:T(8,128)(2,1)S(1)}, bf16[112,2304]{1,0:T(8,128)(2,1)S(1)}, u32[]{:S(2)}, u32[]{:S(2)}) %collective-permute-start.28) | collective-permute-done | bytes 516128 | tf_op jit(solution)/shard_map/ppermute | solution.py:144
  324.2 11.1 %collective-permute-done.25 = bf16[112,2304]{1,0:T(8,128)(2,1)S(1)} collective-permute-done((bf16[112,2304]{1,0:T(8,128)(2,1)S(1)}, bf16[112,2304]{1,0:T(8,128)(2,1)S(1)}, u32[]{:S(2)}, u32[]{:S(2)}) %collective-permute-start.25) | collective-permute-done | bytes 516128 | tf_op jit(solution)/shard_map/ppermute | solution.py:144
  338.3 8.0 collective-permute-done.27
  346.4 10.1 %collective-permute-done.29 = bf16[112,2304]{1,0:T(8,128)(2,1)S(1)} collective-permute-done((bf16[112,2304]{1,0:T(8,128)(2,1)S(1)}, bf16[112,2304]{1,0:T(8,128)(2,1)S(1)}, u32[]{:S(2)}, u32[]{:S(2)}) %collective-permute-start.29) | collective-permute-done | bytes 516128 | tf_op jit(solution)/shard_map/ppermute | solution.py:144
  358.9 7.7 collective-permute-done.26
  366.6 10.9 %collective-permute-done.30 = bf16[112,2304]{1,0:T(8,128)(2,1)} collective-permute-done((bf16[112,2304]{1,0:T(8,128)(2,1)S(1)}, bf16[112,2304]{1,0:T(8,128)(2,1)}, u32[]{:S(2)}, u32[]{:S(2)}) %collective-permute-start.30) | collective-permute-done | bytes 516128 | tf_op jit(solution)/shard_map/ppermute | solution.py:144
  382.8 7.8 collective-permute-done.33
  390.6 8.6 %collective-permute-done.32 = bf16[112,2304]{1,0:T(8,128)(2,1)S(1)} collective-permute-done((bf16[112,2304]{1,0:T(8,128)(2,1)S(1)}, bf16[112,2304]{1,0:T(8,128)(2,1)S(1)}, u32[]{:S(2)}, u32[]{:S(2)}) %collective-permute-start.32) | collective-permute-done | bytes 516128 | tf_op jit(solution)/shard_map/ppermute | solution.py:144
  402.1 8.4 %collective-permute-done.35 = bf16[112,2304]{1,0:T(8,128)(2,1)S(1)} collective-permute-done((bf16[112,2304]{1,0:T(8,128)(2,1)S(1)}, bf16[112,2304]{1,0:T(8,128)(2,1)S(1)}, u32[]{:S(2)}, u32[]{:S(2)}) %collective-permute-start.35) | collective-permute-done | bytes 516128 | tf_op jit(solution)/shard_map/ppermute | solution.py:144
  411.6 13.4 %collective-permute-done.37 = bf16[112,2304]{1,0:T(8,128)(2,1)S(1)} collective-permute-done((bf16[112,2304]{1,0:T(8,128)(2,1)S(1)}, bf16[112,2304]{1,0:T(8,128)(2,1)S(1)}, u32[]{:S(2)}, u32[]{:S(2)}) %collective-permute-start.37) | collective-permute-done | bytes 516128 | tf_op jit(solution)/shard_map/ppermute | solution.py:144
  425.0 7.6 collective-permute-done.38
  441.1 12.8 %select_convert_fusion = (bf16[1792,640]{1,0:T(8,128)(2,1)S(1)}, bf16[1792,640]{1,0:T(8,128)(2,1)S(1)}) fusion(pred[640]{0:T(1024)(128)(4,1)S(1)} %fusion.116, f32[1792,1280]{1,0:T(8,128)S(1)} %bitcast.313, bf16[1792,2304]{1,0:T(8,128)(2,1)} %constant_dynamic-update-slice_fusion.10, bf16[2304,640]{1,0:T(8,128)(2,1)S(1)} %bitcast.340), kind=kOutput, calls=%fused_computation.21 | convolution fusion | flops 5319229440 | bytes 24969856 | tf_op jit(solution)/shard_map/dot_general | solution.py:136
  482.3 17.7 %collective-permute-done.44 = bf16[112,2304]{1,0:T(8,128)(2,1)S(1)} collective-permute-done((bf16[112,2304]{1,0:T(8,128)(2,1)S(1)}, bf16[112,2304]{1,0:T(8,128)(2,1)S(1)}, u32[]{:S(2)}, u32[]{:S(2)}) %collective-permute-start.44) | collective-permute-done | bytes 516128 | tf_op jit(solution)/shard_map/ppermute | solution.py:144
  500.0 10.6 %collective-permute-done.47 = bf16[112,2304]{1,0:T(8,128)(2,1)S(1)} collective-permute-done((bf16[112,2304]{1,0:T(8,128)(2,1)S(1)}, bf16[112,2304]{1,0:T(8,128)(2,1)S(1)}, u32[]{:S(2)}, u32[]{:S(2)}) %collective-permute-start.47) | collective-permute-done | bytes 516128 | tf_op jit(solution)/shard_map/ppermute | solution.py:144
  512.6 9.7 %fusion.155 = f32[2304,640]{1,0:T(8,128)S(1)} fusion(bf16[1792,2304]{1,0:T(8,128)(2,1)} %constant_dynamic-update-slice_fusion.10, bf16[1792,640]{1,0:T(8,128)(2,1)S(1)} %copy-done.25), kind=kOutput, calls=%fused_computation.395 | convolution fusion | flops 5284823040 | bytes 16449536 | tf_op jit(solution)/shard_map/dot_general | solution.py:136
  526.1 9.3 %fusion.156 = f32[2304,640]{1,0:T(8,128)S(1)} fusion(bf16[1792,2304]{1,0:T(8,128)(2,1)} %constant_dynamic-update-slice_fusion, bf16[1792,640]{1,0:T(8,128)(2,1)S(1)} %get-tuple-element.88), kind=kOutput, calls=%fused_computation.396 | convolution fusion | flops 5284823040 | bytes 16449536 | tf_op jit(solution)/shard_map/dot_general | solution.py:136
  536.9 10.4 %fusion.157 = f32[2304,640]{1,0:T(8,128)S(1)} fusion(bf16[1792,2304]{1,0:T(8,128)(2,1)} %constant_dynamic-update-slice_fusion, bf16[1792,640]{1,0:T(8,128)(2,1)S(1)} %get-tuple-element.87), kind=kOutput, calls=%fused_computation.397 | convolution fusion | flops 5284823040 | bytes 16449536 | tf_op jit(solution)/shard_map/dot_general | solution.py:136
  559.8 10.6 %collective-permute-done.51 = bf16[112,2304]{1,0:T(8,128)(2,1)S(1)} collective-permute-done((bf16[112,2304]{1,0:T(8,128)(2,1)S(1)}, bf16[112,2304]{1,0:T(8,128)(2,1)S(1)}, u32[]{:S(2)}, u32[]{:S(2)}) %collective-permute-start.51) | collective-permute-done | bytes 516128 | tf_op jit(solution)/shard_map/ppermute | solution.py:140
  608.2 17.8 %collective-permute-done.57 = bf16[288,1536]{1,0:T(8,128)(2,1)S(1)} collective-permute-done((bf16[288,1536]{1,0:T(8,128)(2,1)S(1)}, bf16[288,1536]{1,0:T(8,128)(2,1)S(1)}, u32[]{:S(2)}, u32[]{:S(2)}) %collective-permute-start.57) | collective-permute-done | bytes 884768 | tf_op jit(solution)/shard_map/ppermute | solution.py:144
  639.3 12.4 %collective-permute-done.58 = bf16[288,1536]{1,0:T(8,128)(2,1)S(1)} collective-permute-done((bf16[288,1536]{1,0:T(8,128)(2,1)}, bf16[288,1536]{1,0:T(8,128)(2,1)S(1)}, u32[]{:S(2)}, u32[]{:S(2)}) %collective-permute-start.58) | collective-permute-done | bytes 884768 | tf_op jit(solution)/shard_map/ppermute | solution.py:144
  684.8 30.0 %collective-permute-done.59 = bf16[288,1536]{1,0:T(8,128)(2,1)} collective-permute-done((bf16[288,1536]{1,0:T(8,128)(2,1)}, bf16[288,1536]{1,0:T(8,128)(2,1)}, u32[]{:S(2)}, u32[]{:S(2)}) %collective-permute-start.59) | collective-permute-done | bytes 884768 | tf_op jit(solution)/shard_map/ppermute | solution.py:144
  722.7 43.7 %collective-permute-done.63 = bf16[288,1536]{1,0:T(8,128)(2,1)} collective-permute-done((bf16[288,1536]{1,0:T(8,128)(2,1)}, bf16[288,1536]{1,0:T(8,128)(2,1)}, u32[]{:S(2)}, u32[]{:S(2)}) %collective-permute-start.63) | collective-permute-done | bytes 884768 | tf_op jit(solution)/shard_map/ppermute | solution.py:144
  (478 shorter events, 361.0 us)
Async XLA Ops:
  7.2 132.9 %all-gather.2.cloned.1.call-start = ((), (), s32[]{:S(2)}) async-start(), calls=%async_computation.4 | async-start | bytes 2654208 | tf_op jit(solution)/shard_map/all_gather | solution.py:306
  11.4 82.4 %collective-permute-start.5 = (bf16[304,1024]{1,0:T(8,128)(2,1)S(1)}, bf16[304,1024]{1,0:T(8,128)(2,1)}, u32[]{:S(2)}, u32[]{:S(2)}) collective-permute-start(bf16[304,1024]{1,0:T(8,128)(2,1)S(1)} %pad_maximum_fusion.20), channel_id=1, source_target_pairs={{0,4},{4,0},{8,12},{12,8},{16,20},{20,16},{24,28},{28,24},{1,5},{5... | collective-permute-start | bytes 1867784 | tf_op jit(solution)/shard_map/ppermute | solution.py:144
  14.4 41.5 %collective-permute-start.3 = (bf16[304,1024]{1,0:T(8,128)(2,1)S(1)}, bf16[304,1024]{1,0:T(8,128)(2,1)}, u32[]{:S(2)}, u32[]{:S(2)}) collective-permute-start(bf16[304,1024]{1,0:T(8,128)(2,1)S(1)} %pad_maximum_fusion.20), channel_id=1, source_target_pairs={{0,8},{4,12},{8,0},{12,4},{16,24},{20,28},{24,16},{28,20},{1,9},{5... | collective-permute-start | bytes 1867784 | tf_op jit(solution)/shard_map/ppermute | solution.py:144
  16.0 35.8 %collective-permute-start.2 = (bf16[304,1024]{1,0:T(8,128)(2,1)S(1)}, bf16[304,1024]{1,0:T(8,128)(2,1)}, u32[]{:S(2)}, u32[]{:S(2)}) collective-permute-start(bf16[304,1024]{1,0:T(8,128)(2,1)S(1)} %pad_maximum_fusion.20), channel_id=1, source_target_pairs={{0,16},{4,20},{8,24},{12,28},{16,0},{20,4},{24,8},{28,12},{1,17},{... | collective-permute-start | bytes 1867784 | tf_op jit(solution)/shard_map/ppermute | solution.py:144
  33.2 28.1 %collective-permute-start.1 = (bf16[112,2304]{1,0:T(8,128)(2,1)}, bf16[112,2304]{1,0:T(8,128)(2,1)S(1)}, u32[]{:S(2)}, u32[]{:S(2)}) collective-permute-start(bf16[112,2304]{1,0:T(8,128)(2,1)} %collective-permute-done), channel_id=1, source_target_pairs={{0,1},{1,0},{2,3},{3,2},{4,5},{5,4},{6,7},{7,6},{8,9},{9,8},{10,11... | collective-permute-start | bytes 1548296 | tf_op jit(solution)/shard_map/ppermute | solution.py:140
  51.8 42.7 %collective-permute-start.6 = (bf16[304,1024]{1,0:T(8,128)(2,1)}, bf16[304,1024]{1,0:T(8,128)(2,1)}, u32[]{:S(2)}, u32[]{:S(2)}) collective-permute-start(bf16[304,1024]{1,0:T(8,128)(2,1)} %collective-permute-done.2), channel_id=1, source_target_pairs={{0,4},{4,0},{8,12},{12,8},{16,20},{20,16},{24,28},{28,24},{1,5},{5... | collective-permute-start | bytes 1867784 | tf_op jit(solution)/shard_map/ppermute | solution.py:144
  55.9 42.1 %collective-permute-start.7 = (bf16[304,1024]{1,0:T(8,128)(2,1)}, bf16[304,1024]{1,0:T(8,128)(2,1)}, u32[]{:S(2)}, u32[]{:S(2)}) collective-permute-start(bf16[304,1024]{1,0:T(8,128)(2,1)} %collective-permute-done.3), channel_id=1, source_target_pairs={{0,4},{4,0},{8,12},{12,8},{16,20},{20,16},{24,28},{28,24},{1,5},{5... | collective-permute-start | bytes 1867784 | tf_op jit(solution)/shard_map/ppermute | solution.py:144
  86.8 92.0 %all-to-all-start = ((bf16[8,144,1280]{2,1,0:T(8,128)(2,1)}), bf16[8,144,1280]{2,1,0:T(8,128)(2,1)}, u32[]{:S(2)}, u32[]{:S(2)}) async-start(bf16[8,144,1280]{2,1,0:T(8,128)(2,1)} %fusion.91), calls=%async_computation | async-start | bytes 5898240 | tf_op jit(solution)/shard_map/all_to_all | solution.py:330
  91.7 39.7 %collective-permute-start.8 = (bf16[304,1024]{1,0:T(8,128)(2,1)S(1)}, bf16[304,1024]{1,0:T(8,128)(2,1)S(1)}, u32[]{:S(2)}, u32[]{:S(2)}) collective-permute-start(bf16[304,1024]{1,0:T(8,128)(2,1)S(1)} %copy-done.37), channel_id=1, source_target_pairs={{0,4},{4,0},{8,12},{12,8},{16,20},{20,16},{24,28},{28,24},{1,5},{5... | collective-permute-start | bytes 1867784 | tf_op jit(solution)/shard_map/ppermute | solution.py:144
  168.7 36.9 %collective-permute-start.13 = (bf16[112,2304]{1,0:T(8,128)(2,1)S(1)}, bf16[112,2304]{1,0:T(8,128)(2,1)}, u32[]{:S(2)}, u32[]{:S(2)}) collective-permute-start(bf16[112,2304]{1,0:T(8,128)(2,1)S(1)} %get-tuple-element.80), channel_id=1, source_target_pairs={{0,8},{4,12},{8,0},{12,4},{16,24},{20,28},{24,16},{28,20},{1,9},{5... | collective-permute-start | bytes 1548296 | tf_op jit(solution)/shard_map/ppermute | solution.py:144
  185.5 73.7 %collective-permute-start.20 = (bf16[8,144,1280]{2,1,0:T(8,128)(2,1)}, bf16[8,144,1280]{2,1,0:T(8,128)(2,1)}, u32[]{:S(2)}, u32[]{:S(2)}) collective-permute-start(bf16[8,144,1280]{2,1,0:T(8,128)(2,1)} %all-to-all-done), channel_id=1, source_target_pairs={{0,2},{2,0},{1,3},{3,1},{4,6},{6,4},{5,7},{7,5},{8,10},{10,8},{9,1... | collective-permute-start | bytes 8847368 | tf_op jit(solution)/shard_map/ppermute | solution.py:140
  203.4 29.5 %collective-permute-start.15 = (bf16[112,2304]{1,0:T(8,128)(2,1)}, bf16[112,2304]{1,0:T(8,128)(2,1)}, u32[]{:S(2)}, u32[]{:S(2)}) collective-permute-start(bf16[112,2304]{1,0:T(8,128)(2,1)} %collective-permute-done.11), channel_id=1, source_target_pairs={{0,4},{4,0},{8,12},{12,8},{16,20},{20,16},{24,28},{28,24},{1,5},{5... | collective-permute-start | bytes 1548296 | tf_op jit(solution)/shard_map/ppermute | solution.py:144
  220.7 45.0 %all-to-all-start.1 = ((bf16[8,144,640]{2,1,0:T(8,128)(2,1)}), bf16[8,144,640]{2,1,0:T(8,128)(2,1)}, u32[]{:S(2)}, u32[]{:S(2)}) async-start(bf16[8,144,640]{2,1,0:T(8,128)(2,1)} %fusion.101), calls=%async_computation.1 | async-start | bytes 2949120 | tf_op jit(solution)/shard_map/all_to_all | solution.py:330
  227.0 35.8 %collective-permute-start.18 = (bf16[448,2304]{1,0:T(8,128)(2,1)S(1)}, bf16[448,2304]{1,0:T(8,128)(2,1)S(1)}, u32[]{:S(2)}, u32[]{:S(2)}) collective-permute-start(bf16[448,2304]{1,0:T(8,128)(2,1)S(1)} %pad_maximum_fusion.5), channel_id=1, source_target_pairs={{0,1},{1,0},{2,3},{3,2},{4,5},{5,4},{6,7},{7,6},{8,9},{9,8},{10,11... | collective-permute-start | bytes 6193160 | tf_op jit(solution)/shard_map/ppermute | solution.py:140
  265.7 34.9 %collective-permute-start.21 = (bf16[8,144,640]{2,1,0:T(8,128)(2,1)}, bf16[8,144,640]{2,1,0:T(8,128)(2,1)S(1)}, u32[]{:S(2)}, u32[]{:S(2)}) collective-permute-start(bf16[8,144,640]{2,1,0:T(8,128)(2,1)} %all-to-all-done.1), channel_id=1, source_target_pairs={{0,2},{2,0},{1,3},{3,1},{4,6},{6,4},{5,7},{7,5},{8,10},{10,8},{9,1... | collective-permute-start | bytes 4423688 | tf_op jit(solution)/shard_map/ppermute | solution.py:140
  311.7 34.7 %collective-permute-start.27 = (bf16[112,2304]{1,0:T(8,128)(2,1)S(1)}, bf16[112,2304]{1,0:T(8,128)(2,1)S(1)}, u32[]{:S(2)}, u32[]{:S(2)}) collective-permute-start(bf16[112,2304]{1,0:T(8,128)(2,1)S(1)} %get-tuple-element.138), channel_id=1, source_target_pairs={{0,4},{4,0},{8,12},{12,8},{16,20},{20,16},{24,28},{28,24},{1,5},{5... | collective-permute-start | bytes 1548296 | tf_op jit(solution)/shard_map/ppermute | solution.py:144
  337.1 29.5 %collective-permute-start.26 = (bf16[112,2304]{1,0:T(8,128)(2,1)}, bf16[112,2304]{1,0:T(8,128)(2,1)}, u32[]{:S(2)}, u32[]{:S(2)}) collective-permute-start(bf16[112,2304]{1,0:T(8,128)(2,1)} %get-tuple-element.110), channel_id=1, source_target_pairs={{0,8},{4,12},{8,0},{12,4},{16,24},{20,28},{24,16},{28,20},{1,9},{5... | collective-permute-start | bytes 1548296 | tf_op jit(solution)/shard_map/ppermute | solution.py:144
  474.3 50.3 %collective-permute-start.46 = (bf16[112,2304]{1,0:T(8,128)(2,1)S(1)}, bf16[112,2304]{1,0:T(8,128)(2,1)S(1)}, u32[]{:S(2)}, u32[]{:S(2)}) collective-permute-start(bf16[112,2304]{1,0:T(8,128)(2,1)S(1)} %get-tuple-element.133), channel_id=1, source_target_pairs={{0,4},{4,0},{8,12},{12,8},{16,20},{20,16},{24,28},{28,24},{1,5},{5... | collective-permute-start | bytes 1548296 | tf_op jit(solution)/shard_map/ppermute | solution.py:144
  476.4 34.2 %collective-permute-start.47 = (bf16[112,2304]{1,0:T(8,128)(2,1)S(1)}, bf16[112,2304]{1,0:T(8,128)(2,1)S(1)}, u32[]{:S(2)}, u32[]{:S(2)}) collective-permute-start(bf16[112,2304]{1,0:T(8,128)(2,1)S(1)} %get-tuple-element.135), channel_id=1, source_target_pairs={{0,4},{4,0},{8,12},{12,8},{16,20},{20,16},{24,28},{28,24},{1,5},{5... | collective-permute-start | bytes 1548296 | tf_op jit(solution)/shard_map/ppermute | solution.py:144
  522.6 33.6 %collective-permute-start.50 = (bf16[8,144,640]{2,1,0:T(8,128)(2,1)S(1)}, bf16[8,144,640]{2,1,0:T(8,128)(2,1)S(1)}, u32[]{:S(2)}, u32[]{:S(2)}) collective-permute-start(bf16[8,144,640]{2,1,0:T(8,128)(2,1)S(1)} %fusion.30), channel_id=1, source_target_pairs={{0,2},{2,0},{1,3},{3,1},{4,6},{6,4},{5,7},{7,5},{8,10},{10,8},{9,1... | collective-permute-start | bytes 4423688 | tf_op jit(solution)/shard_map/ppermute | solution.py:140
  572.6 79.0 %collective-permute-start.65 = (bf16[8,144,640]{2,1,0:T(8,128)(2,1)}, bf16[8,144,640]{2,1,0:T(8,128)(2,1)}, u32[]{:S(2)}, u32[]{:S(2)}) collective-permute-start(bf16[8,144,640]{2,1,0:T(8,128)(2,1)} %fusion.31), channel_id=1, source_target_pairs={{0,2},{2,0},{1,3},{3,1},{4,6},{6,4},{5,7},{7,5},{8,10},{10,8},{9,1... | collective-permute-start | bytes 4423688 | tf_op jit(solution)/shard_map/ppermute | solution.py:140
  574.1 65.1 %collective-permute-start.66 = (bf16[8,144,640]{2,1,0:T(8,128)(2,1)}, bf16[8,144,640]{2,1,0:T(8,128)(2,1)}, u32[]{:S(2)}, u32[]{:S(2)}) collective-permute-start(bf16[8,144,640]{2,1,0:T(8,128)(2,1)} %fusion.32), channel_id=1, source_target_pairs={{0,2},{2,0},{1,3},{3,1},{4,6},{6,4},{5,7},{7,5},{8,10},{10,8},{9,1... | collective-permute-start | bytes 4423688 | tf_op jit(solution)/shard_map/ppermute | solution.py:140
  578.0 52.0 %all-to-all-start.2 = ((bf16[8,144,640]{2,1,0:T(8,128)(2,1)}), bf16[8,144,640]{2,1,0:T(8,128)(2,1)}, u32[]{:S(2)}, u32[]{:S(2)}) async-start(bf16[8,144,640]{2,1,0:T(8,128)(2,1)} %fusion.10), calls=%async_computation.2 | async-start | bytes 2949120 | tf_op jit(solution)/shard_map/all_to_all | solution.py:399
  594.7 69.5 %collective-permute-start.53 = (f32[224,2304]{1,0:T(8,128)}, f32[224,2304]{1,0:T(8,128)}, u32[]{:S(2)}, u32[]{:S(2)}) collective-permute-start(f32[224,2304]{1,0:T(8,128)} %pad_maximum_fusion.10), channel_id=1, source_target_pairs={{0,1},{1,0},{2,3},{3,2},{4,5},{5,4},{6,7},{7,6},{8,9},{9,8},{10,11... | collective-permute-start | bytes 6193160 | tf_op jit(solution)/shard_map/ppermute | solution.py:140
  627.2 40.5 %collective-permute-start.62 = (bf16[288,1536]{1,0:T(8,128)(2,1)}, bf16[288,1536]{1,0:T(8,128)(2,1)}, u32[]{:S(2)}, u32[]{:S(2)}) collective-permute-start(bf16[288,1536]{1,0:T(8,128)(2,1)} %fusion.29), channel_id=1, source_target_pairs={{0,8},{4,12},{8,0},{12,4},{16,24},{20,28},{24,16},{28,20},{1,9},{5... | collective-permute-start | bytes 2654216 | tf_op jit(solution)/shard_map/ppermute | solution.py:144
  657.8 141.5 %all-to-all-start.3 = ((bf16[8,144,1280]{2,1,0:T(8,128)(2,1)}), bf16[8,144,1280]{2,1,0:T(8,128)(2,1)}, u32[]{:S(2)}, u32[]{:S(2)}) async-start(bf16[8,144,1280]{2,1,0:T(8,128)(2,1)} %pad_maximum_fusion), calls=%async_computation.3 | async-start | bytes 5898240 | tf_op jit(solution)/shard_map/all_to_all | solution.py:399
  662.4 52.4 %collective-permute-start.59 = (bf16[288,1536]{1,0:T(8,128)(2,1)}, bf16[288,1536]{1,0:T(8,128)(2,1)}, u32[]{:S(2)}, u32[]{:S(2)}) collective-permute-start(bf16[288,1536]{1,0:T(8,128)(2,1)} %pad_maximum_fusion.17), channel_id=1, source_target_pairs={{0,4},{4,0},{8,12},{12,8},{16,20},{20,16},{24,28},{28,24},{1,5},{5... | collective-permute-start | bytes 2654216 | tf_op jit(solution)/shard_map/ppermute | solution.py:144
  670.1 96.3 %collective-permute-start.63 = (bf16[288,1536]{1,0:T(8,128)(2,1)}, bf16[288,1536]{1,0:T(8,128)(2,1)}, u32[]{:S(2)}, u32[]{:S(2)}) collective-permute-start(bf16[288,1536]{1,0:T(8,128)(2,1)} %fusion.28), channel_id=1, source_target_pairs={{0,16},{4,20},{8,24},{12,28},{16,0},{20,4},{24,8},{28,12},{1,17},{... | collective-permute-start | bytes 2654216 | tf_op jit(solution)/shard_map/ppermute | solution.py:144
  683.0 39.6 %collective-permute-start.68 = (f32[8,4,144]{2,0,1:T(8,128)S(1)}, f32[8,4,144]{2,0,1:T(8,128)S(1)}, u32[]{:S(2)}, u32[]{:S(2)}) collective-permute-start(f32[8,4,144]{2,0,1:T(8,128)S(1)} %bitcast.357), channel_id=1, source_target_pairs={{0,2},{2,0},{1,3},{3,1},{4,6},{6,4},{5,7},{7,5},{8,10},{10,8},{9,1... | collective-permute-start | bytes 55304 | tf_op jit(solution)/shard_map/ppermute | solution.py:140
  714.7 51.6 %collective-permute-start.60 = (bf16[288,1536]{1,0:T(8,128)(2,1)}, bf16[288,1536]{1,0:T(8,128)(2,1)}, u32[]{:S(2)}, u32[]{:S(2)}) collective-permute-start(bf16[288,1536]{1,0:T(8,128)(2,1)} %pad_maximum_fusion.16), channel_id=1, source_target_pairs={{0,4},{4,0},{8,12},{12,8},{16,20},{20,16},{24,28},{28,24},{1,5},{5... | collective-permute-start | bytes 2654216 | tf_op jit(solution)/shard_map/ppermute | solution.py:144
  717.2 54.1 %collective-permute-start.61 = (bf16[288,1536]{1,0:T(8,128)(2,1)}, bf16[288,1536]{1,0:T(8,128)(2,1)}, u32[]{:S(2)}, u32[]{:S(2)}) collective-permute-start(bf16[288,1536]{1,0:T(8,128)(2,1)} %fusion.26), channel_id=1, source_target_pairs={{0,8},{4,12},{8,0},{12,4},{16,24},{20,28},{24,16},{28,20},{1,9},{5... | collective-permute-start | bytes 2654216 | tf_op jit(solution)/shard_map/ppermute | solution.py:144
  720.8 53.2 %collective-permute-start.55 = (bf16[112,2304]{1,0:T(8,128)(2,1)S(1)}, bf16[112,2304]{1,0:T(8,128)(2,1)}, u32[]{:S(2)}, u32[]{:S(2)}) collective-permute-start(bf16[112,2304]{1,0:T(8,128)(2,1)S(1)} %fusion.47), channel_id=1, source_target_pairs={{0,2},{2,0},{1,3},{3,1},{4,6},{6,4},{5,7},{7,5},{8,10},{10,8},{9,1... | collective-permute-start | bytes 1548296 | tf_op jit(solution)/shard_map/ppermute | solution.py:140
  (108 other events, 1494.3 us)
Sparse Core Ops, SparseCore 0:
  20.4 79.1 all-gather.1

commit v4 on v3

--- a/solution.py
+++ b/solution.py
@@ -155,15 +155,14 @@
         bit //= 2
     even = jnp.concatenate(have)
     odd = jnp.concatenate([near] + [hop(piece, 1, n) for piece in have[1:]])
-    rows = jnp.concatenate([even, odd, swap(even, "tp"), swap(odd, "tp")])
-    return rows, have[-1]
+    return [jnp.concatenate([part, swap(part, "tp")]) for part in (even, odd)], have[1]
 
 
 def after(value, *others):
     return lax.optimization_barrier((value, *others))[0]
 
 
-def scatter_blocks(blocks, bit, n, serial=False, gates=()):
+def scatter_blocks(blocks, bit, n, serial=False, gates=None):
     marks = []
     while bit < n:
         keep = len(blocks) // 2
@@ -173,7 +172,7 @@
         for at, k in enumerate(order):
             piece = blocks[keep + k].astype(b16)
             if serial and bit == 1 and at:
-                piece = after(piece, came[order[at - 1]], *(gates if at == 1 else ()))
+                piece = after(piece, came[order[at - 1]], *gates.get(at, ()))
             came[k] = hop(piece, bit, n)
             if serial and bit == 1 and at == 1:
                 marks[0] = came[k]
@@ -183,11 +182,9 @@
 
 
 def scatter_rows(product, sources, n):
-    most = sources[0].shape[0] // 2
-    half = most // 2
-    rows = most // n
-    ends = [(0, half), (half, most), (most, most + half), (most + half, 2 * most)]
-    take = lambda k: product(*[source[ends[k][0] : ends[k][1]] for source in sources])
+    half = sources[0].shape[0] // 2
+    rows = 2 * half // n
+    take = lambda k: product(sources[k % 2][k // 2 * half : (k // 2 + 1) * half])
     far = [swap(take(k).astype(b16), "tp") for k in (3, 2)]
     odd = take(1) + far[0].astype(f32)
     even = take(0) + far[1].astype(f32)
@@ -363,22 +360,24 @@
     down_other = swap(after(down_half, gu_other), "ctx")
     gu_full = both_halves(gu_half, gu_other)
     down_full = both_halves(down_half, down_other)
-    gate_and_up = dot(normed_ffn, gu_full, ((1,), (0,)))
-    gate_act, up_act = gate_and_up[:, :window], gate_and_up[:, window:]
-    hidden = jnp.where(valid, glu_apply(gate_act, up_act), 0.0).astype(b16)
-    ffn_out, _ = scatter_rows(lambda part: dot(part, down_full, ((1,), (1,))), [hidden], n)
+    gates_and_ups = [dot(part, gu_full, ((1,), (0,))) for part in normed_ffn]
+    acts = [(part[:, :window], part[:, window:]) for part in gates_and_ups]
+    hidden = [jnp.where(valid, glu_apply(*pair), 0.0).astype(b16) for pair in acts]
+    ffn_out, _ = scatter_rows(lambda part: dot(part, down_full, ((1,), (1,))), hidden, n)
     block_own = (middle + rms_scale(ffn_out, gains[3])).astype(b16)
     block_out = natural(block_own, swap(block_own, "tp"), tp, 0)
 
     d_out = lax.dynamic_slice_in_dim(cotangent, tp * rows, rows).astype(f32)
     d_ffn_raw, gain_four_term = norm_back(ffn_out, gains[3], d_out)
     d_ffn_out, _ = gather_rows(d_ffn_raw.astype(b16), n)
-    d_hidden = dot(d_ffn_out, down_full, ((1,), (0,)))
-    d_pair = jax.vjp(glu_apply, gate_act, up_act)[1](d_hidden)
-    d_gate, d_up = [jnp.where(valid, part, 0.0).astype(b16) for part in d_pair]
+    d_pairs = [
+        jax.vjp(glu_apply, *pair)[1](dot(part, down_full, ((1,), (0,))))
+        for pair, part in zip(acts, d_ffn_out)
+    ]
+    d_pairs = [[jnp.where(valid, part, 0.0).astype(b16) for part in pair] for pair in d_pairs]
     d_normed_ffn, marks = scatter_rows(
         lambda part: dot(part, gu_full, ((1,), (1,))),
-        [jnp.concatenate([d_gate, d_up], axis=1)],
+        [jnp.concatenate(pair, axis=1) for pair in d_pairs],
         n,
     )
 
@@ -387,7 +386,12 @@
         send = lax.dynamic_index_in_dim(terms, 1 - ctx, 1, keepdims=False).astype(b16)
         return send, lax.dynamic_index_in_dim(terms, ctx, 1, keepdims=False)
 
-    down_send, down_keep = halves(dot(after(d_ffn_out, marks[0]), hidden, ((0,), (0,))))
+    hidden, d_ffn_out, normed_ffn = [
+        jnp.concatenate([after(part, marks[0]) for part in parts])
+        for parts in (hidden, d_ffn_out, normed_ffn)
+    ]
+    d_gate, d_up = [jnp.concatenate(parts) for parts in zip(*d_pairs)]
+    down_send, down_keep = halves(dot(d_ffn_out, hidden, ((0,), (0,))))
     late_normed = after(normed_ffn, marks[-1], down_send)
     gate_send, gate_keep = halves(dot(late_normed, d_gate, ((0,), (0,))))
     up_send, up_keep = halves(dot(after(late_normed, gate_send), d_up, ((0,), (0,))))
@@ -449,6 +453,7 @@
     ).astype(b16)
     tokens_grad = dot(unpick, slot_grad, ((1,), (0,))).astype(b16)
 
+    down_weight_grad = columns_joined(down_rows).T
     attn_terms = [
         dot(normed_attn, d_qkv, ((0,), (0,))).reshape(n, d_rows, -1),
         dot(d_attn_out, attended, ((0,), (0,))).reshape(n, d_rows, -1),
@@ -464,13 +469,12 @@
         1,
         n,
         serial=True,
-        gates=[down_rows],
+        gates={1: [down_rows], 2: [down_weight_grad]},
     )
     gu_rows = after(to_owners([gate_keep, up_keep], [gate_got, up_got], marks[0]), attn_rows)
     gate_rows, up_rows = gu_rows[..., :window], gu_rows[..., window:]
     gate_weight_grad = columns_joined(gate_rows)
     up_weight_grad = columns_joined(up_rows)
-    down_weight_grad = columns_joined(down_rows).T
     attn_rows = attn_rows.reshape(2, d_half, -1)
     attn_own = lax.dynamic_index_in_dim(attn_rows, ctx, 0, keepdims=False)
     attn_other = swap(
@@ -491,7 +495,7 @@
     gain_rows = jnp.stack(
         [lax.dynamic_index_in_dim(gain_terms, me ^ k, 0, keepdims=False) for k in keys_of(n)]
     )
-    gain_rows = after(gain_rows, attn_rows)
+    gain_rows = after(gain_rows, attn_other)
     bit = 1
     while bit < n:
         keep = gain_rows.shape[0] // 2

time: 823 us -> 777 us (0.944)
  waiting for transfers between devices: 423 us -> 342 us
  other arithmetic: 62.1 us -> 82 us
  starting transfers between devices: 97.1 us -> 113 us
    ppermute x45, waiting for transfers between devices: 352 us -> 294 us  [hop(): return lax.ppermute(piece, 'fsdp', [(d, d ^ step) for d in range(n)])]
    ppermute x27, waiting for transfers between devices: 70.7 us -> 47.7 us  [swap(): return lax.ppermute(piece, axis, [(0, 1), (1, 0)])]
    ppermute x45, starting transfers between devices: 58.4 us -> 69.1 us  [hop(): return lax.ppermute(piece, 'fsdp', [(d, d ^ step) for d in range(n)])]
    unnamed x160 -> x222, local copies, waits for them, and re-layouts: 44.7 us -> 39 us
    dot_general x21 -> x23, matrix products: 116 us -> 113 us  [dot(): lax.dot_general(lhs, rhs, (dims, ((), ())), preferred_element_type=f32)]
  transfers between devices with their start and end apart: 77 -> 77, of which waited for: 41 -> 40; matrix products, arithmetic and copies ran while one was open for 27% -> 32% of each run, Pallas kernels for 1% -> 1%
where the time goes in v4:
time: 777 us; the launch traced here: 771 us
  waiting for transfers between devices  342 us (44%)
  starting transfers between devices  113 us (15%)
  matrix products  113 us (15%)
  local copies, waits for them, and re-layouts  99.6 us (13%)
  other arithmetic  82 us (11%)
  between operations  16.9 us (2%)
    ppermute x45, waiting for transfers between devices, hop(): return lax.ppermute(piece, 'fsdp', [(d, d ^ step) for d in range(n)])  294 us
    dot_general x23, matrix products, dot(): lax.dot_general(lhs, rhs, (dims, ((), ())), preferred_element_type=f32)  113 us
    ppermute x45, starting transfers between devices, hop(): return lax.ppermute(piece, 'fsdp', [(d, d ^ step) for d in range(n)])  69.1 us
    ppermute x27, waiting for transfers between devices, swap(): return lax.ppermute(piece, axis, [(0, 1), (1, 0)])  47.7 us
    unnamed x222, local copies, waits for them, and re-layouts  39 us
    ppermute x27, starting transfers between devices, swap(): return lax.ppermute(piece, axis, [(0, 1), (1, 0)])  23 us
  transfers between devices with their start and end apart: 77, of which 40 were waited for; matrix products, arithmetic and copies ran while one was open for 32% of the time, Pallas kernels for 1%

profile of v4, /device:TPU:0, one launch (start us, length us, event | category | flops | bytes accessed | tf_op | source)
XLA Modules:
  0.0 771.1 jit_solution(5309427047355393872)
XLA Ops:
  26.5 6.8 collective-permute-done
  33.4 19.0 %collective-permute-done.2 = bf16[304,1024]{1,0:T(8,128)(2,1)S(1)} collective-permute-done((bf16[304,1024]{1,0:T(8,128)(2,1)S(1)}, bf16[304,1024]{1,0:T(8,128)(2,1)S(1)}, u32[]{:S(2)}, u32[]{:S(2)}) %collective-permute-start.2) | collective-permute-done | bytes 622624 | tf_op jit(solution)/shard_map/ppermute | solution.py:144
  60.2 18.4 %collective-permute-done.4 = bf16[304,1024]{1,0:T(8,128)(2,1)S(1)} collective-permute-done((bf16[304,1024]{1,0:T(8,128)(2,1)S(1)}, bf16[304,1024]{1,0:T(8,128)(2,1)S(1)}, u32[]{:S(2)}, u32[]{:S(2)}) %collective-permute-start.4) | collective-permute-done | bytes 622624 | tf_op jit(solution)/shard_map/ppermute | solution.py:144
  85.6 8.3 %all-to-all-start = ((bf16[8,144,1280]{2,1,0:T(8,128)(2,1)}), bf16[8,144,1280]{2,1,0:T(8,128)(2,1)}, u32[]{:S(2)}, u32[]{:S(2)}) async-start(bf16[8,144,1280]{2,1,0:T(8,128)(2,1)} %fusion.112), calls=%async_computation | async-start | bytes 5898240 | tf_op jit(solution)/shard_map/all_to_all | solution.py:327
  106.5 32.7 %collective-permute-done.8 = bf16[304,1024]{1,0:T(8,128)(2,1)S(1)} collective-permute-done((bf16[304,1024]{1,0:T(8,128)(2,1)}, bf16[304,1024]{1,0:T(8,128)(2,1)S(1)}, u32[]{:S(2)}, u32[]{:S(2)}) %collective-permute-start.8) | collective-permute-done | bytes 622624 | tf_op jit(solution)/shard_map/ppermute | solution.py:144
  160.3 12.2 %collective-permute-done.10 = bf16[112,2304]{1,0:T(8,128)(2,1)S(1)} collective-permute-done((bf16[112,2304]{1,0:T(8,128)(2,1)S(1)}, bf16[112,2304]{1,0:T(8,128)(2,1)S(1)}, u32[]{:S(2)}, u32[]{:S(2)}) %collective-permute-start.10) | collective-permute-done | bytes 516128 | tf_op jit(solution)/shard_map/ppermute | solution.py:140
  191.5 12.0 %collective-permute-done.11 = bf16[112,2304]{1,0:T(8,128)(2,1)} collective-permute-done((bf16[112,2304]{1,0:T(8,128)(2,1)S(1)}, bf16[112,2304]{1,0:T(8,128)(2,1)}, u32[]{:S(2)}, u32[]{:S(2)}) %collective-permute-start.11) | collective-permute-done | bytes 516128 | tf_op jit(solution)/shard_map/ppermute | solution.py:144
  223.4 7.2 collective-permute-done.14
  246.0 9.2 %collective-permute-done.21 = bf16[112,2304]{1,0:T(8,128)(2,1)S(1)} collective-permute-done((bf16[112,2304]{1,0:T(8,128)(2,1)}, bf16[112,2304]{1,0:T(8,128)(2,1)S(1)}, u32[]{:S(2)}, u32[]{:S(2)}) %collective-permute-start.21) | collective-permute-done | bytes 516128 | tf_op jit(solution)/shard_map/ppermute | solution.py:144
  267.4 9.6 %fusion.178 = f32[896,1280]{1,0:T(8,128)S(1)} fusion(bf16[896,2304]{1,0:T(8,128)(2,1)S(1)} %constant_dynamic-update-slice_fusion, bf16[2304,1280]{1,0:T(8,128)(2,1)} %bitcast.35), kind=kOutput, calls=%fused_computation.426 | convolution fusion | flops 5284823040 | bytes 14614528 | tf_op jit(solution)/shard_map/dot_general | solution.py:136
  281.8 9.0 %fusion.179 = f32[896,1280]{1,0:T(8,128)S(1)} fusion(bf16[896,2304]{1,0:T(8,128)(2,1)} %constant_dynamic-update-slice_fusion.5, bf16[2304,1280]{1,0:T(8,128)(2,1)} %bitcast.35), kind=kOutput, calls=%fused_computation.427 | convolution fusion | flops 5284823040 | bytes 14614528 | tf_op jit(solution)/shard_map/dot_general | solution.py:136
  311.7 9.1 %collective-permute-done.25 = bf16[112,2304]{1,0:T(8,128)(2,1)S(1)} collective-permute-done((bf16[112,2304]{1,0:T(8,128)(2,1)S(1)}, bf16[112,2304]{1,0:T(8,128)(2,1)S(1)}, u32[]{:S(2)}, u32[]{:S(2)}) %collective-permute-start.25) | collective-permute-done | bytes 516128 | tf_op jit(solution)/shard_map/ppermute | solution.py:144
  320.8 11.1 %collective-permute-done.28 = bf16[112,2304]{1,0:T(8,128)(2,1)S(1)} collective-permute-done((bf16[112,2304]{1,0:T(8,128)(2,1)S(1)}, bf16[112,2304]{1,0:T(8,128)(2,1)S(1)}, u32[]{:S(2)}, u32[]{:S(2)}) %collective-permute-start.28) | collective-permute-done | bytes 516128 | tf_op jit(solution)/shard_map/ppermute | solution.py:144
  342.9 10.1 %collective-permute-done.29 = bf16[112,2304]{1,0:T(8,128)(2,1)S(1)} collective-permute-done((bf16[112,2304]{1,0:T(8,128)(2,1)S(1)}, bf16[112,2304]{1,0:T(8,128)(2,1)S(1)}, u32[]{:S(2)}, u32[]{:S(2)}) %collective-permute-start.29) | collective-permute-done | bytes 516128 | tf_op jit(solution)/shard_map/ppermute | solution.py:144
  354.8 8.3 %collective-permute-done.26 = bf16[112,2304]{1,0:T(8,128)(2,1)} collective-permute-done((bf16[112,2304]{1,0:T(8,128)(2,1)}, bf16[112,2304]{1,0:T(8,128)(2,1)}, u32[]{:S(2)}, u32[]{:S(2)}) %collective-permute-start.26) | collective-permute-done | bytes 516128 | tf_op jit(solution)/shard_map/ppermute | solution.py:144
  363.1 17.4 %collective-permute-done.30 = bf16[112,2304]{1,0:T(8,128)(2,1)} collective-permute-done((bf16[112,2304]{1,0:T(8,128)(2,1)S(1)}, bf16[112,2304]{1,0:T(8,128)(2,1)}, u32[]{:S(2)}, u32[]{:S(2)}) %collective-permute-start.30) | collective-permute-done | bytes 516128 | tf_op jit(solution)/shard_map/ppermute | solution.py:144
  387.4 11.8 %collective-permute-done.32 = bf16[112,2304]{1,0:T(8,128)(2,1)S(1)} collective-permute-done((bf16[112,2304]{1,0:T(8,128)(2,1)S(1)}, bf16[112,2304]{1,0:T(8,128)(2,1)S(1)}, u32[]{:S(2)}, u32[]{:S(2)}) %collective-permute-start.32) | collective-permute-done | bytes 516128 | tf_op jit(solution)/shard_map/ppermute | solution.py:144
  410.7 9.5 %collective-permute-done.39 = bf16[112,2304]{1,0:T(8,128)(2,1)S(1)} collective-permute-done((bf16[112,2304]{1,0:T(8,128)(2,1)S(1)}, bf16[112,2304]{1,0:T(8,128)(2,1)S(1)}, u32[]{:S(2)}, u32[]{:S(2)}) %collective-permute-start.39) | collective-permute-done | bytes 516128 | tf_op jit(solution)/shard_map/ppermute | solution.py:144
  420.2 7.0 collective-permute-done.40
  433.2 8.8 %fusion.17 = (bf16[896,640]{1,0:T(8,128)(2,1)}, bf16[896,640]{1,0:T(8,128)(2,1)S(1)}, bf16[896,640]{1,0:T(8,128)(2,1)S(1)}, bf16[896,640]{1,0:T(8,128)(2,1)}) fusion(f32[896,1280]{1,0:T(8,128)S(1)} %bitcast.331, pred[640]{0:T(1024)(128)(4,1)S(1)} %fusion.137, f32[896,640]{1,0:T(8,128)S(1)} %fusion.180, f32[896,1280]{1,0:T(8,128)S(1)} %bitcast.329, ...), kind=kOutput, calls=%fused_computation.49 | convolution fusion | flops 2676817920 | bytes 23134848 | tf_op jit(solution)/shard_map/dot_general | solution.py:136
  449.2 6.6 convolution_convert_fusion.1
  466.9 7.1 fusion
  489.6 7.7 %pad_maximum_fusion = bf16[1792,2304]{1,0:T(8,128)(2,1)} fusion(bf16[896,2304]{1,0:T(8,128)(2,1)} %constant_dynamic-update-slice_fusion.5, bf16[896,2304]{1,0:T(8,128)(2,1)} %copy-done.12), kind=kLoop, calls=%fused_computation.4 | loop fusion | flops 16515072 | bytes 16515072 | tf_op jit(solution)/shard_map/concatenate | solution.py:390
  507.4 9.5 %fusion.25 = f32[2304,640]{1,0:T(8,128)S(1)} fusion(bf16[1792,2304]{1,0:T(8,128)(2,1)} %pad_maximum_fusion, bf16[896,640]{1,0:T(8,128)(2,1)S(1)} %copy-done.82, bf16[896,640]{1,0:T(8,128)(2,1)S(1)} %copy-done.78), kind=kOutput, calls=%fused_computation.61 | convolution fusion | flops 5289410560 | bytes 16449536 | tf_op jit(solution)/shard_map/dot_general | solution.py:136
  520.2 7.0 fusion.29
  536.2 7.7 collective-permute-done.51
  582.7 17.0 %collective-permute-done.57 = bf16[288,1536]{1,0:T(8,128)(2,1)S(1)} collective-permute-done((bf16[288,1536]{1,0:T(8,128)(2,1)S(1)}, bf16[288,1536]{1,0:T(8,128)(2,1)S(1)}, u32[]{:S(2)}, u32[]{:S(2)}) %collective-permute-start.57) | collective-permute-done | bytes 884768 | tf_op jit(solution)/shard_map/ppermute | solution.py:144
  607.8 15.5 %collective-permute-done.62 = bf16[288,1536]{1,0:T(8,128)(2,1)} collective-permute-done((bf16[288,1536]{1,0:T(8,128)(2,1)}, bf16[288,1536]{1,0:T(8,128)(2,1)}, u32[]{:S(2)}, u32[]{:S(2)}) %collective-permute-start.62) | collective-permute-done | bytes 884768 | tf_op jit(solution)/shard_map/ppermute | solution.py:144
  675.2 24.5 %collective-permute-done.63 = bf16[288,1536]{1,0:T(8,128)(2,1)} collective-permute-done((bf16[288,1536]{1,0:T(8,128)(2,1)}, bf16[288,1536]{1,0:T(8,128)(2,1)}, u32[]{:S(2)}, u32[]{:S(2)}) %collective-permute-start.63) | collective-permute-done | bytes 884768 | tf_op jit(solution)/shard_map/ppermute | solution.py:144
  699.8 14.9 %collective-permute-done.61 = bf16[288,1536]{1,0:T(8,128)(2,1)} collective-permute-done((bf16[288,1536]{1,0:T(8,128)(2,1)}, bf16[288,1536]{1,0:T(8,128)(2,1)}, u32[]{:S(2)}, u32[]{:S(2)}) %collective-permute-start.61) | collective-permute-done | bytes 884768 | tf_op jit(solution)/shard_map/ppermute | solution.py:144
  721.7 7.6 collective-permute-done.64
  730.1 7.9 %collective-permute-start.69 = (f32[4,4,144]{2,0,1:T(4,128)S(1)}, f32[4,4,144]{2,0,1:T(4,128)S(1)}, u32[]{:S(2)}, u32[]{:S(2)}) collective-permute-start(f32[4,4,144]{2,0,1:T(4,128)S(1)} %slice.507), channel_id=1, source_target_pairs={{0,4},{4,0},{8,12},{12,8},{16,20},{20,16},{24,28},{28,24},{1,5},{5... | collective-permute-start | bytes 27656 | tf_op jit(solution)/shard_map/ppermute | solution.py:144
  (547 shorter events, 383.4 us)
Async XLA Ops:
  7.2 142.6 %all-gather.2.cloned.1.call-start = ((), (), s32[]{:S(2)}) async-start(), calls=%async_computation.4 | async-start | bytes 2654208 | tf_op jit(solution)/shard_map/all_gather | solution.py:303
  11.3 41.1 %collective-permute-start.2 = (bf16[304,1024]{1,0:T(8,128)(2,1)S(1)}, bf16[304,1024]{1,0:T(8,128)(2,1)S(1)}, u32[]{:S(2)}, u32[]{:S(2)}) collective-permute-start(bf16[304,1024]{1,0:T(8,128)(2,1)S(1)} %pad_maximum_fusion.23), channel_id=1, source_target_pairs={{0,16},{4,20},{8,24},{12,28},{16,0},{20,4},{24,8},{28,12},{1,17},{... | collective-permute-start | bytes 1867784 | tf_op jit(solution)/shard_map/ppermute | solution.py:144
  15.4 39.1 %collective-permute-start.3 = (bf16[304,1024]{1,0:T(8,128)(2,1)S(1)}, bf16[304,1024]{1,0:T(8,128)(2,1)S(1)}, u32[]{:S(2)}, u32[]{:S(2)}) collective-permute-start(bf16[304,1024]{1,0:T(8,128)(2,1)S(1)} %pad_maximum_fusion.23), channel_id=1, source_target_pairs={{0,8},{4,12},{8,0},{12,4},{16,24},{20,28},{24,16},{28,20},{1,9},{5... | collective-permute-start | bytes 1867784 | tf_op jit(solution)/shard_map/ppermute | solution.py:144
  17.0 79.8 %collective-permute-start.5 = (bf16[304,1024]{1,0:T(8,128)(2,1)S(1)}, bf16[304,1024]{1,0:T(8,128)(2,1)S(1)}, u32[]{:S(2)}, u32[]{:S(2)}) collective-permute-start(bf16[304,1024]{1,0:T(8,128)(2,1)S(1)} %pad_maximum_fusion.23), channel_id=1, source_target_pairs={{0,4},{4,0},{8,12},{12,8},{16,20},{20,16},{24,28},{28,24},{1,5},{5... | collective-permute-start | bytes 1867784 | tf_op jit(solution)/shard_map/ppermute | solution.py:144
  53.0 43.8 %collective-permute-start.6 = (bf16[304,1024]{1,0:T(8,128)(2,1)S(1)}, bf16[304,1024]{1,0:T(8,128)(2,1)}, u32[]{:S(2)}, u32[]{:S(2)}) collective-permute-start(bf16[304,1024]{1,0:T(8,128)(2,1)S(1)} %collective-permute-done.2), channel_id=1, source_target_pairs={{0,4},{4,0},{8,12},{12,8},{16,20},{20,16},{24,28},{28,24},{1,5},{5... | collective-permute-start | bytes 1867784 | tf_op jit(solution)/shard_map/ppermute | solution.py:144
  54.5 47.4 %collective-permute-start.7 = (bf16[304,1024]{1,0:T(8,128)(2,1)S(1)}, bf16[304,1024]{1,0:T(8,128)(2,1)}, u32[]{:S(2)}, u32[]{:S(2)}) collective-permute-start(bf16[304,1024]{1,0:T(8,128)(2,1)S(1)} %collective-permute-done.3), channel_id=1, source_target_pairs={{0,4},{4,0},{8,12},{12,8},{16,20},{20,16},{24,28},{28,24},{1,5},{5... | collective-permute-start | bytes 1867784 | tf_op jit(solution)/shard_map/ppermute | solution.py:144
  85.6 97.6 %all-to-all-start = ((bf16[8,144,1280]{2,1,0:T(8,128)(2,1)}), bf16[8,144,1280]{2,1,0:T(8,128)(2,1)}, u32[]{:S(2)}, u32[]{:S(2)}) async-start(bf16[8,144,1280]{2,1,0:T(8,128)(2,1)} %fusion.112), calls=%async_computation | async-start | bytes 5898240 | tf_op jit(solution)/shard_map/all_to_all | solution.py:327
  93.9 45.3 %collective-permute-start.8 = (bf16[304,1024]{1,0:T(8,128)(2,1)}, bf16[304,1024]{1,0:T(8,128)(2,1)S(1)}, u32[]{:S(2)}, u32[]{:S(2)}) collective-permute-start(bf16[304,1024]{1,0:T(8,128)(2,1)} %copy-done.40), channel_id=1, source_target_pairs={{0,4},{4,0},{8,12},{12,8},{16,20},{20,16},{24,28},{28,24},{1,5},{5... | collective-permute-start | bytes 1867784 | tf_op jit(solution)/shard_map/ppermute | solution.py:144
  190.0 29.5 %collective-permute-start.13 = (bf16[112,2304]{1,0:T(8,128)(2,1)S(1)}, bf16[112,2304]{1,0:T(8,128)(2,1)}, u32[]{:S(2)}, u32[]{:S(2)}) collective-permute-start(bf16[112,2304]{1,0:T(8,128)(2,1)S(1)} %get-tuple-element.90), channel_id=1, source_target_pairs={{0,8},{4,12},{8,0},{12,4},{16,24},{20,28},{24,16},{28,20},{1,9},{5... | collective-permute-start | bytes 1548296 | tf_op jit(solution)/shard_map/ppermute | solution.py:144
  190.0 68.7 %collective-permute-start.16 = (bf16[8,144,1280]{2,1,0:T(8,128)(2,1)}, bf16[8,144,1280]{2,1,0:T(8,128)(2,1)}, u32[]{:S(2)}, u32[]{:S(2)}) collective-permute-start(bf16[8,144,1280]{2,1,0:T(8,128)(2,1)} %all-to-all-done), channel_id=1, source_target_pairs={{0,2},{2,0},{1,3},{3,1},{4,6},{6,4},{5,7},{7,5},{8,10},{10,8},{9,1... | collective-permute-start | bytes 8847368 | tf_op jit(solution)/shard_map/ppermute | solution.py:140
  203.4 34.4 %collective-permute-start.19 = (bf16[112,2304]{1,0:T(8,128)(2,1)}, bf16[112,2304]{1,0:T(8,128)(2,1)}, u32[]{:S(2)}, u32[]{:S(2)}) collective-permute-start(bf16[112,2304]{1,0:T(8,128)(2,1)} %collective-permute-done.11), channel_id=1, source_target_pairs={{0,4},{4,0},{8,12},{12,8},{16,20},{20,16},{24,28},{28,24},{1,5},{5... | collective-permute-start | bytes 1548296 | tf_op jit(solution)/shard_map/ppermute | solution.py:144
  210.4 51.9 %all-to-all-start.1 = ((bf16[8,144,640]{2,1,0:T(8,128)(2,1)}), bf16[8,144,640]{2,1,0:T(8,128)(2,1)}, u32[]{:S(2)}, u32[]{:S(2)}) async-start(bf16[8,144,640]{2,1,0:T(8,128)(2,1)} %fusion.122), calls=%async_computation.1 | async-start | bytes 2949120 | tf_op jit(solution)/shard_map/all_to_all | solution.py:327
  233.4 32.3 %collective-permute-start.15 = (bf16[448,2304]{1,0:T(8,128)(2,1)}, bf16[448,2304]{1,0:T(8,128)(2,1)}, u32[]{:S(2)}, u32[]{:S(2)}) collective-permute-start(bf16[448,2304]{1,0:T(8,128)(2,1)} %pad_maximum_fusion.6), channel_id=1, source_target_pairs={{0,1},{1,0},{2,3},{3,2},{4,5},{5,4},{6,7},{7,6},{8,9},{9,8},{10,11... | collective-permute-start | bytes 6193160 | tf_op jit(solution)/shard_map/ppermute | solution.py:140
  262.3 34.9 %collective-permute-start.17 = (bf16[8,144,640]{2,1,0:T(8,128)(2,1)}, bf16[8,144,640]{2,1,0:T(8,128)(2,1)S(1)}, u32[]{:S(2)}, u32[]{:S(2)}) collective-permute-start(bf16[8,144,640]{2,1,0:T(8,128)(2,1)} %all-to-all-done.1), channel_id=1, source_target_pairs={{0,2},{2,0},{1,3},{3,1},{4,6},{6,4},{5,7},{7,5},{8,10},{10,8},{9,1... | collective-permute-start | bytes 4423688 | tf_op jit(solution)/shard_map/ppermute | solution.py:140
  308.3 34.7 %collective-permute-start.27 = (bf16[112,2304]{1,0:T(8,128)(2,1)S(1)}, bf16[112,2304]{1,0:T(8,128)(2,1)S(1)}, u32[]{:S(2)}, u32[]{:S(2)}) collective-permute-start(bf16[112,2304]{1,0:T(8,128)(2,1)S(1)} %get-tuple-element.150), channel_id=1, source_target_pairs={{0,4},{4,0},{8,12},{12,8},{16,20},{20,16},{24,28},{28,24},{1,5},{5... | collective-permute-start | bytes 1548296 | tf_op jit(solution)/shard_map/ppermute | solution.py:144
  335.0 28.2 %collective-permute-start.26 = (bf16[112,2304]{1,0:T(8,128)(2,1)}, bf16[112,2304]{1,0:T(8,128)(2,1)}, u32[]{:S(2)}, u32[]{:S(2)}) collective-permute-start(bf16[112,2304]{1,0:T(8,128)(2,1)} %get-tuple-element.122), channel_id=1, source_target_pairs={{0,8},{4,12},{8,0},{12,4},{16,24},{20,28},{24,16},{28,20},{1,9},{5... | collective-permute-start | bytes 1548296 | tf_op jit(solution)/shard_map/ppermute | solution.py:144
  353.3 27.3 %collective-permute-start.30 = (bf16[112,2304]{1,0:T(8,128)(2,1)S(1)}, bf16[112,2304]{1,0:T(8,128)(2,1)}, u32[]{:S(2)}, u32[]{:S(2)}) collective-permute-start(bf16[112,2304]{1,0:T(8,128)(2,1)S(1)} %fusion.78), channel_id=1, source_target_pairs={{0,16},{4,20},{8,24},{12,28},{16,0},{20,4},{24,8},{28,12},{1,17},{... | collective-permute-start | bytes 1548296 | tf_op jit(solution)/shard_map/ppermute | solution.py:144
  464.8 34.7 %collective-permute-start.46 = (bf16[112,2304]{1,0:T(8,128)(2,1)}, bf16[112,2304]{1,0:T(8,128)(2,1)}, u32[]{:S(2)}, u32[]{:S(2)}) collective-permute-start(bf16[112,2304]{1,0:T(8,128)(2,1)} %get-tuple-element.145), channel_id=1, source_target_pairs={{0,4},{4,0},{8,12},{12,8},{16,20},{20,16},{24,28},{28,24},{1,5},{5... | collective-permute-start | bytes 1548296 | tf_op jit(solution)/shard_map/ppermute | solution.py:144
  465.3 63.4 %collective-permute-start.43 = (bf16[112,2304]{1,0:T(8,128)(2,1)}, bf16[112,2304]{1,0:T(8,128)(2,1)}, u32[]{:S(2)}, u32[]{:S(2)}) collective-permute-start(bf16[112,2304]{1,0:T(8,128)(2,1)} %get-tuple-element.144), channel_id=1, source_target_pairs={{0,4},{4,0},{8,12},{12,8},{16,20},{20,16},{24,28},{28,24},{1,5},{5... | collective-permute-start | bytes 1548296 | tf_op jit(solution)/shard_map/ppermute | solution.py:144
  477.0 54.8 %collective-permute-start.50 = (bf16[8,144,640]{2,1,0:T(8,128)(2,1)}, bf16[8,144,640]{2,1,0:T(8,128)(2,1)}, u32[]{:S(2)}, u32[]{:S(2)}) collective-permute-start(bf16[8,144,640]{2,1,0:T(8,128)(2,1)} %fusion.52), channel_id=1, source_target_pairs={{0,2},{2,0},{1,3},{3,1},{4,6},{6,4},{5,7},{7,5},{8,10},{10,8},{9,1... | collective-permute-start | bytes 4423688 | tf_op jit(solution)/shard_map/ppermute | solution.py:140
  497.3 31.3 %collective-permute-start.45 = (bf16[112,2304]{1,0:T(8,128)(2,1)}, bf16[112,2304]{1,0:T(8,128)(2,1)S(1)}, u32[]{:S(2)}, u32[]{:S(2)}) collective-permute-start(bf16[112,2304]{1,0:T(8,128)(2,1)} %get-tuple-element.120), channel_id=1, source_target_pairs={{0,8},{4,12},{8,0},{12,4},{16,24},{20,28},{24,16},{28,20},{1,9},{5... | collective-permute-start | bytes 1548296 | tf_op jit(solution)/shard_map/ppermute | solution.py:144
  546.1 85.3 %collective-permute-start.65 = (bf16[8,144,640]{2,1,0:T(8,128)(2,1)}, bf16[8,144,640]{2,1,0:T(8,128)(2,1)}, u32[]{:S(2)}, u32[]{:S(2)}) collective-permute-start(bf16[8,144,640]{2,1,0:T(8,128)(2,1)} %fusion.53), channel_id=1, source_target_pairs={{0,2},{2,0},{1,3},{3,1},{4,6},{6,4},{5,7},{7,5},{8,10},{10,8},{9,1... | collective-permute-start | bytes 4423688 | tf_op jit(solution)/shard_map/ppermute | solution.py:140
  547.6 83.8 %collective-permute-start.66 = (bf16[8,144,640]{2,1,0:T(8,128)(2,1)}, bf16[8,144,640]{2,1,0:T(8,128)(2,1)}, u32[]{:S(2)}, u32[]{:S(2)}) collective-permute-start(bf16[8,144,640]{2,1,0:T(8,128)(2,1)} %fusion.54), channel_id=1, source_target_pairs={{0,2},{2,0},{1,3},{3,1},{4,6},{6,4},{5,7},{7,5},{8,10},{10,8},{9,1... | collective-permute-start | bytes 4423688 | tf_op jit(solution)/shard_map/ppermute | solution.py:140
  551.8 51.3 %all-to-all-start.2 = ((bf16[8,144,640]{2,1,0:T(8,128)(2,1)}), bf16[8,144,640]{2,1,0:T(8,128)(2,1)S(1)}, u32[]{:S(2)}, u32[]{:S(2)}) async-start(bf16[8,144,640]{2,1,0:T(8,128)(2,1)} %fusion.7), calls=%async_computation.2 | async-start | bytes 2949120 | tf_op jit(solution)/shard_map/all_to_all | solution.py:403
  569.1 64.1 %collective-permute-start.53 = (f32[224,2304]{1,0:T(8,128)}, f32[224,2304]{1,0:T(8,128)}, u32[]{:S(2)}, u32[]{:S(2)}) collective-permute-start(f32[224,2304]{1,0:T(8,128)} %pad_maximum_fusion.11), channel_id=1, source_target_pairs={{0,1},{1,0},{2,3},{3,2},{4,5},{5,4},{6,7},{7,6},{8,9},{9,8},{10,11... | collective-permute-start | bytes 6193160 | tf_op jit(solution)/shard_map/ppermute | solution.py:140
  627.3 72.5 %collective-permute-start.63 = (bf16[288,1536]{1,0:T(8,128)(2,1)}, bf16[288,1536]{1,0:T(8,128)(2,1)}, u32[]{:S(2)}, u32[]{:S(2)}) collective-permute-start(bf16[288,1536]{1,0:T(8,128)(2,1)} %fusion.50), channel_id=1, source_target_pairs={{0,16},{4,20},{8,24},{12,28},{16,0},{20,4},{24,8},{28,12},{1,17},{... | collective-permute-start | bytes 2654216 | tf_op jit(solution)/shard_map/ppermute | solution.py:144
  629.7 27.8 %collective-permute-start.59 = (bf16[288,1536]{1,0:T(8,128)(2,1)}, bf16[288,1536]{1,0:T(8,128)(2,1)}, u32[]{:S(2)}, u32[]{:S(2)}) collective-permute-start(bf16[288,1536]{1,0:T(8,128)(2,1)} %pad_maximum_fusion.20), channel_id=1, source_target_pairs={{0,4},{4,0},{8,12},{12,8},{16,20},{20,16},{24,28},{28,24},{1,5},{5... | collective-permute-start | bytes 2654216 | tf_op jit(solution)/shard_map/ppermute | solution.py:144
  640.7 114.3 %all-to-all-start.3 = ((bf16[8,144,1280]{2,1,0:T(8,128)(2,1)}), bf16[8,144,1280]{2,1,0:T(8,128)(2,1)S(1)}, u32[]{:S(2)}, u32[]{:S(2)}) async-start(bf16[8,144,1280]{2,1,0:T(8,128)(2,1)} %pad_maximum_fusion.1), calls=%async_computation.3 | async-start | bytes 5898240 | tf_op jit(solution)/shard_map/all_to_all | solution.py:403
  659.8 54.9 %collective-permute-start.61 = (bf16[288,1536]{1,0:T(8,128)(2,1)}, bf16[288,1536]{1,0:T(8,128)(2,1)}, u32[]{:S(2)}, u32[]{:S(2)}) collective-permute-start(bf16[288,1536]{1,0:T(8,128)(2,1)} %fusion.48), channel_id=1, source_target_pairs={{0,8},{4,12},{8,0},{12,4},{16,24},{20,28},{24,16},{28,20},{1,9},{5... | collective-permute-start | bytes 2654216 | tf_op jit(solution)/shard_map/ppermute | solution.py:144
  663.9 50.8 %collective-permute-start.60 = (bf16[288,1536]{1,0:T(8,128)(2,1)}, bf16[288,1536]{1,0:T(8,128)(2,1)}, u32[]{:S(2)}, u32[]{:S(2)}) collective-permute-start(bf16[288,1536]{1,0:T(8,128)(2,1)} %pad_maximum_fusion.19), channel_id=1, source_target_pairs={{0,4},{4,0},{8,12},{12,8},{16,20},{20,16},{24,28},{28,24},{1,5},{5... | collective-permute-start | bytes 2654216 | tf_op jit(solution)/shard_map/ppermute | solution.py:144
  667.2 53.2 %collective-permute-start.68 = (f32[8,4,144]{2,0,1:T(8,128)S(1)}, f32[8,4,144]{2,0,1:T(8,128)S(1)}, u32[]{:S(2)}, u32[]{:S(2)}) collective-permute-start(f32[8,4,144]{2,0,1:T(8,128)S(1)} %bitcast.364), channel_id=1, source_target_pairs={{0,2},{2,0},{1,3},{3,1},{4,6},{6,4},{5,7},{7,5},{8,10},{10,8},{9,1... | collective-permute-start | bytes 55304 | tf_op jit(solution)/shard_map/ppermute | solution.py:140
  675.2 65.8 %collective-permute-start.56 = (bf16[224,2304]{1,0:T(8,128)(2,1)}, bf16[224,2304]{1,0:T(8,128)(2,1)}, u32[]{:S(2)}, u32[]{:S(2)}) collective-permute-start(bf16[224,2304]{1,0:T(8,128)(2,1)} %pad_maximum_fusion.18), channel_id=1, source_target_pairs={{0,1},{1,0},{2,3},{3,2},{4,5},{5,4},{6,7},{7,6},{8,9},{9,8},{10,11... | collective-permute-start | bytes 3096584 | tf_op jit(solution)/shard_map/ppermute | solution.py:140
  (140 other events, 1601.9 us)
Sparse Core Ops, SparseCore 0:
  23.7 70.2 all-gather.1

commit v5 on v4

--- a/solution.py
+++ b/solution.py
@@ -480,6 +480,7 @@
     attn_other = swap(
         lax.dynamic_index_in_dim(attn_rows, 1 - ctx, 0, keepdims=False).astype(b16), "ctx"
     )
+    attn_other = after(attn_other, gate_weight_grad, up_weight_grad)
     edges = [0, q_cols, q_cols + k_cols, q_cols + 2 * k_cols, 2 * q_cols + 2 * k_cols]
     attn_grads = [
         natural(attn_own[:, a:b].astype(f32), attn_other[:, a:b].astype(f32), ctx, 1)
@@ -495,7 +496,7 @@
     gain_rows = jnp.stack(
         [lax.dynamic_index_in_dim(gain_terms, me ^ k, 0, keepdims=False) for k in keys_of(n)]
     )
-    gain_rows = after(gain_rows, attn_other)
+    gain_rows = after(gain_rows, attn_rows)
     bit = 1
     while bit < n:
         keep = gain_rows.shape[0] // 2

time: 777 us -> 768 us (0.988)
  waiting for transfers between devices: 342 us -> 333 us
    unnamed x222 -> x216, local copies, waits for them, and re-layouts: 39 us -> 37.1 us
  transfers between devices with their start and end apart: 77 -> 77, of which waited for: 40 -> 41; matrix products, arithmetic and copies ran while one was open for 32% -> 33% of each run, Pallas kernels for 1% -> 1%
where the time goes in v5:
time: 768 us; the launch traced here: 762 us
  waiting for transfers between devices  333 us (43%)
  starting transfers between devices  113 us (15%)
  matrix products  113 us (15%)
  local copies, waits for them, and re-layouts  98.4 us (13%)
  other arithmetic  83.3 us (11%)
  between operations  16.9 us (2%)
    ppermute x45, waiting for transfers between devices, hop(): return lax.ppermute(piece, 'fsdp', [(d, d ^ step) for d in range(n)])  292 us
    dot_general x23, matrix products, dot(): lax.dot_general(lhs, rhs, (dims, ((), ())), preferred_element_type=f32)  113 us
    ppermute x45, starting transfers between devices, hop(): return lax.ppermute(piece, 'fsdp', [(d, d ^ step) for d in range(n)])  69.7 us
    ppermute x27, waiting for transfers between devices, swap(): return lax.ppermute(piece, axis, [(0, 1), (1, 0)])  41 us
    unnamed x216, local copies, waits for them, and re-layouts  37.1 us
    ppermute x27, starting transfers between devices, swap(): return lax.ppermute(piece, axis, [(0, 1), (1, 0)])  21.9 us
  transfers between devices with their start and end apart: 77, of which 41 were waited for; matrix products, arithmetic and copies ran while one was open for 33% of the time, Pallas kernels for 1%

profile of v5, /device:TPU:0, one launch (start us, length us, event | category | flops | bytes accessed | tf_op | source)
XLA Modules:
  0.0 761.6 jit_solution(6495874831143927806)
XLA Ops:
  26.5 6.8 collective-permute-done
  33.4 19.0 %collective-permute-done.2 = bf16[304,1024]{1,0:T(8,128)(2,1)S(1)} collective-permute-done((bf16[304,1024]{1,0:T(8,128)(2,1)S(1)}, bf16[304,1024]{1,0:T(8,128)(2,1)S(1)}, u32[]{:S(2)}, u32[]{:S(2)}) %collective-permute-start.2) | collective-permute-done | bytes 622624 | tf_op jit(solution)/shard_map/ppermute | solution.py:144
  60.2 18.4 %collective-permute-done.4 = bf16[304,1024]{1,0:T(8,128)(2,1)S(1)} collective-permute-done((bf16[304,1024]{1,0:T(8,128)(2,1)S(1)}, bf16[304,1024]{1,0:T(8,128)(2,1)S(1)}, u32[]{:S(2)}, u32[]{:S(2)}) %collective-permute-start.4) | collective-permute-done | bytes 622624 | tf_op jit(solution)/shard_map/ppermute | solution.py:144
  85.7 8.3 %all-to-all-start = ((bf16[8,144,1280]{2,1,0:T(8,128)(2,1)}), bf16[8,144,1280]{2,1,0:T(8,128)(2,1)}, u32[]{:S(2)}, u32[]{:S(2)}) async-start(bf16[8,144,1280]{2,1,0:T(8,128)(2,1)} %fusion.112), calls=%async_computation | async-start | bytes 5898240 | tf_op jit(solution)/shard_map/all_to_all | solution.py:327
  106.5 32.7 %collective-permute-done.8 = bf16[304,1024]{1,0:T(8,128)(2,1)S(1)} collective-permute-done((bf16[304,1024]{1,0:T(8,128)(2,1)}, bf16[304,1024]{1,0:T(8,128)(2,1)S(1)}, u32[]{:S(2)}, u32[]{:S(2)}) %collective-permute-start.8) | collective-permute-done | bytes 622624 | tf_op jit(solution)/shard_map/ppermute | solution.py:144
  160.3 12.2 %collective-permute-done.10 = bf16[112,2304]{1,0:T(8,128)(2,1)S(1)} collective-permute-done((bf16[112,2304]{1,0:T(8,128)(2,1)S(1)}, bf16[112,2304]{1,0:T(8,128)(2,1)S(1)}, u32[]{:S(2)}, u32[]{:S(2)}) %collective-permute-start.10) | collective-permute-done | bytes 516128 | tf_op jit(solution)/shard_map/ppermute | solution.py:140
  191.6 12.0 %collective-permute-done.11 = bf16[112,2304]{1,0:T(8,128)(2,1)} collective-permute-done((bf16[112,2304]{1,0:T(8,128)(2,1)S(1)}, bf16[112,2304]{1,0:T(8,128)(2,1)}, u32[]{:S(2)}, u32[]{:S(2)}) %collective-permute-start.11) | collective-permute-done | bytes 516128 | tf_op jit(solution)/shard_map/ppermute | solution.py:144
  223.5 7.3 collective-permute-done.14
  246.0 9.3 %collective-permute-done.21 = bf16[112,2304]{1,0:T(8,128)(2,1)S(1)} collective-permute-done((bf16[112,2304]{1,0:T(8,128)(2,1)}, bf16[112,2304]{1,0:T(8,128)(2,1)S(1)}, u32[]{:S(2)}, u32[]{:S(2)}) %collective-permute-start.21) | collective-permute-done | bytes 516128 | tf_op jit(solution)/shard_map/ppermute | solution.py:144
  267.5 9.6 %fusion.178 = f32[896,1280]{1,0:T(8,128)S(1)} fusion(bf16[896,2304]{1,0:T(8,128)(2,1)S(1)} %constant_dynamic-update-slice_fusion, bf16[2304,1280]{1,0:T(8,128)(2,1)} %bitcast.35), kind=kOutput, calls=%fused_computation.426 | convolution fusion | flops 5284823040 | bytes 14614528 | tf_op jit(solution)/shard_map/dot_general | solution.py:136
  281.8 9.0 %fusion.179 = f32[896,1280]{1,0:T(8,128)S(1)} fusion(bf16[896,2304]{1,0:T(8,128)(2,1)} %constant_dynamic-update-slice_fusion.5, bf16[2304,1280]{1,0:T(8,128)(2,1)} %bitcast.35), kind=kOutput, calls=%fused_computation.427 | convolution fusion | flops 5284823040 | bytes 14614528 | tf_op jit(solution)/shard_map/dot_general | solution.py:136
  311.9 9.1 %collective-permute-done.25 = bf16[112,2304]{1,0:T(8,128)(2,1)S(1)} collective-permute-done((bf16[112,2304]{1,0:T(8,128)(2,1)S(1)}, bf16[112,2304]{1,0:T(8,128)(2,1)S(1)}, u32[]{:S(2)}, u32[]{:S(2)}) %collective-permute-start.25) | collective-permute-done | bytes 516128 | tf_op jit(solution)/shard_map/ppermute | solution.py:144
  321.0 11.1 %collective-permute-done.28 = bf16[112,2304]{1,0:T(8,128)(2,1)S(1)} collective-permute-done((bf16[112,2304]{1,0:T(8,128)(2,1)S(1)}, bf16[112,2304]{1,0:T(8,128)(2,1)S(1)}, u32[]{:S(2)}, u32[]{:S(2)}) %collective-permute-start.28) | collective-permute-done | bytes 516128 | tf_op jit(solution)/shard_map/ppermute | solution.py:144
  343.1 10.1 %collective-permute-done.29 = bf16[112,2304]{1,0:T(8,128)(2,1)S(1)} collective-permute-done((bf16[112,2304]{1,0:T(8,128)(2,1)S(1)}, bf16[112,2304]{1,0:T(8,128)(2,1)S(1)}, u32[]{:S(2)}, u32[]{:S(2)}) %collective-permute-start.29) | collective-permute-done | bytes 516128 | tf_op jit(solution)/shard_map/ppermute | solution.py:144
  355.0 8.3 %collective-permute-done.26 = bf16[112,2304]{1,0:T(8,128)(2,1)} collective-permute-done((bf16[112,2304]{1,0:T(8,128)(2,1)}, bf16[112,2304]{1,0:T(8,128)(2,1)}, u32[]{:S(2)}, u32[]{:S(2)}) %collective-permute-start.26) | collective-permute-done | bytes 516128 | tf_op jit(solution)/shard_map/ppermute | solution.py:144
  363.3 17.4 %collective-permute-done.30 = bf16[112,2304]{1,0:T(8,128)(2,1)} collective-permute-done((bf16[112,2304]{1,0:T(8,128)(2,1)S(1)}, bf16[112,2304]{1,0:T(8,128)(2,1)}, u32[]{:S(2)}, u32[]{:S(2)}) %collective-permute-start.30) | collective-permute-done | bytes 516128 | tf_op jit(solution)/shard_map/ppermute | solution.py:144
  387.5 11.8 %collective-permute-done.32 = bf16[112,2304]{1,0:T(8,128)(2,1)S(1)} collective-permute-done((bf16[112,2304]{1,0:T(8,128)(2,1)S(1)}, bf16[112,2304]{1,0:T(8,128)(2,1)S(1)}, u32[]{:S(2)}, u32[]{:S(2)}) %collective-permute-start.32) | collective-permute-done | bytes 516128 | tf_op jit(solution)/shard_map/ppermute | solution.py:144
  410.8 9.6 %collective-permute-done.39 = bf16[112,2304]{1,0:T(8,128)(2,1)S(1)} collective-permute-done((bf16[112,2304]{1,0:T(8,128)(2,1)S(1)}, bf16[112,2304]{1,0:T(8,128)(2,1)S(1)}, u32[]{:S(2)}, u32[]{:S(2)}) %collective-permute-start.39) | collective-permute-done | bytes 516128 | tf_op jit(solution)/shard_map/ppermute | solution.py:144
  420.4 7.0 collective-permute-done.40
  433.4 8.8 %fusion.17 = (bf16[896,640]{1,0:T(8,128)(2,1)}, bf16[896,640]{1,0:T(8,128)(2,1)S(1)}, bf16[896,640]{1,0:T(8,128)(2,1)S(1)}, bf16[896,640]{1,0:T(8,128)(2,1)}) fusion(f32[896,1280]{1,0:T(8,128)S(1)} %bitcast.331, pred[640]{0:T(1024)(128)(4,1)S(1)} %fusion.137, f32[896,640]{1,0:T(8,128)S(1)} %fusion.180, f32[896,1280]{1,0:T(8,128)S(1)} %bitcast.329, ...), kind=kOutput, calls=%fused_computation.49 | convolution fusion | flops 2676817920 | bytes 23134848 | tf_op jit(solution)/shard_map/dot_general | solution.py:136
  442.2 6.6 convolution_convert_fusion
  449.4 6.6 convolution_convert_fusion.1
  467.0 7.1 fusion
  489.7 7.7 %pad_maximum_fusion = bf16[1792,2304]{1,0:T(8,128)(2,1)} fusion(bf16[896,2304]{1,0:T(8,128)(2,1)} %constant_dynamic-update-slice_fusion.5, bf16[896,2304]{1,0:T(8,128)(2,1)} %copy-done.11), kind=kLoop, calls=%fused_computation.4 | loop fusion | flops 16515072 | bytes 16515072 | tf_op jit(solution)/shard_map/concatenate | solution.py:390
  507.5 9.6 %fusion.25 = f32[2304,640]{1,0:T(8,128)S(1)} fusion(bf16[1792,2304]{1,0:T(8,128)(2,1)} %pad_maximum_fusion, bf16[896,640]{1,0:T(8,128)(2,1)S(1)} %copy-done.79, bf16[896,640]{1,0:T(8,128)(2,1)S(1)} %copy-done.75), kind=kOutput, calls=%fused_computation.61 | convolution fusion | flops 5289410560 | bytes 16449536 | tf_op jit(solution)/shard_map/dot_general | solution.py:136
  520.4 7.0 fusion.29
  536.2 7.8 %collective-permute-done.51 = bf16[112,2304]{1,0:T(8,128)(2,1)S(1)} collective-permute-done((bf16[112,2304]{1,0:T(8,128)(2,1)S(1)}, bf16[112,2304]{1,0:T(8,128)(2,1)S(1)}, u32[]{:S(2)}, u32[]{:S(2)}) %collective-permute-start.51) | collective-permute-done | bytes 516128 | tf_op jit(solution)/shard_map/ppermute | solution.py:140
  582.9 17.0 %collective-permute-done.57 = bf16[288,1536]{1,0:T(8,128)(2,1)S(1)} collective-permute-done((bf16[288,1536]{1,0:T(8,128)(2,1)S(1)}, bf16[288,1536]{1,0:T(8,128)(2,1)S(1)}, u32[]{:S(2)}, u32[]{:S(2)}) %collective-permute-start.57) | collective-permute-done | bytes 884768 | tf_op jit(solution)/shard_map/ppermute | solution.py:144
  608.0 15.5 %collective-permute-done.62 = bf16[288,1536]{1,0:T(8,128)(2,1)} collective-permute-done((bf16[288,1536]{1,0:T(8,128)(2,1)}, bf16[288,1536]{1,0:T(8,128)(2,1)}, u32[]{:S(2)}, u32[]{:S(2)}) %collective-permute-start.62) | collective-permute-done | bytes 884768 | tf_op jit(solution)/shard_map/ppermute | solution.py:144
  674.7 25.3 %collective-permute-done.63 = bf16[288,1536]{1,0:T(8,128)(2,1)} collective-permute-done((bf16[288,1536]{1,0:T(8,128)(2,1)}, bf16[288,1536]{1,0:T(8,128)(2,1)}, u32[]{:S(2)}, u32[]{:S(2)}) %collective-permute-start.63) | collective-permute-done | bytes 884768 | tf_op jit(solution)/shard_map/ppermute | solution.py:144
  700.0 14.9 %collective-permute-done.61 = bf16[288,1536]{1,0:T(8,128)(2,1)} collective-permute-done((bf16[288,1536]{1,0:T(8,128)(2,1)}, bf16[288,1536]{1,0:T(8,128)(2,1)}, u32[]{:S(2)}, u32[]{:S(2)}) %collective-permute-start.61) | collective-permute-done | bytes 884768 | tf_op jit(solution)/shard_map/ppermute | solution.py:144
  717.4 9.1 %collective-permute-start.69 = (f32[4,4,144]{2,0,1:T(4,128)S(1)}, f32[4,4,144]{2,0,1:T(4,128)S(1)}, u32[]{:S(2)}, u32[]{:S(2)}) collective-permute-start(f32[4,4,144]{2,0,1:T(4,128)S(1)} %slice.507), channel_id=1, source_target_pairs={{0,4},{4,0},{8,12},{12,8},{16,20},{20,16},{24,28},{28,24},{1,5},{5... | collective-permute-start | bytes 27656 | tf_op jit(solution)/shard_map/ppermute | solution.py:144
  (541 shorter events, 372.8 us)
Async XLA Ops:
  7.2 142.6 %all-gather.2.cloned.1.call-start = ((), (), s32[]{:S(2)}) async-start(), calls=%async_computation.4 | async-start | bytes 2654208 | tf_op jit(solution)/shard_map/all_gather | solution.py:303
  11.3 41.1 %collective-permute-start.2 = (bf16[304,1024]{1,0:T(8,128)(2,1)S(1)}, bf16[304,1024]{1,0:T(8,128)(2,1)S(1)}, u32[]{:S(2)}, u32[]{:S(2)}) collective-permute-start(bf16[304,1024]{1,0:T(8,128)(2,1)S(1)} %pad_maximum_fusion.23), channel_id=1, source_target_pairs={{0,16},{4,20},{8,24},{12,28},{16,0},{20,4},{24,8},{28,12},{1,17},{... | collective-permute-start | bytes 1867784 | tf_op jit(solution)/shard_map/ppermute | solution.py:144
  15.4 39.1 %collective-permute-start.3 = (bf16[304,1024]{1,0:T(8,128)(2,1)S(1)}, bf16[304,1024]{1,0:T(8,128)(2,1)S(1)}, u32[]{:S(2)}, u32[]{:S(2)}) collective-permute-start(bf16[304,1024]{1,0:T(8,128)(2,1)S(1)} %pad_maximum_fusion.23), channel_id=1, source_target_pairs={{0,8},{4,12},{8,0},{12,4},{16,24},{20,28},{24,16},{28,20},{1,9},{5... | collective-permute-start | bytes 1867784 | tf_op jit(solution)/shard_map/ppermute | solution.py:144
  17.0 79.8 %collective-permute-start.5 = (bf16[304,1024]{1,0:T(8,128)(2,1)S(1)}, bf16[304,1024]{1,0:T(8,128)(2,1)S(1)}, u32[]{:S(2)}, u32[]{:S(2)}) collective-permute-start(bf16[304,1024]{1,0:T(8,128)(2,1)S(1)} %pad_maximum_fusion.23), channel_id=1, source_target_pairs={{0,4},{4,0},{8,12},{12,8},{16,20},{20,16},{24,28},{28,24},{1,5},{5... | collective-permute-start | bytes 1867784 | tf_op jit(solution)/shard_map/ppermute | solution.py:144
  52.4 26.2 %collective-permute-start.4 = (bf16[304,1024]{1,0:T(8,128)(2,1)S(1)}, bf16[304,1024]{1,0:T(8,128)(2,1)S(1)}, u32[]{:S(2)}, u32[]{:S(2)}) collective-permute-start(bf16[304,1024]{1,0:T(8,128)(2,1)S(1)} %collective-permute-done.2), channel_id=1, source_target_pairs={{0,8},{4,12},{8,0},{12,4},{16,24},{20,28},{24,16},{28,20},{1,9},{5... | collective-permute-start | bytes 1867784 | tf_op jit(solution)/shard_map/ppermute | solution.py:144
  53.0 43.8 %collective-permute-start.6 = (bf16[304,1024]{1,0:T(8,128)(2,1)S(1)}, bf16[304,1024]{1,0:T(8,128)(2,1)}, u32[]{:S(2)}, u32[]{:S(2)}) collective-permute-start(bf16[304,1024]{1,0:T(8,128)(2,1)S(1)} %collective-permute-done.2), channel_id=1, source_target_pairs={{0,4},{4,0},{8,12},{12,8},{16,20},{20,16},{24,28},{28,24},{1,5},{5... | collective-permute-start | bytes 1867784 | tf_op jit(solution)/shard_map/ppermute | solution.py:144
  54.5 47.3 %collective-permute-start.7 = (bf16[304,1024]{1,0:T(8,128)(2,1)S(1)}, bf16[304,1024]{1,0:T(8,128)(2,1)}, u32[]{:S(2)}, u32[]{:S(2)}) collective-permute-start(bf16[304,1024]{1,0:T(8,128)(2,1)S(1)} %collective-permute-done.3), channel_id=1, source_target_pairs={{0,4},{4,0},{8,12},{12,8},{16,20},{20,16},{24,28},{28,24},{1,5},{5... | collective-permute-start | bytes 1867784 | tf_op jit(solution)/shard_map/ppermute | solution.py:144
  85.7 97.7 %all-to-all-start = ((bf16[8,144,1280]{2,1,0:T(8,128)(2,1)}), bf16[8,144,1280]{2,1,0:T(8,128)(2,1)}, u32[]{:S(2)}, u32[]{:S(2)}) async-start(bf16[8,144,1280]{2,1,0:T(8,128)(2,1)} %fusion.112), calls=%async_computation | async-start | bytes 5898240 | tf_op jit(solution)/shard_map/all_to_all | solution.py:327
  93.9 45.3 %collective-permute-start.8 = (bf16[304,1024]{1,0:T(8,128)(2,1)}, bf16[304,1024]{1,0:T(8,128)(2,1)S(1)}, u32[]{:S(2)}, u32[]{:S(2)}) collective-permute-start(bf16[304,1024]{1,0:T(8,128)(2,1)} %copy-done.38), channel_id=1, source_target_pairs={{0,4},{4,0},{8,12},{12,8},{16,20},{20,16},{24,28},{28,24},{1,5},{5... | collective-permute-start | bytes 1867784 | tf_op jit(solution)/shard_map/ppermute | solution.py:144
  190.1 29.5 %collective-permute-start.13 = (bf16[112,2304]{1,0:T(8,128)(2,1)S(1)}, bf16[112,2304]{1,0:T(8,128)(2,1)}, u32[]{:S(2)}, u32[]{:S(2)}) collective-permute-start(bf16[112,2304]{1,0:T(8,128)(2,1)S(1)} %get-tuple-element.92), channel_id=1, source_target_pairs={{0,8},{4,12},{8,0},{12,4},{16,24},{20,28},{24,16},{28,20},{1,9},{5... | collective-permute-start | bytes 1548296 | tf_op jit(solution)/shard_map/ppermute | solution.py:144
  190.1 68.7 %collective-permute-start.16 = (bf16[8,144,1280]{2,1,0:T(8,128)(2,1)}, bf16[8,144,1280]{2,1,0:T(8,128)(2,1)}, u32[]{:S(2)}, u32[]{:S(2)}) collective-permute-start(bf16[8,144,1280]{2,1,0:T(8,128)(2,1)} %all-to-all-done), channel_id=1, source_target_pairs={{0,2},{2,0},{1,3},{3,1},{4,6},{6,4},{5,7},{7,5},{8,10},{10,8},{9,1... | collective-permute-start | bytes 8847368 | tf_op jit(solution)/shard_map/ppermute | solution.py:140
  203.6 34.4 %collective-permute-start.19 = (bf16[112,2304]{1,0:T(8,128)(2,1)}, bf16[112,2304]{1,0:T(8,128)(2,1)}, u32[]{:S(2)}, u32[]{:S(2)}) collective-permute-start(bf16[112,2304]{1,0:T(8,128)(2,1)} %collective-permute-done.11), channel_id=1, source_target_pairs={{0,4},{4,0},{8,12},{12,8},{16,20},{20,16},{24,28},{28,24},{1,5},{5... | collective-permute-start | bytes 1548296 | tf_op jit(solution)/shard_map/ppermute | solution.py:144
  210.5 51.9 %all-to-all-start.1 = ((bf16[8,144,640]{2,1,0:T(8,128)(2,1)}), bf16[8,144,640]{2,1,0:T(8,128)(2,1)}, u32[]{:S(2)}, u32[]{:S(2)}) async-start(bf16[8,144,640]{2,1,0:T(8,128)(2,1)} %fusion.122), calls=%async_computation.1 | async-start | bytes 2949120 | tf_op jit(solution)/shard_map/all_to_all | solution.py:327
  233.6 32.2 %collective-permute-start.15 = (bf16[448,2304]{1,0:T(8,128)(2,1)}, bf16[448,2304]{1,0:T(8,128)(2,1)}, u32[]{:S(2)}, u32[]{:S(2)}) collective-permute-start(bf16[448,2304]{1,0:T(8,128)(2,1)} %pad_maximum_fusion.6), channel_id=1, source_target_pairs={{0,1},{1,0},{2,3},{3,2},{4,5},{5,4},{6,7},{7,6},{8,9},{9,8},{10,11... | collective-permute-start | bytes 6193160 | tf_op jit(solution)/shard_map/ppermute | solution.py:140
  262.4 34.9 %collective-permute-start.17 = (bf16[8,144,640]{2,1,0:T(8,128)(2,1)}, bf16[8,144,640]{2,1,0:T(8,128)(2,1)S(1)}, u32[]{:S(2)}, u32[]{:S(2)}) collective-permute-start(bf16[8,144,640]{2,1,0:T(8,128)(2,1)} %all-to-all-done.1), channel_id=1, source_target_pairs={{0,2},{2,0},{1,3},{3,1},{4,6},{6,4},{5,7},{7,5},{8,10},{10,8},{9,1... | collective-permute-start | bytes 4423688 | tf_op jit(solution)/shard_map/ppermute | solution.py:140
  308.4 34.7 %collective-permute-start.27 = (bf16[112,2304]{1,0:T(8,128)(2,1)S(1)}, bf16[112,2304]{1,0:T(8,128)(2,1)S(1)}, u32[]{:S(2)}, u32[]{:S(2)}) collective-permute-start(bf16[112,2304]{1,0:T(8,128)(2,1)S(1)} %get-tuple-element.152), channel_id=1, source_target_pairs={{0,4},{4,0},{8,12},{12,8},{16,20},{20,16},{24,28},{28,24},{1,5},{5... | collective-permute-start | bytes 1548296 | tf_op jit(solution)/shard_map/ppermute | solution.py:144
  335.1 28.2 %collective-permute-start.26 = (bf16[112,2304]{1,0:T(8,128)(2,1)}, bf16[112,2304]{1,0:T(8,128)(2,1)}, u32[]{:S(2)}, u32[]{:S(2)}) collective-permute-start(bf16[112,2304]{1,0:T(8,128)(2,1)} %get-tuple-element.124), channel_id=1, source_target_pairs={{0,8},{4,12},{8,0},{12,4},{16,24},{20,28},{24,16},{28,20},{1,9},{5... | collective-permute-start | bytes 1548296 | tf_op jit(solution)/shard_map/ppermute | solution.py:144
  353.4 27.3 %collective-permute-start.30 = (bf16[112,2304]{1,0:T(8,128)(2,1)S(1)}, bf16[112,2304]{1,0:T(8,128)(2,1)}, u32[]{:S(2)}, u32[]{:S(2)}) collective-permute-start(bf16[112,2304]{1,0:T(8,128)(2,1)S(1)} %fusion.78), channel_id=1, source_target_pairs={{0,16},{4,20},{8,24},{12,28},{16,0},{20,4},{24,8},{28,12},{1,17},{... | collective-permute-start | bytes 1548296 | tf_op jit(solution)/shard_map/ppermute | solution.py:144
  465.0 34.7 %collective-permute-start.46 = (bf16[112,2304]{1,0:T(8,128)(2,1)}, bf16[112,2304]{1,0:T(8,128)(2,1)}, u32[]{:S(2)}, u32[]{:S(2)}) collective-permute-start(bf16[112,2304]{1,0:T(8,128)(2,1)} %get-tuple-element.147), channel_id=1, source_target_pairs={{0,4},{4,0},{8,12},{12,8},{16,20},{20,16},{24,28},{28,24},{1,5},{5... | collective-permute-start | bytes 1548296 | tf_op jit(solution)/shard_map/ppermute | solution.py:144
  465.4 63.4 %collective-permute-start.43 = (bf16[112,2304]{1,0:T(8,128)(2,1)}, bf16[112,2304]{1,0:T(8,128)(2,1)}, u32[]{:S(2)}, u32[]{:S(2)}) collective-permute-start(bf16[112,2304]{1,0:T(8,128)(2,1)} %get-tuple-element.146), channel_id=1, source_target_pairs={{0,4},{4,0},{8,12},{12,8},{16,20},{20,16},{24,28},{28,24},{1,5},{5... | collective-permute-start | bytes 1548296 | tf_op jit(solution)/shard_map/ppermute | solution.py:144
  477.1 54.8 %collective-permute-start.50 = (bf16[8,144,640]{2,1,0:T(8,128)(2,1)}, bf16[8,144,640]{2,1,0:T(8,128)(2,1)}, u32[]{:S(2)}, u32[]{:S(2)}) collective-permute-start(bf16[8,144,640]{2,1,0:T(8,128)(2,1)} %fusion.52), channel_id=1, source_target_pairs={{0,2},{2,0},{1,3},{3,1},{4,6},{6,4},{5,7},{7,5},{8,10},{10,8},{9,1... | collective-permute-start | bytes 4423688 | tf_op jit(solution)/shard_map/ppermute | solution.py:140
  497.4 31.4 %collective-permute-start.45 = (bf16[112,2304]{1,0:T(8,128)(2,1)}, bf16[112,2304]{1,0:T(8,128)(2,1)S(1)}, u32[]{:S(2)}, u32[]{:S(2)}) collective-permute-start(bf16[112,2304]{1,0:T(8,128)(2,1)} %get-tuple-element.122), channel_id=1, source_target_pairs={{0,8},{4,12},{8,0},{12,4},{16,24},{20,28},{24,16},{28,20},{1,9},{5... | collective-permute-start | bytes 1548296 | tf_op jit(solution)/shard_map/ppermute | solution.py:144
  546.3 85.3 %collective-permute-start.65 = (bf16[8,144,640]{2,1,0:T(8,128)(2,1)}, bf16[8,144,640]{2,1,0:T(8,128)(2,1)}, u32[]{:S(2)}, u32[]{:S(2)}) collective-permute-start(bf16[8,144,640]{2,1,0:T(8,128)(2,1)} %fusion.53), channel_id=1, source_target_pairs={{0,2},{2,0},{1,3},{3,1},{4,6},{6,4},{5,7},{7,5},{8,10},{10,8},{9,1... | collective-permute-start | bytes 4423688 | tf_op jit(solution)/shard_map/ppermute | solution.py:140
  547.7 83.9 %collective-permute-start.66 = (bf16[8,144,640]{2,1,0:T(8,128)(2,1)}, bf16[8,144,640]{2,1,0:T(8,128)(2,1)}, u32[]{:S(2)}, u32[]{:S(2)}) collective-permute-start(bf16[8,144,640]{2,1,0:T(8,128)(2,1)} %fusion.54), channel_id=1, source_target_pairs={{0,2},{2,0},{1,3},{3,1},{4,6},{6,4},{5,7},{7,5},{8,10},{10,8},{9,1... | collective-permute-start | bytes 4423688 | tf_op jit(solution)/shard_map/ppermute | solution.py:140
  552.0 51.3 %all-to-all-start.2 = ((bf16[8,144,640]{2,1,0:T(8,128)(2,1)}), bf16[8,144,640]{2,1,0:T(8,128)(2,1)S(1)}, u32[]{:S(2)}, u32[]{:S(2)}) async-start(bf16[8,144,640]{2,1,0:T(8,128)(2,1)} %fusion.7), calls=%async_computation.2 | async-start | bytes 2949120 | tf_op jit(solution)/shard_map/all_to_all | solution.py:403
  569.3 64.2 %collective-permute-start.53 = (f32[224,2304]{1,0:T(8,128)}, f32[224,2304]{1,0:T(8,128)}, u32[]{:S(2)}, u32[]{:S(2)}) collective-permute-start(f32[224,2304]{1,0:T(8,128)} %pad_maximum_fusion.11), channel_id=1, source_target_pairs={{0,1},{1,0},{2,3},{3,2},{4,5},{5,4},{6,7},{7,6},{8,9},{9,8},{10,11... | collective-permute-start | bytes 6193160 | tf_op jit(solution)/shard_map/ppermute | solution.py:140
  627.5 72.5 %collective-permute-start.63 = (bf16[288,1536]{1,0:T(8,128)(2,1)}, bf16[288,1536]{1,0:T(8,128)(2,1)}, u32[]{:S(2)}, u32[]{:S(2)}) collective-permute-start(bf16[288,1536]{1,0:T(8,128)(2,1)} %fusion.50), channel_id=1, source_target_pairs={{0,16},{4,20},{8,24},{12,28},{16,0},{20,4},{24,8},{28,12},{1,17},{... | collective-permute-start | bytes 2654216 | tf_op jit(solution)/shard_map/ppermute | solution.py:144
  629.9 27.9 %collective-permute-start.59 = (bf16[288,1536]{1,0:T(8,128)(2,1)}, bf16[288,1536]{1,0:T(8,128)(2,1)}, u32[]{:S(2)}, u32[]{:S(2)}) collective-permute-start(bf16[288,1536]{1,0:T(8,128)(2,1)} %pad_maximum_fusion.20), channel_id=1, source_target_pairs={{0,4},{4,0},{8,12},{12,8},{16,20},{20,16},{24,28},{28,24},{1,5},{5... | collective-permute-start | bytes 2654216 | tf_op jit(solution)/shard_map/ppermute | solution.py:144
  640.8 99.3 %all-to-all-start.3 = ((bf16[8,144,1280]{2,1,0:T(8,128)(2,1)}), bf16[8,144,1280]{2,1,0:T(8,128)(2,1)S(1)}, u32[]{:S(2)}, u32[]{:S(2)}) async-start(bf16[8,144,1280]{2,1,0:T(8,128)(2,1)} %pad_maximum_fusion.1), calls=%async_computation.3 | async-start | bytes 5898240 | tf_op jit(solution)/shard_map/all_to_all | solution.py:403
  660.6 54.3 %collective-permute-start.61 = (bf16[288,1536]{1,0:T(8,128)(2,1)}, bf16[288,1536]{1,0:T(8,128)(2,1)}, u32[]{:S(2)}, u32[]{:S(2)}) collective-permute-start(bf16[288,1536]{1,0:T(8,128)(2,1)} %fusion.48), channel_id=1, source_target_pairs={{0,8},{4,12},{8,0},{12,4},{16,24},{20,28},{24,16},{28,20},{1,9},{5... | collective-permute-start | bytes 2654216 | tf_op jit(solution)/shard_map/ppermute | solution.py:144
  664.6 50.3 %collective-permute-start.60 = (bf16[288,1536]{1,0:T(8,128)(2,1)}, bf16[288,1536]{1,0:T(8,128)(2,1)}, u32[]{:S(2)}, u32[]{:S(2)}) collective-permute-start(bf16[288,1536]{1,0:T(8,128)(2,1)} %pad_maximum_fusion.19), channel_id=1, source_target_pairs={{0,4},{4,0},{8,12},{12,8},{16,20},{20,16},{24,28},{28,24},{1,5},{5... | collective-permute-start | bytes 2654216 | tf_op jit(solution)/shard_map/ppermute | solution.py:144
  667.0 59.5 %collective-permute-start.55 = (bf16[112,2304]{1,0:T(8,128)(2,1)}, bf16[112,2304]{1,0:T(8,128)(2,1)}, u32[]{:S(2)}, u32[]{:S(2)}) collective-permute-start(bf16[112,2304]{1,0:T(8,128)(2,1)} %fusion.68), channel_id=1, source_target_pairs={{0,2},{2,0},{1,3},{3,1},{4,6},{6,4},{5,7},{7,5},{8,10},{10,8},{9,1... | collective-permute-start | bytes 1548296 | tf_op jit(solution)/shard_map/ppermute | solution.py:140
  (137 other events, 1548.7 us)
Sparse Core Ops, SparseCore 0:
  23.7 70.2 all-gather.1

commit v6 on v5

--- a/solution.py
+++ b/solution.py
@@ -300,6 +300,7 @@
         have = have + [(k ^ bit, hop(piece, bit, n)) for k, piece in have]
         bit //= 2
     out_own = lax.dynamic_slice_in_dim(output_weight, ctx * q_cols, q_cols, 0).T
+    out_own = after(out_own, have[1][1])
     out_weight = lax.all_gather(out_own, "fsdp", axis=0, tiled=True)
     qkv_weight = jnp.zeros((n, d_rows, heads_cols), b16)
     gains = jnp.zeros((n, gain_rows, heads_cols), b16)

time: 768 us -> 768 us (level)
  starting transfers between devices: 113 us -> 122 us
    ppermute x45, waiting for transfers between devices: 292 us -> 273 us  [hop(): return lax.ppermute(piece, 'fsdp', [(d, d ^ step) for d in range(n)])]
    ppermute x27, waiting for transfers between devices: 41 us -> 53 us  [swap(): return lax.ppermute(piece, axis, [(0, 1), (1, 0)])]
    ppermute x45, starting transfers between devices: 69.7 us -> 81.6 us  [hop(): return lax.ppermute(piece, 'fsdp', [(d, d ^ step) for d in range(n)])]
    unnamed x216 -> x224, local copies, waits for them, and re-layouts: 37.1 us -> 37.1 us
  transfers between devices with their start and end apart: 77 -> 77, of which waited for: 41 -> 39; matrix products, arithmetic and copies ran while one was open for 33% -> 32% of each run, Pallas kernels for 1% -> 1%
where the time goes in v6:
time: 768 us; the launch traced here: 762 us
  waiting for transfers between devices  326 us (42%)
  starting transfers between devices  122 us (16%)
  matrix products  114 us (15%)
  local copies, waits for them, and re-layouts  97.2 us (13%)
  other arithmetic  82 us (11%)
  between operations  16.9 us (2%)
    ppermute x45, waiting for transfers between devices, hop(): return lax.ppermute(piece, 'fsdp', [(d, d ^ step) for d in range(n)])  273 us
    dot_general x23, matrix products, dot(): lax.dot_general(lhs, rhs, (dims, ((), ())), preferred_element_type=f32)  114 us
    ppermute x45, starting transfers between devices, hop(): return lax.ppermute(piece, 'fsdp', [(d, d ^ step) for d in range(n)])  81.6 us
    ppermute x27, waiting for transfers between devices, swap(): return lax.ppermute(piece, axis, [(0, 1), (1, 0)])  53 us
    unnamed x224, local copies, waits for them, and re-layouts  37.1 us
    ppermute x27, starting transfers between devices, swap(): return lax.ppermute(piece, axis, [(0, 1), (1, 0)])  16.8 us
    all_to_all x2, starting transfers between devices, to_units(): return lax.all_to_all(own, 'fsdp', 0, 0, tiled=True)  16.5 us
  transfers between devices with their start and end apart: 77, of which 39 were waited for; matrix products, arithmetic and copies ran while one was open for 32% of the time, Pallas kernels for 1%

profile of v6, /device:TPU:0, one launch (start us, length us, event | category | flops | bytes accessed | tf_op | source)
XLA Modules:
  0.0 762.2 jit_solution(9132093955608148348)
XLA Ops:
  33.4 9.6 %collective-permute-done.2 = bf16[304,1024]{1,0:T(8,128)(2,1)S(1)} collective-permute-done((bf16[304,1024]{1,0:T(8,128)(2,1)S(1)}, bf16[304,1024]{1,0:T(8,128)(2,1)S(1)}, u32[]{:S(2)}, u32[]{:S(2)}) %collective-permute-start.2) | collective-permute-done | bytes 622624 | tf_op jit(solution)/shard_map/ppermute | solution.py:144
  52.2 10.7 %collective-permute-done.4 = bf16[304,1024]{1,0:T(8,128)(2,1)S(1)} collective-permute-done((bf16[304,1024]{1,0:T(8,128)(2,1)S(1)}, bf16[304,1024]{1,0:T(8,128)(2,1)S(1)}, u32[]{:S(2)}, u32[]{:S(2)}) %collective-permute-start.4) | collective-permute-done | bytes 622624 | tf_op jit(solution)/shard_map/ppermute | solution.py:144
  69.9 11.4 %all-to-all-start = ((bf16[8,144,1280]{2,1,0:T(8,128)(2,1)}), bf16[8,144,1280]{2,1,0:T(8,128)(2,1)}, u32[]{:S(2)}, u32[]{:S(2)}) async-start(bf16[8,144,1280]{2,1,0:T(8,128)(2,1)} %fusion.112), calls=%async_computation | async-start | bytes 5898240 | tf_op jit(solution)/shard_map/all_to_all | solution.py:328
  92.4 33.4 %collective-permute-done.8 = bf16[304,1024]{1,0:T(8,128)(2,1)S(1)} collective-permute-done((bf16[304,1024]{1,0:T(8,128)(2,1)}, bf16[304,1024]{1,0:T(8,128)(2,1)S(1)}, u32[]{:S(2)}, u32[]{:S(2)}) %collective-permute-start.8) | collective-permute-done | bytes 622624 | tf_op jit(solution)/shard_map/ppermute | solution.py:144
  147.1 11.9 %collective-permute-done.10 = bf16[112,2304]{1,0:T(8,128)(2,1)S(1)} collective-permute-done((bf16[112,2304]{1,0:T(8,128)(2,1)S(1)}, bf16[112,2304]{1,0:T(8,128)(2,1)S(1)}, u32[]{:S(2)}, u32[]{:S(2)}) %collective-permute-start.10) | collective-permute-done | bytes 516128 | tf_op jit(solution)/shard_map/ppermute | solution.py:140
  181.6 8.8 %collective-permute-done.11 = bf16[112,2304]{1,0:T(8,128)(2,1)} collective-permute-done((bf16[112,2304]{1,0:T(8,128)(2,1)S(1)}, bf16[112,2304]{1,0:T(8,128)(2,1)}, u32[]{:S(2)}, u32[]{:S(2)}) %collective-permute-start.11) | collective-permute-done | bytes 516128 | tf_op jit(solution)/shard_map/ppermute | solution.py:144
  212.7 10.2 %collective-permute-start.21 = (bf16[112,2304]{1,0:T(8,128)(2,1)}, bf16[112,2304]{1,0:T(8,128)(2,1)S(1)}, u32[]{:S(2)}, u32[]{:S(2)}) collective-permute-start(bf16[112,2304]{1,0:T(8,128)(2,1)} %collective-permute-done.14), channel_id=1, source_target_pairs={{0,4},{4,0},{8,12},{12,8},{16,20},{20,16},{24,28},{28,24},{1,5},{5... | collective-permute-start | bytes 1548296 | tf_op jit(solution)/shard_map/ppermute | solution.py:144
  225.1 9.5 %collective-permute-done.20 = bf16[112,2304]{1,0:T(8,128)(2,1)S(1)} collective-permute-done((bf16[112,2304]{1,0:T(8,128)(2,1)}, bf16[112,2304]{1,0:T(8,128)(2,1)S(1)}, u32[]{:S(2)}, u32[]{:S(2)}) %collective-permute-start.20) | collective-permute-done | bytes 516128 | tf_op jit(solution)/shard_map/ppermute | solution.py:144
  234.6 9.3 %collective-permute-done.21 = bf16[112,2304]{1,0:T(8,128)(2,1)S(1)} collective-permute-done((bf16[112,2304]{1,0:T(8,128)(2,1)}, bf16[112,2304]{1,0:T(8,128)(2,1)S(1)}, u32[]{:S(2)}, u32[]{:S(2)}) %collective-permute-start.21) | collective-permute-done | bytes 516128 | tf_op jit(solution)/shard_map/ppermute | solution.py:144
  253.7 9.8 %fusion.178 = f32[896,1280]{1,0:T(8,128)} fusion(bf16[896,2304]{1,0:T(8,128)(2,1)S(1)} %constant_dynamic-update-slice_fusion, bf16[2304,1280]{1,0:T(8,128)(2,1)} %bitcast.35), kind=kOutput, calls=%fused_computation.426 | convolution fusion | flops 5284823040 | bytes 14614528 | tf_op jit(solution)/shard_map/dot_general | solution.py:136
  268.7 9.7 %fusion.179 = f32[896,1280]{1,0:T(8,128)S(1)} fusion(bf16[896,2304]{1,0:T(8,128)(2,1)S(1)} %constant_dynamic-update-slice_fusion.5, bf16[2304,1280]{1,0:T(8,128)(2,1)} %bitcast.35), kind=kOutput, calls=%fused_computation.427 | convolution fusion | flops 5284823040 | bytes 14614528 | tf_op jit(solution)/shard_map/dot_general | solution.py:136
  280.7 17.8 %collective-permute-done.17 = bf16[8,144,640]{2,1,0:T(8,128)(2,1)S(1)} collective-permute-done((bf16[8,144,640]{2,1,0:T(8,128)(2,1)}, bf16[8,144,640]{2,1,0:T(8,128)(2,1)S(1)}, u32[]{:S(2)}, u32[]{:S(2)}) %collective-permute-start.17) | collective-permute-done | bytes 1474592 | tf_op jit(solution)/shard_map/ppermute | solution.py:140
  311.7 10.4 %collective-permute-done.25 = bf16[112,2304]{1,0:T(8,128)(2,1)S(1)} collective-permute-done((bf16[112,2304]{1,0:T(8,128)(2,1)S(1)}, bf16[112,2304]{1,0:T(8,128)(2,1)S(1)}, u32[]{:S(2)}, u32[]{:S(2)}) %collective-permute-start.25) | collective-permute-done | bytes 516128 | tf_op jit(solution)/shard_map/ppermute | solution.py:144
  322.0 11.1 %collective-permute-done.28 = bf16[112,2304]{1,0:T(8,128)(2,1)S(1)} collective-permute-done((bf16[112,2304]{1,0:T(8,128)(2,1)S(1)}, bf16[112,2304]{1,0:T(8,128)(2,1)S(1)}, u32[]{:S(2)}, u32[]{:S(2)}) %collective-permute-start.28) | collective-permute-done | bytes 516128 | tf_op jit(solution)/shard_map/ppermute | solution.py:144
  336.5 7.7 %collective-permute-done.27 = bf16[112,2304]{1,0:T(8,128)(2,1)S(1)} collective-permute-done((bf16[112,2304]{1,0:T(8,128)(2,1)S(1)}, bf16[112,2304]{1,0:T(8,128)(2,1)S(1)}, u32[]{:S(2)}, u32[]{:S(2)}) %collective-permute-start.27) | collective-permute-done | bytes 516128 | tf_op jit(solution)/shard_map/ppermute | solution.py:144
  344.2 10.1 %collective-permute-done.29 = bf16[112,2304]{1,0:T(8,128)(2,1)S(1)} collective-permute-done((bf16[112,2304]{1,0:T(8,128)(2,1)S(1)}, bf16[112,2304]{1,0:T(8,128)(2,1)S(1)}, u32[]{:S(2)}, u32[]{:S(2)}) %collective-permute-start.29) | collective-permute-done | bytes 516128 | tf_op jit(solution)/shard_map/ppermute | solution.py:144
  356.0 8.6 %collective-permute-done.26 = bf16[112,2304]{1,0:T(8,128)(2,1)} collective-permute-done((bf16[112,2304]{1,0:T(8,128)(2,1)}, bf16[112,2304]{1,0:T(8,128)(2,1)}, u32[]{:S(2)}, u32[]{:S(2)}) %collective-permute-start.26) | collective-permute-done | bytes 516128 | tf_op jit(solution)/shard_map/ppermute | solution.py:144
  364.6 17.5 %collective-permute-done.30 = bf16[112,2304]{1,0:T(8,128)(2,1)} collective-permute-done((bf16[112,2304]{1,0:T(8,128)(2,1)S(1)}, bf16[112,2304]{1,0:T(8,128)(2,1)}, u32[]{:S(2)}, u32[]{:S(2)}) %collective-permute-start.30) | collective-permute-done | bytes 516128 | tf_op jit(solution)/shard_map/ppermute | solution.py:144
  388.4 11.9 %collective-permute-done.32 = bf16[112,2304]{1,0:T(8,128)(2,1)S(1)} collective-permute-done((bf16[112,2304]{1,0:T(8,128)(2,1)S(1)}, bf16[112,2304]{1,0:T(8,128)(2,1)S(1)}, u32[]{:S(2)}, u32[]{:S(2)}) %collective-permute-start.32) | collective-permute-done | bytes 516128 | tf_op jit(solution)/shard_map/ppermute | solution.py:144
  411.5 9.0 %collective-permute-done.39 = bf16[112,2304]{1,0:T(8,128)(2,1)S(1)} collective-permute-done((bf16[112,2304]{1,0:T(8,128)(2,1)S(1)}, bf16[112,2304]{1,0:T(8,128)(2,1)S(1)}, u32[]{:S(2)}, u32[]{:S(2)}) %collective-permute-start.39) | collective-permute-done | bytes 516128 | tf_op jit(solution)/shard_map/ppermute | solution.py:144
  420.5 7.5 collective-permute-done.40
  434.1 8.8 %fusion.17 = (bf16[896,640]{1,0:T(8,128)(2,1)}, bf16[896,640]{1,0:T(8,128)(2,1)S(1)}, bf16[896,640]{1,0:T(8,128)(2,1)S(1)}, bf16[896,640]{1,0:T(8,128)(2,1)}) fusion(f32[896,1280]{1,0:T(8,128)S(1)} %bitcast.333, pred[640]{0:T(1024)(128)(4,1)S(1)} %fusion.137, f32[896,640]{1,0:T(8,128)S(1)} %fusion.180, f32[896,1280]{1,0:T(8,128)S(1)} %bitcast.331, ...), kind=kOutput, calls=%fused_computation.49 | convolution fusion | flops 2676817920 | bytes 23134848 | tf_op jit(solution)/shard_map/dot_general | solution.py:136
  467.7 7.1 fusion
  490.8 7.7 %pad_maximum_fusion = bf16[1792,2304]{1,0:T(8,128)(2,1)} fusion(bf16[896,2304]{1,0:T(8,128)(2,1)} %copy-done.14, bf16[896,2304]{1,0:T(8,128)(2,1)} %copy-done.11), kind=kLoop, calls=%fused_computation.4 | loop fusion | flops 16515072 | bytes 16515072 | tf_op jit(solution)/shard_map/concatenate | solution.py:391
  508.6 9.3 %fusion.25 = f32[2304,640]{1,0:T(8,128)S(1)} fusion(bf16[1792,2304]{1,0:T(8,128)(2,1)} %pad_maximum_fusion, bf16[896,640]{1,0:T(8,128)(2,1)S(1)} %copy-done.81, bf16[896,640]{1,0:T(8,128)(2,1)S(1)} %copy-done.77), kind=kOutput, calls=%fused_computation.61 | convolution fusion | flops 5289410560 | bytes 16449536 | tf_op jit(solution)/shard_map/dot_general | solution.py:136
  521.2 7.0 fusion.29
  536.5 8.4 %collective-permute-done.51 = bf16[112,2304]{1,0:T(8,128)(2,1)S(1)} collective-permute-done((bf16[112,2304]{1,0:T(8,128)(2,1)S(1)}, bf16[112,2304]{1,0:T(8,128)(2,1)S(1)}, u32[]{:S(2)}, u32[]{:S(2)}) %collective-permute-start.51) | collective-permute-done | bytes 516128 | tf_op jit(solution)/shard_map/ppermute | solution.py:140
  583.8 17.0 %collective-permute-done.57 = bf16[288,1536]{1,0:T(8,128)(2,1)S(1)} collective-permute-done((bf16[288,1536]{1,0:T(8,128)(2,1)S(1)}, bf16[288,1536]{1,0:T(8,128)(2,1)S(1)}, u32[]{:S(2)}, u32[]{:S(2)}) %collective-permute-start.57) | collective-permute-done | bytes 884768 | tf_op jit(solution)/shard_map/ppermute | solution.py:144
  608.8 15.5 %collective-permute-done.62 = bf16[288,1536]{1,0:T(8,128)(2,1)} collective-permute-done((bf16[288,1536]{1,0:T(8,128)(2,1)}, bf16[288,1536]{1,0:T(8,128)(2,1)}, u32[]{:S(2)}, u32[]{:S(2)}) %collective-permute-start.62) | collective-permute-done | bytes 884768 | tf_op jit(solution)/shard_map/ppermute | solution.py:144
  674.8 26.0 %collective-permute-done.63 = bf16[288,1536]{1,0:T(8,128)(2,1)} collective-permute-done((bf16[288,1536]{1,0:T(8,128)(2,1)}, bf16[288,1536]{1,0:T(8,128)(2,1)}, u32[]{:S(2)}, u32[]{:S(2)}) %collective-permute-start.63) | collective-permute-done | bytes 884768 | tf_op jit(solution)/shard_map/ppermute | solution.py:144
  700.8 15.0 %collective-permute-done.61 = bf16[288,1536]{1,0:T(8,128)(2,1)} collective-permute-done((bf16[288,1536]{1,0:T(8,128)(2,1)}, bf16[288,1536]{1,0:T(8,128)(2,1)}, u32[]{:S(2)}, u32[]{:S(2)}) %collective-permute-start.61) | collective-permute-done | bytes 884768 | tf_op jit(solution)/shard_map/ppermute | solution.py:144
  718.3 8.8 %collective-permute-start.69 = (f32[4,4,144]{2,0,1:T(4,128)S(1)}, f32[4,4,144]{2,0,1:T(4,128)S(1)}, u32[]{:S(2)}, u32[]{:S(2)}) collective-permute-start(f32[4,4,144]{2,0,1:T(4,128)S(1)} %slice.507), channel_id=1, source_target_pairs={{0,4},{4,0},{8,12},{12,8},{16,20},{20,16},{24,28},{28,24},{1,5},{5... | collective-permute-start | bytes 27656 | tf_op jit(solution)/shard_map/ppermute | solution.py:144
  (550 shorter events, 368.9 us)
Async XLA Ops:
  7.2 129.1 %all-gather.2.cloned.1.call-start = ((), (), s32[]{:S(2)}) async-start(), calls=%async_computation.4 | async-start | bytes 2654208 | tf_op jit(solution)/shard_map/all_gather | solution.py:304
  11.3 31.6 %collective-permute-start.2 = (bf16[304,1024]{1,0:T(8,128)(2,1)S(1)}, bf16[304,1024]{1,0:T(8,128)(2,1)S(1)}, u32[]{:S(2)}, u32[]{:S(2)}) collective-permute-start(bf16[304,1024]{1,0:T(8,128)(2,1)S(1)} %pad_maximum_fusion.23), channel_id=1, source_target_pairs={{0,16},{4,20},{8,24},{12,28},{16,0},{20,4},{24,8},{28,12},{1,17},{... | collective-permute-start | bytes 1867784 | tf_op jit(solution)/shard_map/ppermute | solution.py:144
  15.4 29.7 %collective-permute-start.3 = (bf16[304,1024]{1,0:T(8,128)(2,1)S(1)}, bf16[304,1024]{1,0:T(8,128)(2,1)S(1)}, u32[]{:S(2)}, u32[]{:S(2)}) collective-permute-start(bf16[304,1024]{1,0:T(8,128)(2,1)S(1)} %pad_maximum_fusion.23), channel_id=1, source_target_pairs={{0,8},{4,12},{8,0},{12,4},{16,24},{20,28},{24,16},{28,20},{1,9},{5... | collective-permute-start | bytes 1867784 | tf_op jit(solution)/shard_map/ppermute | solution.py:144
  17.0 67.2 %collective-permute-start.5 = (bf16[304,1024]{1,0:T(8,128)(2,1)S(1)}, bf16[304,1024]{1,0:T(8,128)(2,1)S(1)}, u32[]{:S(2)}, u32[]{:S(2)}) collective-permute-start(bf16[304,1024]{1,0:T(8,128)(2,1)S(1)} %pad_maximum_fusion.23), channel_id=1, source_target_pairs={{0,4},{4,0},{8,12},{12,8},{16,20},{20,16},{24,28},{28,24},{1,5},{5... | collective-permute-start | bytes 1867784 | tf_op jit(solution)/shard_map/ppermute | solution.py:144
  43.6 40.6 %collective-permute-start.6 = (bf16[304,1024]{1,0:T(8,128)(2,1)S(1)}, bf16[304,1024]{1,0:T(8,128)(2,1)}, u32[]{:S(2)}, u32[]{:S(2)}) collective-permute-start(bf16[304,1024]{1,0:T(8,128)(2,1)S(1)} %collective-permute-done.2), channel_id=1, source_target_pairs={{0,4},{4,0},{8,12},{12,8},{16,20},{20,16},{24,28},{28,24},{1,5},{5... | collective-permute-start | bytes 1867784 | tf_op jit(solution)/shard_map/ppermute | solution.py:144
  45.2 42.6 %collective-permute-start.7 = (bf16[304,1024]{1,0:T(8,128)(2,1)S(1)}, bf16[304,1024]{1,0:T(8,128)(2,1)}, u32[]{:S(2)}, u32[]{:S(2)}) collective-permute-start(bf16[304,1024]{1,0:T(8,128)(2,1)S(1)} %collective-permute-done.3), channel_id=1, source_target_pairs={{0,4},{4,0},{8,12},{12,8},{16,20},{20,16},{24,28},{28,24},{1,5},{5... | collective-permute-start | bytes 1867784 | tf_op jit(solution)/shard_map/ppermute | solution.py:144
  69.9 100.5 %all-to-all-start = ((bf16[8,144,1280]{2,1,0:T(8,128)(2,1)}), bf16[8,144,1280]{2,1,0:T(8,128)(2,1)}, u32[]{:S(2)}, u32[]{:S(2)}) async-start(bf16[8,144,1280]{2,1,0:T(8,128)(2,1)} %fusion.112), calls=%async_computation | async-start | bytes 5898240 | tf_op jit(solution)/shard_map/all_to_all | solution.py:328
  81.4 44.3 %collective-permute-start.8 = (bf16[304,1024]{1,0:T(8,128)(2,1)}, bf16[304,1024]{1,0:T(8,128)(2,1)S(1)}, u32[]{:S(2)}, u32[]{:S(2)}) collective-permute-start(bf16[304,1024]{1,0:T(8,128)(2,1)} %copy-done.40), channel_id=1, source_target_pairs={{0,4},{4,0},{8,12},{12,8},{16,20},{20,16},{24,28},{28,24},{1,5},{5... | collective-permute-start | bytes 1867784 | tf_op jit(solution)/shard_map/ppermute | solution.py:144
  177.1 29.9 %collective-permute-start.13 = (bf16[112,2304]{1,0:T(8,128)(2,1)S(1)}, bf16[112,2304]{1,0:T(8,128)(2,1)}, u32[]{:S(2)}, u32[]{:S(2)}) collective-permute-start(bf16[112,2304]{1,0:T(8,128)(2,1)S(1)} %get-tuple-element.94), channel_id=1, source_target_pairs={{0,8},{4,12},{8,0},{12,4},{16,24},{20,28},{24,16},{28,20},{1,9},{5... | collective-permute-start | bytes 1548296 | tf_op jit(solution)/shard_map/ppermute | solution.py:144
  180.2 66.3 %collective-permute-start.16 = (bf16[8,144,1280]{2,1,0:T(8,128)(2,1)}, bf16[8,144,1280]{2,1,0:T(8,128)(2,1)}, u32[]{:S(2)}, u32[]{:S(2)}) collective-permute-start(bf16[8,144,1280]{2,1,0:T(8,128)(2,1)} %all-to-all-done), channel_id=1, source_target_pairs={{0,2},{2,0},{1,3},{3,1},{4,6},{6,4},{5,7},{7,5},{8,10},{10,8},{9,1... | collective-permute-start | bytes 8847368 | tf_op jit(solution)/shard_map/ppermute | solution.py:140
  190.4 33.6 %collective-permute-start.19 = (bf16[112,2304]{1,0:T(8,128)(2,1)}, bf16[112,2304]{1,0:T(8,128)(2,1)}, u32[]{:S(2)}, u32[]{:S(2)}) collective-permute-start(bf16[112,2304]{1,0:T(8,128)(2,1)} %collective-permute-done.11), channel_id=1, source_target_pairs={{0,4},{4,0},{8,12},{12,8},{16,20},{20,16},{24,28},{28,24},{1,5},{5... | collective-permute-start | bytes 1548296 | tf_op jit(solution)/shard_map/ppermute | solution.py:144
  199.0 64.5 %all-to-all-start.1 = ((bf16[8,144,640]{2,1,0:T(8,128)(2,1)}), bf16[8,144,640]{2,1,0:T(8,128)(2,1)}, u32[]{:S(2)}, u32[]{:S(2)}) async-start(bf16[8,144,640]{2,1,0:T(8,128)(2,1)} %fusion.122), calls=%async_computation.1 | async-start | bytes 2949120 | tf_op jit(solution)/shard_map/all_to_all | solution.py:328
  212.6 39.0 %collective-permute-start.15 = (bf16[448,2304]{1,0:T(8,128)(2,1)S(1)}, bf16[448,2304]{1,0:T(8,128)(2,1)S(1)}, u32[]{:S(2)}, u32[]{:S(2)}) collective-permute-start(bf16[448,2304]{1,0:T(8,128)(2,1)S(1)} %pad_maximum_fusion.6), channel_id=1, source_target_pairs={{0,1},{1,0},{2,3},{3,2},{4,5},{5,4},{6,7},{7,6},{8,9},{9,8},{10,11... | collective-permute-start | bytes 6193160 | tf_op jit(solution)/shard_map/ppermute | solution.py:140
  212.7 31.1 %collective-permute-start.21 = (bf16[112,2304]{1,0:T(8,128)(2,1)}, bf16[112,2304]{1,0:T(8,128)(2,1)S(1)}, u32[]{:S(2)}, u32[]{:S(2)}) collective-permute-start(bf16[112,2304]{1,0:T(8,128)(2,1)} %collective-permute-done.14), channel_id=1, source_target_pairs={{0,4},{4,0},{8,12},{12,8},{16,20},{20,16},{24,28},{28,24},{1,5},{5... | collective-permute-start | bytes 1548296 | tf_op jit(solution)/shard_map/ppermute | solution.py:144
  263.5 34.9 %collective-permute-start.17 = (bf16[8,144,640]{2,1,0:T(8,128)(2,1)}, bf16[8,144,640]{2,1,0:T(8,128)(2,1)S(1)}, u32[]{:S(2)}, u32[]{:S(2)}) collective-permute-start(bf16[8,144,640]{2,1,0:T(8,128)(2,1)} %all-to-all-done.1), channel_id=1, source_target_pairs={{0,2},{2,0},{1,3},{3,1},{4,6},{6,4},{5,7},{7,5},{8,10},{10,8},{9,1... | collective-permute-start | bytes 4423688 | tf_op jit(solution)/shard_map/ppermute | solution.py:140
  309.5 34.7 %collective-permute-start.27 = (bf16[112,2304]{1,0:T(8,128)(2,1)S(1)}, bf16[112,2304]{1,0:T(8,128)(2,1)S(1)}, u32[]{:S(2)}, u32[]{:S(2)}) collective-permute-start(bf16[112,2304]{1,0:T(8,128)(2,1)S(1)} %get-tuple-element.154), channel_id=1, source_target_pairs={{0,4},{4,0},{8,12},{12,8},{16,20},{20,16},{24,28},{28,24},{1,5},{5... | collective-permute-start | bytes 1548296 | tf_op jit(solution)/shard_map/ppermute | solution.py:144
  336.2 28.4 %collective-permute-start.26 = (bf16[112,2304]{1,0:T(8,128)(2,1)}, bf16[112,2304]{1,0:T(8,128)(2,1)}, u32[]{:S(2)}, u32[]{:S(2)}) collective-permute-start(bf16[112,2304]{1,0:T(8,128)(2,1)} %get-tuple-element.126), channel_id=1, source_target_pairs={{0,8},{4,12},{8,0},{12,4},{16,24},{20,28},{24,16},{28,20},{1,9},{5... | collective-permute-start | bytes 1548296 | tf_op jit(solution)/shard_map/ppermute | solution.py:144
  354.5 27.6 %collective-permute-start.30 = (bf16[112,2304]{1,0:T(8,128)(2,1)S(1)}, bf16[112,2304]{1,0:T(8,128)(2,1)}, u32[]{:S(2)}, u32[]{:S(2)}) collective-permute-start(bf16[112,2304]{1,0:T(8,128)(2,1)S(1)} %fusion.78), channel_id=1, source_target_pairs={{0,16},{4,20},{8,24},{12,28},{16,0},{20,4},{24,8},{28,12},{1,17},{... | collective-permute-start | bytes 1548296 | tf_op jit(solution)/shard_map/ppermute | solution.py:144
  465.7 34.7 %collective-permute-start.46 = (bf16[112,2304]{1,0:T(8,128)(2,1)}, bf16[112,2304]{1,0:T(8,128)(2,1)}, u32[]{:S(2)}, u32[]{:S(2)}) collective-permute-start(bf16[112,2304]{1,0:T(8,128)(2,1)} %get-tuple-element.149), channel_id=1, source_target_pairs={{0,4},{4,0},{8,12},{12,8},{16,20},{20,16},{24,28},{28,24},{1,5},{5... | collective-permute-start | bytes 1548296 | tf_op jit(solution)/shard_map/ppermute | solution.py:144
  466.4 63.2 %collective-permute-start.43 = (bf16[112,2304]{1,0:T(8,128)(2,1)}, bf16[112,2304]{1,0:T(8,128)(2,1)}, u32[]{:S(2)}, u32[]{:S(2)}) collective-permute-start(bf16[112,2304]{1,0:T(8,128)(2,1)} %get-tuple-element.148), channel_id=1, source_target_pairs={{0,4},{4,0},{8,12},{12,8},{16,20},{20,16},{24,28},{28,24},{1,5},{5... | collective-permute-start | bytes 1548296 | tf_op jit(solution)/shard_map/ppermute | solution.py:144
  477.8 54.8 %collective-permute-start.50 = (bf16[8,144,640]{2,1,0:T(8,128)(2,1)}, bf16[8,144,640]{2,1,0:T(8,128)(2,1)}, u32[]{:S(2)}, u32[]{:S(2)}) collective-permute-start(bf16[8,144,640]{2,1,0:T(8,128)(2,1)} %fusion.52), channel_id=1, source_target_pairs={{0,2},{2,0},{1,3},{3,1},{4,6},{6,4},{5,7},{7,5},{8,10},{10,8},{9,1... | collective-permute-start | bytes 4423688 | tf_op jit(solution)/shard_map/ppermute | solution.py:140
  498.6 31.1 %collective-permute-start.45 = (bf16[112,2304]{1,0:T(8,128)(2,1)}, bf16[112,2304]{1,0:T(8,128)(2,1)S(1)}, u32[]{:S(2)}, u32[]{:S(2)}) collective-permute-start(bf16[112,2304]{1,0:T(8,128)(2,1)} %get-tuple-element.124), channel_id=1, source_target_pairs={{0,8},{4,12},{8,0},{12,4},{16,24},{20,28},{24,16},{28,20},{1,9},{5... | collective-permute-start | bytes 1548296 | tf_op jit(solution)/shard_map/ppermute | solution.py:144
  547.2 85.3 %collective-permute-start.65 = (bf16[8,144,640]{2,1,0:T(8,128)(2,1)}, bf16[8,144,640]{2,1,0:T(8,128)(2,1)}, u32[]{:S(2)}, u32[]{:S(2)}) collective-permute-start(bf16[8,144,640]{2,1,0:T(8,128)(2,1)} %fusion.53), channel_id=1, source_target_pairs={{0,2},{2,0},{1,3},{3,1},{4,6},{6,4},{5,7},{7,5},{8,10},{10,8},{9,1... | collective-permute-start | bytes 4423688 | tf_op jit(solution)/shard_map/ppermute | solution.py:140
  548.3 84.1 %collective-permute-start.66 = (bf16[8,144,640]{2,1,0:T(8,128)(2,1)}, bf16[8,144,640]{2,1,0:T(8,128)(2,1)}, u32[]{:S(2)}, u32[]{:S(2)}) collective-permute-start(bf16[8,144,640]{2,1,0:T(8,128)(2,1)} %fusion.54), channel_id=1, source_target_pairs={{0,2},{2,0},{1,3},{3,1},{4,6},{6,4},{5,7},{7,5},{8,10},{10,8},{9,1... | collective-permute-start | bytes 4423688 | tf_op jit(solution)/shard_map/ppermute | solution.py:140
  552.9 51.3 %all-to-all-start.2 = ((bf16[8,144,640]{2,1,0:T(8,128)(2,1)}), bf16[8,144,640]{2,1,0:T(8,128)(2,1)S(1)}, u32[]{:S(2)}, u32[]{:S(2)}) async-start(bf16[8,144,640]{2,1,0:T(8,128)(2,1)} %fusion.7), calls=%async_computation.2 | async-start | bytes 2949120 | tf_op jit(solution)/shard_map/all_to_all | solution.py:404
  570.1 64.1 %collective-permute-start.53 = (f32[224,2304]{1,0:T(8,128)}, f32[224,2304]{1,0:T(8,128)}, u32[]{:S(2)}, u32[]{:S(2)}) collective-permute-start(f32[224,2304]{1,0:T(8,128)} %pad_maximum_fusion.11), channel_id=1, source_target_pairs={{0,1},{1,0},{2,3},{3,2},{4,5},{5,4},{6,7},{7,6},{8,9},{9,8},{10,11... | collective-permute-start | bytes 6193160 | tf_op jit(solution)/shard_map/ppermute | solution.py:140
  628.3 72.5 %collective-permute-start.63 = (bf16[288,1536]{1,0:T(8,128)(2,1)}, bf16[288,1536]{1,0:T(8,128)(2,1)}, u32[]{:S(2)}, u32[]{:S(2)}) collective-permute-start(bf16[288,1536]{1,0:T(8,128)(2,1)} %fusion.50), channel_id=1, source_target_pairs={{0,16},{4,20},{8,24},{12,28},{16,0},{20,4},{24,8},{28,12},{1,17},{... | collective-permute-start | bytes 2654216 | tf_op jit(solution)/shard_map/ppermute | solution.py:144
  630.7 28.3 %collective-permute-start.59 = (bf16[288,1536]{1,0:T(8,128)(2,1)}, bf16[288,1536]{1,0:T(8,128)(2,1)}, u32[]{:S(2)}, u32[]{:S(2)}) collective-permute-start(bf16[288,1536]{1,0:T(8,128)(2,1)} %pad_maximum_fusion.20), channel_id=1, source_target_pairs={{0,4},{4,0},{8,12},{12,8},{16,20},{20,16},{24,28},{28,24},{1,5},{5... | collective-permute-start | bytes 2654216 | tf_op jit(solution)/shard_map/ppermute | solution.py:144
  641.4 99.3 %all-to-all-start.3 = ((bf16[8,144,1280]{2,1,0:T(8,128)(2,1)}), bf16[8,144,1280]{2,1,0:T(8,128)(2,1)S(1)}, u32[]{:S(2)}, u32[]{:S(2)}) async-start(bf16[8,144,1280]{2,1,0:T(8,128)(2,1)} %pad_maximum_fusion.1), calls=%async_computation.3 | async-start | bytes 5898240 | tf_op jit(solution)/shard_map/all_to_all | solution.py:404
  661.9 53.9 %collective-permute-start.61 = (bf16[288,1536]{1,0:T(8,128)(2,1)}, bf16[288,1536]{1,0:T(8,128)(2,1)}, u32[]{:S(2)}, u32[]{:S(2)}) collective-permute-start(bf16[288,1536]{1,0:T(8,128)(2,1)} %fusion.48), channel_id=1, source_target_pairs={{0,8},{4,12},{8,0},{12,4},{16,24},{20,28},{24,16},{28,20},{1,9},{5... | collective-permute-start | bytes 2654216 | tf_op jit(solution)/shard_map/ppermute | solution.py:144
  665.4 50.3 %collective-permute-start.60 = (bf16[288,1536]{1,0:T(8,128)(2,1)}, bf16[288,1536]{1,0:T(8,128)(2,1)}, u32[]{:S(2)}, u32[]{:S(2)}) collective-permute-start(bf16[288,1536]{1,0:T(8,128)(2,1)} %pad_maximum_fusion.19), channel_id=1, source_target_pairs={{0,4},{4,0},{8,12},{12,8},{16,20},{20,16},{24,28},{28,24},{1,5},{5... | collective-permute-start | bytes 2654216 | tf_op jit(solution)/shard_map/ppermute | solution.py:144
  671.2 55.9 %collective-permute-start.55 = (bf16[112,2304]{1,0:T(8,128)(2,1)}, bf16[112,2304]{1,0:T(8,128)(2,1)}, u32[]{:S(2)}, u32[]{:S(2)}) collective-permute-start(bf16[112,2304]{1,0:T(8,128)(2,1)} %fusion.68), channel_id=1, source_target_pairs={{0,2},{2,0},{1,3},{3,1},{4,6},{6,4},{5,7},{7,5},{8,10},{10,8},{9,1... | collective-permute-start | bytes 1548296 | tf_op jit(solution)/shard_map/ppermute | solution.py:140
  (141 other events, 1539.6 us)
Sparse Core Ops, SparseCore 0:
  43.1 76.6 all-gather.1
